TPU v7x, 512 devices: a whole 4x4x16 slice. The times are simulated.
512 devices in a mesh: dp: 64 (over y, z_hi, x, core), fsdp: 8 (over z_lo).
Axes of the slice: x: 4, y: 4, z: 16 (z_hi: 2, z_lo: 8; z = z_hi * 8 + z_lo), core: 2. Of those that a mesh axis runs over, the one named last changes fastest.
Arguments:
- inputs: bfloat16 [65536, 4096], P(('dp', 'fsdp')), may hold values from -6 to 6
- out_grad: bfloat16 [65536, 2048], P(('dp', 'fsdp')), may hold values from -24 to 24
- weight: bfloat16 [4096, 2048], P('fsdp'), may hold values from -0.125 to 0.125
- proj_basis: bfloat16 [4096, 256], P('fsdp'), may hold values from -0.09375 to 0.09375
- first_moment: float32 [64, 8192], P('dp'), may hold values from -6 to 6
- second_moment: float32 [64, 8192], P('dp'), may hold values from 0.25 to 4
Outputs:
- input_grad: bfloat16 [65536, 4096], P(('dp', 'fsdp'))
- new_first: float32 [64, 8192], P('dp')
- new_second: float32 [64, 8192], P('dp')
- update: float32 [4096, 2048], P('fsdp', 'dp')
All inputs are finite; a program needn't handle non-finite values.
Results may differ from a plain program's by a relative error of at most 0.0029.
Values may be sent and summed in bfloat16 or wider, within the bound.
No kernel may reach another device: no remote copies, remote signals or barrier semaphores. Data moves between devices by JAX's collectives and lax.ppermute only.
A program may use at most 64 MiB of HBM per device.

v0:
```python
import math

import jax
import jax.numpy as jnp
from jax import lax
from jax.sharding import PartitionSpec as P

STEP = 1000


beta_one = 0.9
beta_two = 0.999
epsilon = 1e-08


def on_device(inputs, out_grad, weight, proj_basis, first_moment, second_moment):
    tok_rows = inputs.shape[0]
    data_count = lax.axis_size("dp")
    shard_count = lax.axis_size("fsdp")
    rank_cols = proj_basis.shape[1]
    feature_grad = lax.dot_general(
        lax.all_gather(out_grad, "fsdp", axis=0, tiled=True),
        weight,
        (((1,), (1,)), ((), ())),
        preferred_element_type=jnp.float32,
    ).astype(jnp.bfloat16)
    input_grad = lax.all_to_all(feature_grad, "fsdp", split_axis=0, concat_axis=1, tiled=True)
    proj_full = jnp.dot(
        inputs,
        lax.all_gather(proj_basis, "fsdp", axis=0, tiled=True),
        preferred_element_type=jnp.float32,
    )
    projected_in = proj_full.astype(jnp.bfloat16)
    scale_factor = 1.0 / math.sqrt(tok_rows * data_count * shard_count)
    low_rank = (
        lax.dot_general(
            projected_in, out_grad, (((0,), (0,)), ((), ())), preferred_element_type=jnp.float32
        )
        * scale_factor
    )
    col_width = low_rank.shape[1] // data_count
    summed = lax.psum(low_rank, ("dp", "fsdp"))
    grad_block = lax.dynamic_slice_in_dim(summed, lax.axis_index("dp") * col_width, col_width, 1)
    flat_grad = grad_block.reshape(1, rank_cols * col_width)
    new_first = beta_one * first_moment + (1.0 - beta_one) * flat_grad
    new_second = beta_two * second_moment + (1.0 - beta_two) * flat_grad * flat_grad
    corr_one = 1.0 - beta_one**STEP
    corr_two = 1.0 - beta_two**STEP
    direction = (new_first / corr_one / (jnp.sqrt(new_second / corr_two) + epsilon)).astype(
        jnp.bfloat16
    )
    direction = direction.reshape(rank_cols, col_width)
    update = jnp.dot(proj_basis, direction, preferred_element_type=jnp.float32)
    return (input_grad, new_first, new_second, update)


def solution(mesh):
    in_specs = (
        P(("dp", "fsdp"), None),
        P(("dp", "fsdp"), None),
        P("fsdp", None),
        P("fsdp", None),
        P("dp", None),
        P("dp", None),
    )
    out_specs = (P(("dp", "fsdp"), None), P("dp", None), P("dp", None), P("fsdp", "dp"))
    return jax.shard_map(
        on_device, mesh=mesh, in_specs=in_specs, out_specs=out_specs, check_vma=False
    )
```

profile of v0, /device:TPU:1, one launch (start us, length us, event | category | flops | bytes accessed | tf_op | source)
XLA Modules:
  0.0 714.3 jit_solution(5845049301039747095)
XLA Ops:
  7.2 0.0 copy-start
  7.2 0.0 all-gather.3.cloned.1.call-start
  7.2 0.7 all-gather.3.cloned.1.call-update
  7.9 0.0 all-gather.5.cloned.1.call-start
  8.0 0.7 all-gather.5.cloned.1.call-update
  8.7 111.0 %all-gather.3.cloned.1.call-done = bf16[1024,2048]{1,0:T(8,128)(2,1)} async-done(((bf16[128,2048]{1,0:T(8,128)(2,1)}), bf16[1024,2048]{1,0:T(8,128)(2,1)}) %all-gather.3.cloned.1.call-update) | async-done | bytes 4194320 | tf_op jit(solution)/shard_map/all_gather | solution.py:22
  119.7 0.0 copy-done
  119.7 5.5 convolution_convert_fusion
  125.2 3.6 all-to-all-start
  128.8 0.0 all-reduce.2.cloned.1.call-start
  128.8 89.4 %all-gather.5.cloned.1.call-done = bf16[4096,256]{1,0:T(8,128)(2,1)} async-done(((bf16[512,256]{1,0:T(8,128)(2,1)}), bf16[4096,256]{1,0:T(8,128)(2,1)}) %all-gather.5.cloned.1.call-update) | async-done | bytes 2097168 | tf_op jit(solution)/shard_map/all_gather | solution.py:30
  218.2 4.7 convolution_multiply_fusion
  222.9 0.0 copy-start.1
  222.9 0.0 all-reduce.2.cloned.1.call-update
  222.9 478.2 %all-reduce.2.cloned.1.call-done = f32[256,2048]{0,1:T(8,128)} async-done(((f32[256,2048]{0,1:T(8,128)}), f32[256,2048]{0,1:T(8,128)}) %all-reduce.2.cloned.1.call-update) | async-done | bytes 2097168 | tf_op jit(solution)/shard_map/psum | solution.py:42
  701.2 1.4 constant_dynamic-slice_fusion
  702.5 0.9 copy.12
  703.4 0.7 reshape.53
  704.1 1.6 convert_reduce_fusion
  705.7 0.1 reshape.54
  705.8 0.0 copy-done.1
  705.8 0.8 convolution_bitcast_fusion
  706.7 0.0 all-to-all-done
  706.7 1.1 copy.13
Async XLA Ops:
  7.2 112.5 %copy-start = (bf16[512,2048]{1,0:T(8,128)(2,1)S(1)}, bf16[512,2048]{1,0:T(8,128)(2,1)}, u32[]{:S(2)}) copy-start(bf16[512,2048]{1,0:T(8,128)(2,1)} %param.8) | copy-start | bytes 6291460
  7.2 112.5 %all-gather.3.cloned.1.call-start = ((), (), s32[]{:S(2)}) async-start(), calls=%async_computation.1 | async-start | bytes 4718592 | tf_op jit(solution)/shard_map/all_gather | solution.py:22
  7.9 210.3 %all-gather.5.cloned.1.call-start = ((), (), s32[]{:S(2)}) async-start(), calls=%async_computation.2 | async-start | bytes 2359296 | tf_op jit(solution)/shard_map/all_gather | solution.py:30
  125.2 581.5 %all-to-all-start = ((bf16[8,128,512]{2,1,0:T(8,128)(2,1)}), bf16[8,128,512]{2,1,0:T(8,128)(2,1)S(1)}, u32[]{:S(2)}, u32[]{:S(2)}) async-start(bf16[8,128,512]{2,1,0:T(8,128)(2,1)} %bitcast.14), calls=%async_computation | async-start | bytes 2097152 | tf_op jit(solution)/shard_map/all_to_all | solution.py:27
  128.8 572.4 %all-reduce.2.cloned.1.call-start = ((), (), s32[]{:S(2)}) async-start(), calls=%async_computation.3 | async-start | bytes 4194304 | tf_op jit(solution)/shard_map/psum | solution.py:42
  222.9 482.9 %copy-start.1 = (bf16[512,256]{1,0:T(8,128)(2,1)S(1)}, bf16[512,256]{1,0:T(8,128)(2,1)}, u32[]{:S(2)}) copy-start(bf16[512,256]{1,0:T(8,128)(2,1)} %param.9) | copy-start | bytes 786436
Sparse Core Ops, SparseCore 0:
  10.1 109.5 all-gather.2
  121.8 96.4 all-gather.4
  223.6 477.5 all-reduce.1
where the time goes:
time: 715 us; the launch traced here: 714 us
  waiting for transfers between devices  680 us (95%)
  between operations  13.8 us (2%)
  matrix products  11 us (2%)
    psum x1, waiting for transfers between devices, on_device(): summed = lax.psum(low_rank, ('dp', 'fsdp'))  478 us
    all_gather x1, waiting for transfers between devices, on_device(): lax.all_gather(out_grad, 'fsdp', axis=0, tiled=True)  111 us
    all_gather x1, waiting for transfers between devices, on_device(): lax.all_gather(proj_basis, 'fsdp', axis=0, tiled=True)  89.4 us
  transfers between devices with their start and end apart: 4, of which 3 were waited for; matrix products, arithmetic and copies ran while one was open for 2% of the time, Pallas kernels for 0%

commit v1 on v0

v1 whole, which is shorter than its diff:
```python
import math

import jax
import jax.numpy as jnp
from jax import lax
from jax.sharding import Mesh
from jax.sharding import PartitionSpec as P

STEP = 1000

beta_one = 0.9
beta_two = 0.999
epsilon = 1e-08

AXES = ("y", "zh", "x", "c", "q", "p")
SIZES = (4, 2, 4, 2, 4, 2)
PLANE = ("y", "x")
LINE = ("q", "p")
COLUMN = ("zh", "c", "q", "p")
SWAP = [(0, 1), (1, 0)]


def spread(block, axes, count):
    sent = jnp.broadcast_to(block[None], (count,) + block.shape)
    return lax.all_to_all(sent, axes, 0, 0, tiled=True)


def project_basis(proj_basis, plane, core):
    rows = proj_basis.shape[0] // 16
    half = proj_basis.shape[1] // 2
    piece = lax.dynamic_slice(proj_basis, (plane * rows, core * half), (rows, half))
    line = spread(piece, LINE, 8)
    whole = spread(line, PLANE, 16)
    return whole.transpose(1, 0, 2, 3).reshape(-1, half)


def weight_half(weight, plane, core):
    half = weight.shape[0] // 2
    rows = half // 16
    piece = lax.dynamic_slice(weight, (core * half + plane * rows, 0), (rows, weight.shape[1]))
    line = spread(piece, "q", 4)
    whole = spread(line, PLANE, 16)
    return whole.transpose(1, 0, 2, 3).reshape(4 * half, weight.shape[1])


def on_device(inputs, out_grad, weight, proj_basis, first_moment, second_moment):
    f32, bf16 = jnp.float32, jnp.bfloat16
    core = lax.axis_index("c")
    parity = lax.axis_index("p")
    plane = lax.axis_index(PLANE)
    tokens = inputs.shape[0] * 512
    scale_factor = 1.0 / math.sqrt(tokens)

    basis = project_basis(proj_basis, plane, core)
    grad_c = lax.ppermute(out_grad, "c", SWAP)
    inputs_c = lax.ppermute(inputs, "c", SWAP)
    wide = weight_half(weight, plane, core)
    grad_z = lax.ppermute(out_grad, "p", SWAP)
    grad_zc = lax.ppermute(grad_z, "c", SWAP)

    proj = jnp.concatenate(
        [
            jnp.dot(inputs, basis, preferred_element_type=f32).astype(bf16),
            jnp.dot(inputs_c, basis, preferred_element_type=f32).astype(bf16),
        ],
        axis=0,
    )
    chip_grad = jnp.concatenate([out_grad, grad_c], axis=0)
    low = (
        lax.dot_general(chip_grad, proj, (((0,), (0,)), ((), ())), preferred_element_type=f32)
        * scale_factor
    )
    half = low.shape[1]
    cols = low.shape[0] // 64
    low = low.reshape(4, 2, 4, 2 * cols, half).transpose(0, 2, 1, 3, 4).reshape(16, 4 * cols, half)
    low = lax.all_to_all(low, PLANE, 0, 0, tiled=True).sum(axis=0)
    low = low.reshape(2, 2, 1, cols, half).astype(bf16)
    low = jnp.broadcast_to(low, (2, 2, 8, cols, half)).reshape(32, cols, half)
    low = lax.all_to_all(low, COLUMN, 0, 0, tiled=True).reshape(2, 2, 8, cols, half)
    low = low.astype(f32).sum(axis=(0, 2))
    flat_grad = low.transpose(0, 2, 1).reshape(1, 2 * half * cols)

    new_first = beta_one * first_moment + (1.0 - beta_one) * flat_grad
    new_second = beta_two * second_moment + (1.0 - beta_two) * flat_grad * flat_grad
    corr_one = 1.0 - beta_one**STEP
    corr_two = 1.0 - beta_two**STEP
    direction = (new_first / corr_one / (jnp.sqrt(new_second / corr_two) + epsilon)).astype(bf16)
    direction = direction.reshape(2 * half, cols)
    update = jnp.dot(proj_basis, direction, preferred_element_type=f32)

    both = jnp.concatenate([grad_z, grad_zc, chip_grad], axis=0)
    feats = lax.dot_general(
        both, wide, (((1,), (1,)), ((), ())), preferred_element_type=f32
    ).astype(bf16)
    n = inputs.shape[0]
    back = lax.ppermute(feats[: 2 * n], "p", SWAP)
    mine = jnp.stack([feats[2 * n : 3 * n], back[:n]])
    theirs = jnp.stack([feats[3 * n :], back[n:]])
    other = lax.ppermute(theirs, "c", SWAP)
    mine, other = (v.reshape(2, n, 4, -1) for v in (mine, other))
    lower = jnp.where(core == 0, mine, other)
    upper = jnp.where(core == 0, other, mine)
    even = [jnp.where(parity == 0, v[0], v[1]) for v in (lower, upper)]
    odd = [jnp.where(parity == 0, v[1], v[0]) for v in (lower, upper)]
    input_grad = jnp.stack(even + odd, axis=2).reshape(n, -1)
    return (input_grad, new_first, new_second, update)


def solution(mesh):
    fine = Mesh(mesh.devices.reshape(SIZES), AXES)
    dp, fsdp = AXES[:4], AXES[4:]
    in_specs = (
        P(AXES, None),
        P(AXES, None),
        P(fsdp, None),
        P(fsdp, None),
        P(dp, None),
        P(dp, None),
    )
    out_specs = (P(AXES, None), P(dp, None), P(dp, None), P(fsdp, dp))
    return jax.shard_map(
        on_device, mesh=fine, in_specs=in_specs, out_specs=out_specs, check_vma=False
    )
```

time: 715 us -> 205 us (0.29)
  waiting for transfers between devices: 680 us -> 67.1 us
  starting transfers between devices: 3.68 us -> 60.2 us
  blocking collectives: 0 us -> 45.7 us
  local copies, waits for them, and re-layouts: 4.15 us -> 17.3 us
  between operations: 13.8 us -> 1.01 us
    psum x1 -> x0, waiting for transfers between devices: 478 us -> none  [on_device(): summed = lax.psum(low_rank, ('dp', 'fsdp'))]
    all_gather x2 -> x0, waiting for transfers between devices: 200 us -> none  [the longest x1 111 us: on_device(): lax.all_gather(out_grad, 'fsdp', axis=0, tiled=True)]
    all_to_all x1 -> x4, waiting for transfers between devices: 0.01 us -> 53.5 us  [the longest x3 42.5 us: spread(): return lax.all_to_all(sent, axes, 0, 0, tiled=True)]
    all_to_all x0 -> x2, blocking collectives: none -> 45.7 us  [the longest x1 23.1 us: on_device(): low = lax.all_to_all(low, PLANE, 0, 0, tiled=True).sum(axis=0)]
    all_to_all x1 -> x4, starting transfers between devices: 3.56 us -> 34.4 us  [the longest x1 19.7 us: on_device(): lax.all_to_all(low, COLUMN, 0, 0, tiled=True).reshape(2, 2, 8, cols, half)]
    ppermute x0 -> x6, starting transfers between devices: none -> 25.9 us  [the longest x1 5.54 us: on_device(): grad_c = lax.ppermute(out_grad, 'c', SWAP)]
    ppermute x0 -> x6, waiting for transfers between devices: none -> 13.5 us  [the longest x1 10.1 us: on_device(): grad_z = lax.ppermute(out_grad, 'p', SWAP)]
  transfers between devices with their start and end apart: 4 -> 10, of which waited for: 3 -> 5; matrix products, arithmetic and copies ran while one was open for 2% -> 8% of each run, Pallas kernels for 0% -> 0%
where the time goes in v1:
time: 205 us; the launch traced here: 204 us
  waiting for transfers between devices  67.1 us (33%)
  starting transfers between devices  60.2 us (29%)
  blocking collectives  45.7 us (22%)
  local copies, waits for them, and re-layouts  17.3 us (8%)
  matrix products  9.14 us (4%)
  other arithmetic  3.23 us (2%)
    all_to_all x3, waiting for transfers between devices, spread(): return lax.all_to_all(sent, axes, 0, 0, tiled=True)  42.5 us
    all_to_all x1, blocking collectives, on_device(): low = lax.all_to_all(low, PLANE, 0, 0, tiled=True).sum(axis=0)  23.1 us
    all_to_all x1, blocking collectives, spread(): return lax.all_to_all(sent, axes, 0, 0, tiled=True)  22.6 us
    all_to_all x1, starting transfers between devices, on_device(): lax.all_to_all(low, COLUMN, 0, 0, tiled=True).reshape(2, 2, 8, cols, half)  19.7 us
    all_to_all x3, starting transfers between devices, spread(): return lax.all_to_all(sent, axes, 0, 0, tiled=True)  14.7 us
    all_to_all x1, waiting for transfers between devices, on_device(): lax.all_to_all(low, COLUMN, 0, 0, tiled=True).reshape(2, 2, 8, cols, half)  11 us
    ppermute x1, waiting for transfers between devices, on_device(): grad_z = lax.ppermute(out_grad, 'p', SWAP)  10.1 us
    ppermute x1, starting transfers between devices, on_device(): grad_c = lax.ppermute(out_grad, 'c', SWAP)  5.54 us
  transfers between devices with their start and end apart: 10, of which 5 were waited for; matrix products, arithmetic and copies ran while one was open for 8% of the time, Pallas kernels for 0%

profile of v1, /device:TPU:1, one launch (start us, length us, event | category | flops | bytes accessed | tf_op | source)
XLA Modules:
  0.0 203.7 jit_solution(9876395381957796044)
XLA Ops:
  0.6 0.0 copy-start
  0.7 0.8 dynamic_slice.7
  1.5 22.6 %all_to_all.30 = bf16[8,32,128]{2,1,0:T(8,128)(2,1)S(1)} all-to-all(bf16[8,32,128]{2,1,0:T(8,128)(2,1)S(1)} %broadcast_in_dim.12), channel_id=1, replica_groups=mesh['y'=4,'zh'=2,'x'=4,'c'=2,'q'=4,'p'=2] {'q','p'}, dimensions={0} | all-to-all | bytes 131072 | tf_op jit(solution)/shard_map/all_to_all | solution.py:25
  24.1 1.2 broadcast_in_dim.13
  25.3 6.8 %all-to-all-start.3 = ((bf16[16,8,32,128]{3,2,1,0:T(8,128)(2,1)}), bf16[16,8,32,128]{3,2,1,0:T(8,128)(2,1)S(1)}, u32[]{:S(2)}, u32[]{:S(2)}) async-start(bf16[16,8,32,128]{3,2,1,0:T(8,128)(2,1)} %broadcast_in_dim.13), calls=%async_computation.3 | async-start | bytes 2097152 | tf_op jit(solution)/shard_map/all_to_all | solution.py:25
  32.1 4.3 %collective-permute-start.5 = (bf16[128,4096]{1,0:T(8,128)(2,1)}, bf16[128,4096]{1,0:T(8,128)(2,1)}, u32[]{:S(2)}, u32[]{:S(2)}) collective-permute-start(bf16[128,4096]{1,0:T(8,128)(2,1)} %param.6), channel_id=1, source_target_pairs={{0,8},{8,0},{1,9},{9,1},{2,10},{10,2},{3,11},{11,3},{4,12},{12,4},... | collective-permute-start | bytes 3145736 | tf_op jit(solution)/shard_map/ppermute | solution.py:56
  36.4 0.0 copy-done
  36.4 10.7 %all-to-all-done.3 = bf16[16,8,32,128]{3,2,1,0:T(8,128)(2,1)S(1)} async-done(((bf16[16,8,32,128]{3,2,1,0:T(8,128)(2,1)}), bf16[16,8,32,128]{3,2,1,0:T(8,128)(2,1)S(1)}, u32[]{:S(2)}, u32[]{:S(2)}) %all-to-all-start.3) | async-done | bytes 1048608 | tf_op jit(solution)/shard_map/all_to_all | solution.py:25
  47.1 0.7 broadcast_in_dim.10
  47.8 3.4 %all-to-all-start = ((bf16[4,16,2048]{2,1,0:T(8,128)(2,1)}), bf16[4,16,2048]{2,1,0:T(8,128)(2,1)S(1)}, u32[]{:S(2)}, u32[]{:S(2)}) async-start(bf16[4,16,2048]{2,1,0:T(8,128)(2,1)} %broadcast_in_dim.10), calls=%async_computation | async-start | bytes 524288 | tf_op jit(solution)/shard_map/all_to_all | solution.py:25
  51.2 0.0 copy-start.3
  51.2 5.5 %collective-permute-start.2 = (bf16[128,2048]{1,0:T(8,128)(2,1)}, bf16[128,2048]{1,0:T(8,128)(2,1)S(1)}, u32[]{:S(2)}, u32[]{:S(2)}) collective-permute-start(bf16[128,2048]{1,0:T(8,128)(2,1)} %param.7), channel_id=1, source_target_pairs={{0,8},{8,0},{1,9},{9,1},{2,10},{10,2},{3,11},{11,3},{4,12},{12,4},... | collective-permute-start | bytes 1572872 | tf_op jit(solution)/shard_map/ppermute | solution.py:55
  56.8 0.1 copy.19
  56.9 1.6 fusion.11
  58.5 0.0 collective-permute-done.5
  58.6 1.6 fusion.12
  60.2 0.0 collective-permute-done.2
  60.2 0.0 copy-done.3
  60.2 0.0 copy-start.5
  60.2 0.5 convolution_multiply_fusion
  60.7 0.3 copy-done.5
  61.1 1.1 copy.20
  62.2 0.0 all-to-all-done
  62.2 23.1 %all_to_all.31 = f32[16,128,128]{2,1,0:T(8,128)S(1)} all-to-all(f32[16,128,128]{2,1,0:T(8,128)} %bitcast.47), channel_id=1, replica_groups=mesh['y'=4,'zh'=2,'x'=4,'c'=2,'q'=4,'p'=2] {'y','x'}, dimensions={0} | all-to-all | bytes 2097152 | tf_op jit(solution)/shard_map/all_to_all | solution.py:76
  85.2 2.5 %broadcast_in_dim.11 = bf16[16,4,16,2048]{3,2,1,0:T(8,128)(2,1)} broadcast(bf16[4,16,2048]{2,1,0:T(8,128)(2,1)S(1)} %all-to-all-done), dimensions={1,2,3} | broadcast | bytes 4456448 | tf_op jit(solution)/shard_map/broadcast_in_dim | solution.py:24
  87.8 4.5 %all-to-all-start.1 = ((bf16[16,4,16,2048]{3,2,1,0:T(8,128)(2,1)}), bf16[16,4,16,2048]{3,2,1,0:T(8,128)(2,1)}, u32[]{:S(2)}, u32[]{:S(2)}) async-start(bf16[16,4,16,2048]{3,2,1,0:T(8,128)(2,1)} %broadcast_in_dim.11), calls=%async_computation.1 | async-start | bytes 8388608 | tf_op jit(solution)/shard_map/all_to_all | solution.py:25
  92.3 5.3 %collective-permute-start = (bf16[128,2048]{1,0:T(8,128)(2,1)}, bf16[128,2048]{1,0:T(8,128)(2,1)}, u32[]{:S(2)}, u32[]{:S(2)}) collective-permute-start(bf16[128,2048]{1,0:T(8,128)(2,1)} %param.7), channel_id=1, source_target_pairs={{0,1},{1,0},{2,3},{3,2},{4,5},{5,4},{6,7},{7,6},{8,9},{9,8},{10,11... | collective-permute-start | bytes 1572872 | tf_op jit(solution)/shard_map/ppermute | solution.py:58
  97.6 10.1 %collective-permute-done = bf16[128,2048]{1,0:T(8,128)(2,1)} collective-permute-done((bf16[128,2048]{1,0:T(8,128)(2,1)}, bf16[128,2048]{1,0:T(8,128)(2,1)}, u32[]{:S(2)}, u32[]{:S(2)}) %collective-permute-start) | collective-permute-done | bytes 524320 | tf_op jit(solution)/shard_map/ppermute | solution.py:58
  107.7 5.0 %collective-permute-start.1 = (bf16[128,2048]{1,0:T(8,128)(2,1)}, bf16[128,2048]{1,0:T(8,128)(2,1)}, u32[]{:S(2)}, u32[]{:S(2)}) collective-permute-start(bf16[128,2048]{1,0:T(8,128)(2,1)} %collective-permute-done), channel_id=1, source_target_pairs={{0,8},{8,0},{1,9},{9,1},{2,10},{10,2},{3,11},{11,3},{4,12},{12,4},... | collective-permute-start | bytes 1572872 | tf_op jit(solution)/shard_map/ppermute | solution.py:59
  112.7 0.1 reduce_sum.18
  112.7 31.9 %all-to-all-done.1 = bf16[16,4,16,2048]{3,2,1,0:T(8,128)(2,1)} async-done(((bf16[16,4,16,2048]{3,2,1,0:T(8,128)(2,1)}), bf16[16,4,16,2048]{3,2,1,0:T(8,128)(2,1)}, u32[]{:S(2)}, u32[]{:S(2)}) %all-to-all-start.1) | async-done | bytes 4194336 | tf_op jit(solution)/shard_map/all_to_all | solution.py:25
  144.6 0.7 broadcast_in_dim.14
  145.3 19.7 %all-to-all-start.5 = ((bf16[32,32,128]{2,1,0:T(8,128)(2,1)}), bf16[32,32,128]{2,1,0:T(8,128)(2,1)S(1)}, u32[]{:S(2)}, u32[]{:S(2)}) async-start(bf16[32,32,128]{2,1,0:T(8,128)(2,1)} %bitcast.17), calls=%async_computation.5 | async-start | bytes 524288 | tf_op jit(solution)/shard_map/all_to_all | solution.py:79
  165.0 0.0 copy-start.4
  165.0 0.0 copy-start.6
  165.0 2.6 %copy.17 = bf16[16,4,16,2048]{3,2,0,1:T(8,128)(2,1)S(1)} copy(bf16[16,4,16,2048]{3,2,1,0:T(8,128)(2,1)} %all-to-all-done.1) | data formatting | bytes 8388608 | tf_op jit(solution)/shard_map/all_to_all | solution.py:25
  167.6 0.0 collective-permute-done.1
  167.6 0.0 copy-done.4
  167.6 3.6 %fusion.8 = bf16[512,1024]{1,0:T(8,128)(2,1)S(1)} fusion(bf16[1024,2048]{1,0:T(8,128)(2,1)S(1)} %bitcast.46, bf16[128,2048]{1,0:T(8,128)(2,1)S(1)} %copy-done.6, bf16[128,2048]{1,0:T(8,128)(2,1)S(1)} %copy-done.4, bf16[128,2048]{1,0:T(8,128)(2,1)} %collective-permute-done.1, bf16[128,2048]{1,0:T(8,128)(2,1)} %collective-permute-done), kind=kOutput, calls=%fused_computation.9 | convolution fusion | flops 2156396544 | bytes 7340032 | tf_op jit(solution)/shard_map/dot_general | solution.py:92
  171.2 0.0 copy-start.1
  171.2 0.0 copy-start.2
  171.2 0.8 slice.41
  172.1 3.3 %collective-permute-start.3 = (bf16[256,1024]{1,0:T(8,128)(2,1)}, bf16[256,1024]{1,0:T(8,128)(2,1)}, u32[]{:S(2)}, u32[]{:S(2)}) collective-permute-start(bf16[256,1024]{1,0:T(8,128)(2,1)} %slice.41), channel_id=1, source_target_pairs={{0,1},{1,0},{2,3},{3,2},{4,5},{5,4},{6,7},{7,6},{8,9},{9,8},{10,11... | collective-permute-start | bytes 1572872 | tf_op jit(solution)/shard_map/ppermute | solution.py:96
  175.4 11.0 %all-to-all-done.5 = bf16[32,32,128]{2,1,0:T(8,128)(2,1)S(1)} async-done(((bf16[32,32,128]{2,1,0:T(8,128)(2,1)}), bf16[32,32,128]{2,1,0:T(8,128)(2,1)S(1)}, u32[]{:S(2)}, u32[]{:S(2)}) %all-to-all-start.5) | async-done | bytes 262176 | tf_op jit(solution)/shard_map/all_to_all | solution.py:79
  186.4 0.1 copy.21
  186.5 0.1 reshape.175
  186.7 3.4 %collective-permute-done.3 = bf16[256,1024]{1,0:T(8,128)(2,1)} collective-permute-done((bf16[256,1024]{1,0:T(8,128)(2,1)}, bf16[256,1024]{1,0:T(8,128)(2,1)}, u32[]{:S(2)}, u32[]{:S(2)}) %collective-permute-start.3) | collective-permute-done | bytes 524320 | tf_op jit(solution)/shard_map/ppermute | solution.py:96
  190.1 1.1 fusion.24
  191.2 0.8 pad_maximum_fusion.1
  192.0 2.5 %collective-permute-start.4 = (bf16[2,128,1024]{2,1,0:T(8,128)(2,1)}, bf16[2,128,1024]{2,1,0:T(8,128)(2,1)}, u32[]{:S(2)}, u32[]{:S(2)}) collective-permute-start(bf16[2,128,1024]{2,1,0:T(8,128)(2,1)} %pad_maximum_fusion.1), channel_id=1, source_target_pairs={{0,8},{8,0},{1,9},{9,1},{2,10},{10,2},{3,11},{11,3},{4,12},{12,4},... | collective-permute-start | bytes 1572872 | tf_op jit(solution)/shard_map/ppermute | solution.py:99
  194.6 0.8 convert_reduce_fusion.1
  195.4 0.1 reshape.176
  195.5 1.8 convolution_bitcast_fusion
  197.2 0.2 stack.25
  197.4 0.1 constant_dynamic-update-slice_fusion.1
  197.5 0.2 stack.26
  197.7 0.1 constant_dynamic-update-slice_fusion
  197.8 0.0 collective-permute-done.4
  197.8 1.4 reshape.169
  199.3 0.1 broadcast_select_fusion.1
  199.4 0.5 select_bitcast_fusion.2
  199.8 1.0 pad_maximum_fusion
  200.8 1.4 copy.18
  202.1 1.6 reshape.170
  (7 shorter events, 0.1 us)
Async XLA Ops:
  0.6 35.8 %copy-start = (bf16[512,2048]{1,0:T(8,128)(2,1)S(1)}, bf16[512,2048]{1,0:T(8,128)(2,1)}, u32[]{:S(2)}) copy-start(bf16[512,2048]{1,0:T(8,128)(2,1)} %param.8) | copy-start | bytes 6291460
  25.3 21.8 %all-to-all-start.3 = ((bf16[16,8,32,128]{3,2,1,0:T(8,128)(2,1)}), bf16[16,8,32,128]{3,2,1,0:T(8,128)(2,1)S(1)}, u32[]{:S(2)}, u32[]{:S(2)}) async-start(bf16[16,8,32,128]{3,2,1,0:T(8,128)(2,1)} %broadcast_in_dim.13), calls=%async_computation.3 | async-start | bytes 2097152 | tf_op jit(solution)/shard_map/all_to_all | solution.py:25
  32.1 26.5 %collective-permute-start.5 = (bf16[128,4096]{1,0:T(8,128)(2,1)}, bf16[128,4096]{1,0:T(8,128)(2,1)}, u32[]{:S(2)}, u32[]{:S(2)}) collective-permute-start(bf16[128,4096]{1,0:T(8,128)(2,1)} %param.6), channel_id=1, source_target_pairs={{0,8},{8,0},{1,9},{9,1},{2,10},{10,2},{3,11},{11,3},{4,12},{12,4},... | collective-permute-start | bytes 3145736 | tf_op jit(solution)/shard_map/ppermute | solution.py:56
  47.8 14.3 %all-to-all-start = ((bf16[4,16,2048]{2,1,0:T(8,128)(2,1)}), bf16[4,16,2048]{2,1,0:T(8,128)(2,1)S(1)}, u32[]{:S(2)}, u32[]{:S(2)}) async-start(bf16[4,16,2048]{2,1,0:T(8,128)(2,1)} %broadcast_in_dim.10), calls=%async_computation | async-start | bytes 524288 | tf_op jit(solution)/shard_map/all_to_all | solution.py:25
  51.2 9.0 %copy-start.3 = (bf16[128,2048]{1,0:T(8,128)(2,1)S(1)}, bf16[128,2048]{1,0:T(8,128)(2,1)}, u32[]{:S(2)}) copy-start(bf16[128,2048]{1,0:T(8,128)(2,1)} %param.7) | copy-start | bytes 1572868
  51.2 9.0 %collective-permute-start.2 = (bf16[128,2048]{1,0:T(8,128)(2,1)}, bf16[128,2048]{1,0:T(8,128)(2,1)S(1)}, u32[]{:S(2)}, u32[]{:S(2)}) collective-permute-start(bf16[128,2048]{1,0:T(8,128)(2,1)} %param.7), channel_id=1, source_target_pairs={{0,8},{8,0},{1,9},{9,1},{2,10},{10,2},{3,11},{11,3},{4,12},{12,4},... | collective-permute-start | bytes 1572872 | tf_op jit(solution)/shard_map/ppermute | solution.py:55
  60.2 0.8 copy-start.5
  87.8 56.8 %all-to-all-start.1 = ((bf16[16,4,16,2048]{3,2,1,0:T(8,128)(2,1)}), bf16[16,4,16,2048]{3,2,1,0:T(8,128)(2,1)}, u32[]{:S(2)}, u32[]{:S(2)}) async-start(bf16[16,4,16,2048]{3,2,1,0:T(8,128)(2,1)} %broadcast_in_dim.11), calls=%async_computation.1 | async-start | bytes 8388608 | tf_op jit(solution)/shard_map/all_to_all | solution.py:25
  92.3 15.4 %collective-permute-start = (bf16[128,2048]{1,0:T(8,128)(2,1)}, bf16[128,2048]{1,0:T(8,128)(2,1)}, u32[]{:S(2)}, u32[]{:S(2)}) collective-permute-start(bf16[128,2048]{1,0:T(8,128)(2,1)} %param.7), channel_id=1, source_target_pairs={{0,1},{1,0},{2,3},{3,2},{4,5},{5,4},{6,7},{7,6},{8,9},{9,8},{10,11... | collective-permute-start | bytes 1572872 | tf_op jit(solution)/shard_map/ppermute | solution.py:58
  107.7 59.9 %collective-permute-start.1 = (bf16[128,2048]{1,0:T(8,128)(2,1)}, bf16[128,2048]{1,0:T(8,128)(2,1)}, u32[]{:S(2)}, u32[]{:S(2)}) collective-permute-start(bf16[128,2048]{1,0:T(8,128)(2,1)} %collective-permute-done), channel_id=1, source_target_pairs={{0,8},{8,0},{1,9},{9,1},{2,10},{10,2},{3,11},{11,3},{4,12},{12,4},... | collective-permute-start | bytes 1572872 | tf_op jit(solution)/shard_map/ppermute | solution.py:59
  145.3 41.1 %all-to-all-start.5 = ((bf16[32,32,128]{2,1,0:T(8,128)(2,1)}), bf16[32,32,128]{2,1,0:T(8,128)(2,1)S(1)}, u32[]{:S(2)}, u32[]{:S(2)}) async-start(bf16[32,32,128]{2,1,0:T(8,128)(2,1)} %bitcast.17), calls=%async_computation.5 | async-start | bytes 524288 | tf_op jit(solution)/shard_map/all_to_all | solution.py:79
  165.0 2.6 %copy-start.4 = (bf16[128,2048]{1,0:T(8,128)(2,1)S(1)}, bf16[128,2048]{1,0:T(8,128)(2,1)}, u32[]{:S(2)}) copy-start(bf16[128,2048]{1,0:T(8,128)(2,1)} %param.7) | copy-start | bytes 1572868
  165.0 2.6 %copy-start.6 = (bf16[128,2048]{1,0:T(8,128)(2,1)S(1)}, bf16[128,2048]{1,0:T(8,128)(2,1)}, u32[]{:S(2)}) copy-start(bf16[128,2048]{1,0:T(8,128)(2,1)} %copy-done.5) | copy-start | bytes 1572868
  171.2 23.3 %copy-start.1 = (f32[1,8192]{1,0:T(1,128)S(1)}, f32[1,8192]{1,0:T(1,128)}, u32[]{:S(2)}) copy-start(f32[1,8192]{1,0:T(1,128)} %param.11) | copy-start | bytes 98308
  171.2 23.3 %copy-start.2 = (f32[1,8192]{1,0:T(1,128)S(1)}, f32[1,8192]{1,0:T(1,128)}, u32[]{:S(2)}) copy-start(f32[1,8192]{1,0:T(1,128)} %param.10) | copy-start | bytes 98308
  172.1 18.1 %collective-permute-start.3 = (bf16[256,1024]{1,0:T(8,128)(2,1)}, bf16[256,1024]{1,0:T(8,128)(2,1)}, u32[]{:S(2)}, u32[]{:S(2)}) collective-permute-start(bf16[256,1024]{1,0:T(8,128)(2,1)} %slice.41), channel_id=1, source_target_pairs={{0,1},{1,0},{2,3},{3,2},{4,5},{5,4},{6,7},{7,6},{8,9},{9,8},{10,11... | collective-permute-start | bytes 1572872 | tf_op jit(solution)/shard_map/ppermute | solution.py:96
  192.0 5.8 %collective-permute-start.4 = (bf16[2,128,1024]{2,1,0:T(8,128)(2,1)}, bf16[2,128,1024]{2,1,0:T(8,128)(2,1)}, u32[]{:S(2)}, u32[]{:S(2)}) collective-permute-start(bf16[2,128,1024]{2,1,0:T(8,128)(2,1)} %pad_maximum_fusion.1), channel_id=1, source_target_pairs={{0,8},{8,0},{1,9},{9,1},{2,10},{10,2},{3,11},{11,3},{4,12},{12,4},... | collective-permute-start | bytes 1572872 | tf_op jit(solution)/shard_map/ppermute | solution.py:99

commit v2 on v1

v2 whole, which is shorter than its diff:
```python
import functools
import math

import jax
import jax.numpy as jnp
from jax import lax
from jax.experimental import pallas as pl
from jax.experimental.pallas import tpu as pltpu
from jax.sharding import Mesh
from jax.sharding import PartitionSpec as P

STEP = 1000

beta_one = 0.9
beta_two = 0.999
epsilon = 1e-08

AXES = ("y", "zh", "x", "c", "q", "p")
SIZES = (4, 2, 4, 2, 4, 2)
PLANE = ("y", "x")
LINE = ("q", "p")
COLUMN = ("zh", "c", "q", "p")
SWAP = [(0, 1), (1, 0)]
F32, BF16 = jnp.float32, jnp.bfloat16
PARAMS = pltpu.CompilerParams(vmem_limit_bytes=40 * 1024 * 1024)


def spread(block, axes, count):
    sent = jnp.broadcast_to(block[None], (count,) + block.shape)
    return lax.all_to_all(sent, axes, 0, 0, tiled=True)


def dot(a, b, dims):
    return lax.dot_general(a, b, (dims, ((), ())), preferred_element_type=F32)


def low_kernel(scale, x0, x1, g0, g1, basis, out):
    shards, half = basis.shape[1], basis.shape[3]
    depth = basis.shape[0] * basis.shape[2]
    proj = []
    for x in (x0, x1):
        total = None
        for s in range(shards):
            part = dot(
                x[:, s * depth : (s + 1) * depth],
                basis[:, s].reshape(depth, half),
                ((1,), (0,)),
            )
            total = part if total is None else total + part
        proj.append(total.astype(BF16))
    width = out.shape[1] // 2
    for y in range(4):
        for zh in range(2):
            at = (y * 2 + zh) * 4 * width
            part = dot(g0[:, at : at + 4 * width], proj[0], ((0,), (0,))) + dot(
                g1[:, at : at + 4 * width], proj[1], ((0,), (0,))
            )
            part = part * scale
            for x in range(4):
                out[y * 4 + x, zh * width : (zh + 1) * width, :] = part[
                    x * width : (x + 1) * width
                ]


def low_rank(x0, x1, g0, g1, basis, scale):
    cols, half = g0.shape[1], basis.shape[3]
    n = x0.shape[0]
    flops = 4 * n * half * (x0.shape[1] + cols)
    return pl.pallas_call(
        functools.partial(low_kernel, scale),
        out_shape=jax.ShapeDtypeStruct((16, cols // 16, half), F32),
        compiler_params=PARAMS,
        cost_estimate=pl.CostEstimate(flops=flops, bytes_accessed=6 << 20, transcendentals=0),
        name="low_rank",
    )(x0, x1, g0, g1, basis)


def feature_kernel(core, a, b, own, rest, out):
    del core
    n = a.shape[0]

    def write(rows):
        out[:n, :] = dot(a[...], rows, ((1,), (1,))).astype(BF16)
        out[n:, :] = dot(b[...], rows, ((1,), (1,))).astype(BF16)

    @pl.when(pl.program_id(0) == 0)
    def _():
        write(own[...])

    @pl.when(pl.program_id(0) > 0)
    def _():
        write(rest[...].reshape(own.shape))


def features(core, a, b, own, rest):
    n, depth = a.shape
    feat = own.shape[0] // 2
    rows = rest.shape[2]
    spec = pltpu.PrefetchScalarGridSpec(
        num_scalar_prefetch=1,
        grid=(4,),
        in_specs=[
            pl.BlockSpec((n, depth), lambda r, c: (0, 0)),
            pl.BlockSpec((n, depth), lambda r, c: (0, 0)),
            pl.BlockSpec((feat, depth), lambda r, c: (c[0], 0)),
            pl.BlockSpec((16, None, rows, depth), lambda r, c: (0, jnp.maximum(r - 1, 0), 0, 0)),
        ],
        out_specs=pl.BlockSpec((2 * n, feat), lambda r, c: (0, r)),
    )
    return pl.pallas_call(
        feature_kernel,
        grid_spec=spec,
        out_shape=jax.ShapeDtypeStruct((2 * n, 4 * feat), BF16),
        compiler_params=PARAMS,
        cost_estimate=pl.CostEstimate(
            flops=16 * n * depth * feat, bytes_accessed=6 << 20, transcendentals=0
        ),
        name="features",
    )(core[None], a, b, own, rest)


def assemble_kernel(where, mine, core_own, core_back, back, out):
    quad, parity, core = where[0], where[1], where[2]
    feat = mine.shape[1] // 4
    for ref, par, half in (
        (mine, parity, core),
        (core_own, parity, 1 - core),
        (back, 1 - parity, core),
        (core_back, 1 - parity, 1 - core),
    ):
        for r in range(4):
            shard = lax.rem(quad + r, 4) * 2 + par
            at = pl.multiple_of((shard * 2 + half) * feat, feat)
            out[:, pl.ds(at, feat)] = ref[:, r * feat : (r + 1) * feat]


def assemble(where, mine, core_own, core_back, back):
    n, wide = core_own.shape
    spec = pltpu.PrefetchScalarGridSpec(
        num_scalar_prefetch=1,
        grid=(1,),
        in_specs=[pl.BlockSpec((n, wide), lambda i, w: (0, 0))] * 4,
        out_specs=pl.BlockSpec((n, 4 * wide), lambda i, w: (0, 0)),
    )
    return pl.pallas_call(
        assemble_kernel,
        grid_spec=spec,
        out_shape=jax.ShapeDtypeStruct((n, 4 * wide), BF16),
        compiler_params=PARAMS,
        cost_estimate=pl.CostEstimate(flops=0, bytes_accessed=2 << 20, transcendentals=0),
        name="assemble",
    )(where, mine, core_own, core_back, back)


def on_device(inputs, out_grad, weight, proj_basis, first_moment, second_moment):
    core = lax.axis_index("c")
    parity = lax.axis_index("p")
    quad = lax.axis_index("q")
    plane = lax.axis_index(PLANE)
    n, feat = inputs.shape[0], weight.shape[0] // 2
    scale = 1.0 / math.sqrt(n * 512)
    half = proj_basis.shape[1] // 2

    rows = feat // 16
    piece = lax.dynamic_slice(weight, (core * feat + plane * rows, 0), (rows, weight.shape[1]))
    p_rows = proj_basis.shape[0] // 16
    p_piece = lax.dynamic_slice(proj_basis, (plane * p_rows, core * half), (p_rows, half))
    line = jnp.stack(
        [lax.ppermute(piece, "q", [((i + r) % 4, i) for i in range(4)]) for r in (1, 2, 3)]
    )
    rest = lax.all_gather(line, PLANE, axis=0)
    p_line = spread(p_piece, LINE, 8)
    basis = spread(p_line, PLANE, 16)

    grad_z = lax.ppermute(out_grad, "p", SWAP)
    grad_c = lax.ppermute(out_grad, "c", SWAP)
    inputs_c = lax.ppermute(inputs, "c", SWAP)
    grad_zc = lax.ppermute(grad_z, "c", SWAP)
    basis, inputs_c, grad_c, grad_z, grad_zc = lax.optimization_barrier(
        (basis, inputs_c, grad_c, grad_z, grad_zc)
    )

    low = low_rank(inputs, inputs_c, out_grad, grad_c, basis, scale)
    cols = low.shape[1] // 4
    low = lax.all_to_all(low, PLANE, 0, 0, tiled=True).sum(axis=0)
    low = low.reshape(2, 2, 1, cols, half).astype(BF16)
    low = jnp.broadcast_to(low, (2, 2, 8, cols, half)).reshape(32, cols, half)
    low = lax.all_to_all(low, COLUMN, 0, 0, tiled=True).reshape(2, 2, 8, cols, half)
    low = low.astype(F32).sum(axis=(0, 2))
    flat_grad = low.transpose(0, 2, 1).reshape(1, 2 * half * cols)
    new_first = beta_one * first_moment + (1.0 - beta_one) * flat_grad
    new_second = beta_two * second_moment + (1.0 - beta_two) * flat_grad * flat_grad
    corr_one = 1.0 - beta_one**STEP
    corr_two = 1.0 - beta_two**STEP
    direction = (new_first / corr_one / (jnp.sqrt(new_second / corr_two) + epsilon)).astype(BF16)
    direction = direction.reshape(2 * half, cols)
    update = jnp.dot(proj_basis, direction, preferred_element_type=F32)

    far = features(core, grad_z, grad_zc, weight, rest)
    back = lax.ppermute(far, "p", SWAP)
    near = features(core, out_grad, grad_c, weight, rest)
    core_own = lax.ppermute(near[n:], "c", SWAP)
    core_back = lax.ppermute(back[n:], "c", SWAP)
    where = jnp.stack([quad, parity, core])
    input_grad = assemble(where, near, core_own, core_back, back)
    return (input_grad, new_first, new_second, update)


def solution(mesh):
    fine = Mesh(mesh.devices.reshape(SIZES), AXES)
    dp, fsdp = AXES[:4], AXES[4:]
    in_specs = (
        P(AXES, None),
        P(AXES, None),
        P(fsdp, None),
        P(fsdp, None),
        P(dp, None),
        P(dp, None),
    )
    out_specs = (P(AXES, None), P(dp, None), P(dp, None), P(fsdp, dp))
    return jax.shard_map(
        on_device, mesh=fine, in_specs=in_specs, out_specs=out_specs, check_vma=False
    )
```

time: 205 us -> 167 us (0.81)
  waiting for transfers between devices: 67.1 us -> 27 us
  blocking collectives: 45.7 us -> 23.1 us
  Pallas kernels: 0 us -> 14 us
  between operations: 1.01 us -> 14.4 us
  starting transfers between devices: 60.2 us -> 69 us
  matrix products: 9.14 us -> 0.82 us
    all_to_all x3 -> x2, waiting for transfers between devices: 42.5 us -> 8.33 us  [spread(): return lax.all_to_all(sent, axes, 0, 0, tiled=True)]
    all_to_all x1 -> x0, blocking collectives: 22.6 us -> none  [spread(): return lax.all_to_all(sent, axes, 0, 0, tiled=True)]
    ppermute x2 -> x6, starting transfers between devices: 5.77 us -> 24.9 us  [the longest x3 16.5 us: on_device(): lax.ppermute(piece, 'q', [((i + r) % 4, i) for i in range(4)])]
    pallas_call x0 -> x4, Pallas kernels: none -> 14 us  [the longest x2 9.02 us: features(): pl.pallas_call(feature_kernel, grid_spec=spec, out_shape=jax.ShapeDtypeSt...]
    unnamed x15 -> x32, local copies, waits for them, and re-layouts: 0.47 us -> 10.8 us
    ppermute x1, waiting for transfers between devices: 10.1 us -> 0.01 us  [on_device(): grad_z = lax.ppermute(out_grad, 'p', SWAP)]
    dot_general x5 -> x1, matrix products: 9.14 us -> 0.82 us  [on_device(): update = jnp.dot(proj_basis, direction, preferred_element_type=F32)]
    ppermute x2 -> x6, waiting for transfers between devices: 3.44 us -> 8.51 us  [the longest x3 8.51 us: on_device(): lax.ppermute(piece, 'q', [((i + r) % 4, i) for i in range(4)])]
  transfers between devices with their start and end apart: 10 -> 14, of which waited for: 5 -> 6; matrix products, arithmetic and copies ran while one was open for 8% -> 4% of each run, Pallas kernels for 0% -> 7%
where the time goes in v2:
time: 167 us; the launch traced here: 166 us
  starting transfers between devices  69 us (41%)
  waiting for transfers between devices  27 us (16%)
  blocking collectives  23.1 us (14%)
  local copies, waits for them, and re-layouts  16.4 us (10%)
  between operations  14.4 us (9%)
  Pallas kernels  14 us (8%)
  other arithmetic  1.68 us (1%)
    all_to_all x1, blocking collectives, on_device(): low = lax.all_to_all(low, PLANE, 0, 0, tiled=True).sum(axis=0)  23.1 us
    ppermute x3, starting transfers between devices, on_device(): lax.ppermute(piece, 'q', [((i + r) % 4, i) for i in range(4)])  16.5 us
    all_to_all x1, starting transfers between devices, on_device(): lax.all_to_all(low, COLUMN, 0, 0, tiled=True).reshape(2, 2, 8, cols, half)  16.2 us
    all_to_all x2, starting transfers between devices, spread(): return lax.all_to_all(sent, axes, 0, 0, tiled=True)  14.1 us
    unnamed x32, local copies, waits for them, and re-layouts  10.8 us
    pallas_call x2, Pallas kernels, features(): pl.pallas_call(feature_kernel, grid_spec=spec, out_shape=jax.ShapeDtypeSt...  9.02 us
    ppermute x3, waiting for transfers between devices, on_device(): lax.ppermute(piece, 'q', [((i + r) % 4, i) for i in range(4)])  8.51 us
    all_to_all x2, waiting for transfers between devices, spread(): return lax.all_to_all(sent, axes, 0, 0, tiled=True)  8.33 us
  transfers between devices with their start and end apart: 14, of which 6 were waited for; matrix products, arithmetic and copies ran while one was open for 4% of the time, Pallas kernels for 7%

profile of v2, /device:TPU:1, one launch (start us, length us, event | category | flops | bytes accessed | tf_op | source)
XLA Modules:
  0.0 166.3 jit_solution(9933625860291404174)
XLA Ops:
  7.2 0.0 all-gather.3.cloned.1.call-start
  7.2 0.0 copy-start.6
  7.2 0.0 copy-start.10
  7.2 1.0 constant_dynamic-slice_fusion
  8.2 12.3 %collective-permute-start.4 = (bf16[16,2048]{1,0:T(8,128)(2,1)S(1)}, bf16[16,2048]{1,0:T(8,128)(2,1)S(1)}, u32[]{:S(2)}, u32[]{:S(2)}) collective-permute-start(bf16[16,2048]{1,0:T(8,128)(2,1)S(1)} %constant_dynamic-slice_fusion), channel_id=1, source_target_pairs={{2,0},{4,2},{6,4},{0,6},{3,1},{5,3},{7,5},{1,7},{10,8},{12,10},{14... | collective-permute-start | bytes 196616 | tf_op jit(solution)/shard_map/ppermute | solution.py:169
  20.6 1.9 %collective-permute-start.5 = (bf16[16,2048]{1,0:T(8,128)(2,1)S(1)}, bf16[16,2048]{1,0:T(8,128)(2,1)S(1)}, u32[]{:S(2)}, u32[]{:S(2)}) collective-permute-start(bf16[16,2048]{1,0:T(8,128)(2,1)S(1)} %constant_dynamic-slice_fusion), channel_id=1, source_target_pairs={{4,0},{6,2},{0,4},{2,6},{5,1},{7,3},{1,5},{3,7},{12,8},{14,10},{8,... | collective-permute-start | bytes 196616 | tf_op jit(solution)/shard_map/ppermute | solution.py:169
  22.5 2.2 %collective-permute-start.6 = (bf16[16,2048]{1,0:T(8,128)(2,1)S(1)}, bf16[16,2048]{1,0:T(8,128)(2,1)S(1)}, u32[]{:S(2)}, u32[]{:S(2)}) collective-permute-start(bf16[16,2048]{1,0:T(8,128)(2,1)S(1)} %constant_dynamic-slice_fusion), channel_id=1, source_target_pairs={{6,0},{0,2},{2,4},{4,6},{7,1},{1,3},{3,5},{5,7},{14,8},{8,10},{10,... | collective-permute-start | bytes 196616 | tf_op jit(solution)/shard_map/ppermute | solution.py:169
  24.7 0.0 collective-permute-done.4
  24.7 4.8 %collective-permute-done.5 = bf16[16,2048]{1,0:T(8,128)(2,1)S(1)} collective-permute-done((bf16[16,2048]{1,0:T(8,128)(2,1)S(1)}, bf16[16,2048]{1,0:T(8,128)(2,1)S(1)}, u32[]{:S(2)}, u32[]{:S(2)}) %collective-permute-start.5) | collective-permute-done | bytes 65568 | tf_op jit(solution)/shard_map/ppermute | solution.py:169
  29.5 3.7 %collective-permute-done.6 = bf16[16,2048]{1,0:T(8,128)(2,1)S(1)} collective-permute-done((bf16[16,2048]{1,0:T(8,128)(2,1)S(1)}, bf16[16,2048]{1,0:T(8,128)(2,1)S(1)}, u32[]{:S(2)}, u32[]{:S(2)}) %collective-permute-start.6) | collective-permute-done | bytes 65568 | tf_op jit(solution)/shard_map/ppermute | solution.py:169
  33.2 0.7 pad_maximum_fusion
  33.9 0.0 all-gather.3.cloned.1.call-update
  33.9 0.7 dynamic_slice.6
  34.6 0.6 broadcast_in_dim.6
  35.3 7.3 %all-to-all-start = ((bf16[8,32,128]{2,1,0:T(8,128)(2,1)}), bf16[8,32,128]{2,1,0:T(8,128)(2,1)S(1)}, u32[]{:S(2)}, u32[]{:S(2)}) async-start(bf16[8,32,128]{2,1,0:T(8,128)(2,1)} %broadcast_in_dim.6), calls=%async_computation | async-start | bytes 131072 | tf_op jit(solution)/shard_map/all_to_all | solution.py:30
  42.6 3.4 %collective-permute-start.2 = (bf16[128,2048]{1,0:T(8,128)(2,1)}, bf16[128,2048]{1,0:T(8,128)(2,1)}, u32[]{:S(2)}, u32[]{:S(2)}) collective-permute-start(bf16[128,2048]{1,0:T(8,128)(2,1)} %g0.1), channel_id=1, source_target_pairs={{0,1},{1,0},{2,3},{3,2},{4,5},{5,4},{6,7},{7,6},{8,9},{9,8},{10,11... | collective-permute-start | bytes 1572872 | tf_op jit(solution)/shard_map/ppermute | solution.py:175
  46.0 3.7 %collective-permute-start = (bf16[128,4096]{1,0:T(8,128)(2,1)}, bf16[128,4096]{1,0:T(8,128)(2,1)}, u32[]{:S(2)}, u32[]{:S(2)}) collective-permute-start(bf16[128,4096]{1,0:T(8,128)(2,1)} %x0.1), channel_id=1, source_target_pairs={{0,8},{8,0},{1,9},{9,1},{2,10},{10,2},{3,11},{11,3},{4,12},{12,4},... | collective-permute-start | bytes 3145736 | tf_op jit(solution)/shard_map/ppermute | solution.py:177
  49.7 2.7 %all-to-all-done = bf16[8,32,128]{2,1,0:T(8,128)(2,1)S(1)} async-done(((bf16[8,32,128]{2,1,0:T(8,128)(2,1)}), bf16[8,32,128]{2,1,0:T(8,128)(2,1)S(1)}, u32[]{:S(2)}, u32[]{:S(2)}) %all-to-all-start) | async-done | bytes 65568 | tf_op jit(solution)/shard_map/all_to_all | solution.py:30
  52.4 1.2 broadcast_in_dim.7
  53.5 6.8 %all-to-all-start.1 = ((bf16[16,8,32,128]{3,2,1,0:T(8,128)(2,1)}), bf16[16,8,32,128]{3,2,1,0:T(8,128)(2,1)S(1)}, u32[]{:S(2)}, u32[]{:S(2)}) async-start(bf16[16,8,32,128]{3,2,1,0:T(8,128)(2,1)} %broadcast_in_dim.7), calls=%async_computation.1 | async-start | bytes 2097152 | tf_op jit(solution)/shard_map/all_to_all | solution.py:30
  60.3 4.7 %collective-permute-start.1 = (bf16[128,2048]{1,0:T(8,128)(2,1)S(1)}, bf16[128,2048]{1,0:T(8,128)(2,1)S(1)}, u32[]{:S(2)}, u32[]{:S(2)}) collective-permute-start(bf16[128,2048]{1,0:T(8,128)(2,1)S(1)} %copy-done.6), channel_id=1, source_target_pairs={{0,8},{8,0},{1,9},{9,1},{2,10},{10,2},{3,11},{11,3},{4,12},{12,4},... | collective-permute-start | bytes 1572872 | tf_op jit(solution)/shard_map/ppermute | solution.py:176
  65.1 0.0 collective-permute-done.2.a
  65.1 1.9 %collective-permute-start.3 = (bf16[128,2048]{1,0:T(8,128)(2,1)}, bf16[128,2048]{1,0:T(8,128)(2,1)S(1)}, u32[]{:S(2)}, u32[]{:S(2)}) collective-permute-start(bf16[128,2048]{1,0:T(8,128)(2,1)} %collective-permute-done.2.a), channel_id=1, source_target_pairs={{0,8},{8,0},{1,9},{9,1},{2,10},{10,2},{3,11},{11,3},{4,12},{12,4},... | collective-permute-start | bytes 1572872 | tf_op jit(solution)/shard_map/ppermute | solution.py:178
  67.0 0.0 collective-permute-done.1.b.g1
  67.0 0.0 copy-start.8
  67.0 2.1 %collective-permute-done.3.b = bf16[128,2048]{1,0:T(8,128)(2,1)S(1)} collective-permute-done((bf16[128,2048]{1,0:T(8,128)(2,1)}, bf16[128,2048]{1,0:T(8,128)(2,1)S(1)}, u32[]{:S(2)}, u32[]{:S(2)}) %collective-permute-start.3) | collective-permute-done | bytes 524320 | tf_op jit(solution)/shard_map/ppermute | solution.py:178
  69.1 0.8 copy-done.11
  69.9 0.0 collective-permute-done.x1
  69.9 5.7 %all-to-all-done.1.basis = bf16[16,8,32,128]{3,2,1,0:T(8,128)(2,1)S(1)} async-done(((bf16[16,8,32,128]{3,2,1,0:T(8,128)(2,1)}), bf16[16,8,32,128]{3,2,1,0:T(8,128)(2,1)S(1)}, u32[]{:S(2)}, u32[]{:S(2)}) %all-to-all-start.1) | async-done | bytes 1048608 | tf_op jit(solution)/shard_map/all_to_all | solution.py:30
  75.6 2.3 %low_rank.1 = f32[16,128,128]{2,1,0:T(8,128)S(1)} custom-call(bf16[128,4096]{1,0:T(8,128)(2,1)S(1)} %copy-done.10, bf16[128,4096]{1,0:T(8,128)(2,1)} %collective-permute-done.x1, bf16[128,2048]{1,0:T(8,128)(2,1)S(1)} %copy-done.6, bf16[128,2048]{1,0:T(8,128)(2,1)S(1)} %collective-permute-done.1.b.g1, bf16[16,8,32,128]{3,2,1,0:T(8,128)(2,1)S(1)} %all-to-all-done.1.basis), custom_call_target="tpu_custom_call" | custom-call | flops 402653184 | bytes 6291456 | tf_op jit(solution)/shard_map/low_rank/pallas_call | solution.py:69
  77.9 23.1 %all_to_all.20 = f32[16,128,128]{2,1,0:T(8,128)S(1)} all-to-all(f32[16,128,128]{2,1,0:T(8,128)S(1)} %low_rank.1), channel_id=1, replica_groups=mesh['y'=4,'zh'=2,'x'=4,'c'=2,'q'=4,'p'=2] {'y','x'}, dimensions={0} | all-to-all | bytes 2097152 | tf_op jit(solution)/shard_map/all_to_all | solution.py:185
  101.1 0.1 reduce_sum.18
  101.1 0.7 broadcast_in_dim.8
  101.9 16.2 %all-to-all-start.3 = ((bf16[32,32,128]{2,1,0:T(8,128)(2,1)}), bf16[32,32,128]{2,1,0:T(8,128)(2,1)S(1)}, u32[]{:S(2)}, u32[]{:S(2)}) async-start(bf16[32,32,128]{2,1,0:T(8,128)(2,1)} %bitcast.8), calls=%async_computation.3 | async-start | bytes 524288 | tf_op jit(solution)/shard_map/all_to_all | solution.py:188
  118.1 0.0 all-gather.3.cloned.1.call-done
  118.1 1.9 %copy-done = bf16[48,16,2048]{2,1,0:T(8,128)(2,1)S(1)} copy-done((bf16[48,16,2048]{2,1,0:T(8,128)(2,1)S(1)}, bf16[48,16,2048]{2,1,0:T(8,128)(2,1)}, u32[]{:S(2)}) %copy-start) | copy-done | bytes 3145752
  120.0 1.6 copy-done.2
  121.6 1.0 copy-done.12
  122.6 5.4 %features.3 = bf16[256,1024]{1,0:T(8,128)(2,1)} custom-call(s32[1]{0:T(128)} %bitcast.2.core, bf16[128,2048]{1,0:T(8,128)(2,1)} %collective-permute-done.2.a, bf16[128,2048]{1,0:T(8,128)(2,1)S(1)} %copy-done.12, bf16[512,2048]{1,0:T(8,128)(2,1)S(1)} %copy-done.2, bf16[16,3,16,2048]{3,2,1,0:T(8,128)(2,1)S(1)} %bitcast.16), custom_call_target="tpu_custom_call" | custom-call | flops 1073741824 | bytes 6291456 | tf_op jit(solution)/shard_map/features/pallas_call | solution.py:110
  128.0 3.3 %collective-permute-start.8 = (bf16[256,1024]{1,0:T(8,128)(2,1)}, bf16[256,1024]{1,0:T(8,128)(2,1)}, u32[]{:S(2)}, u32[]{:S(2)}) collective-permute-start(bf16[256,1024]{1,0:T(8,128)(2,1)} %features.3), channel_id=1, source_target_pairs={{0,1},{1,0},{2,3},{3,2},{4,5},{5,4},{6,7},{7,6},{8,9},{9,8},{10,11... | collective-permute-start | bytes 1572872 | tf_op jit(solution)/shard_map/ppermute | solution.py:200
  131.3 0.1 pad_add_fusion.where
  131.4 8.0 %all-to-all-done.3 = bf16[32,32,128]{2,1,0:T(8,128)(2,1)S(1)} async-done(((bf16[32,32,128]{2,1,0:T(8,128)(2,1)}), bf16[32,32,128]{2,1,0:T(8,128)(2,1)S(1)}, u32[]{:S(2)}, u32[]{:S(2)}) %all-to-all-start.3) | async-done | bytes 262176 | tf_op jit(solution)/shard_map/all_to_all | solution.py:188
  139.5 0.1 copy.10
  139.6 0.1 reshape.68
  139.7 0.0 copy-start.3
  139.7 1.6 copy-done.3
  141.3 1.0 copy-done.7
  142.4 1.0 copy-done.9
  143.4 3.6 %features.2.mine = bf16[256,1024]{1,0:T(8,128)(2,1)S(1)} custom-call(s32[1]{0:T(128)} %bitcast.2.core, bf16[128,2048]{1,0:T(8,128)(2,1)S(1)} %copy-done.7, bf16[128,2048]{1,0:T(8,128)(2,1)S(1)} %copy-done.9, bf16[512,2048]{1,0:T(8,128)(2,1)S(1)} %copy-done.3, bf16[16,3,16,2048]{3,2,1,0:T(8,128)(2,1)S(1)} %bitcast.17), custom_call_target="tpu_custom_call" | custom-call | flops 1073741824 | bytes 6291456 | tf_op jit(solution)/shard_map/features/pallas_call | solution.py:110
  147.1 0.0 copy-start.4
  147.1 0.8 copy-done.4
  147.8 3.3 %collective-permute-start.7 = (bf16[128,1024]{1,0:T(8,128)(2,1)S(1)}, bf16[128,1024]{1,0:T(8,128)(2,1)S(1)}, u32[]{:S(2)}, u32[]{:S(2)}) collective-permute-start(bf16[128,1024]{1,0:T(8,128)(2,1)S(1)} %slice.8), channel_id=1, source_target_pairs={{0,8},{8,0},{1,9},{9,1},{2,10},{10,2},{3,11},{11,3},{4,12},{12,4},... | collective-permute-start | bytes 786440 | tf_op jit(solution)/shard_map/ppermute | solution.py:202
  151.1 0.0 collective-permute-done.8.back
  151.2 1.0 slice.9
  152.1 1.9 %collective-permute-start.9 = (bf16[128,1024]{1,0:T(8,128)(2,1)S(1)}, bf16[128,1024]{1,0:T(8,128)(2,1)S(1)}, u32[]{:S(2)}, u32[]{:S(2)}) collective-permute-start(bf16[128,1024]{1,0:T(8,128)(2,1)S(1)} %slice.9), channel_id=1, source_target_pairs={{0,8},{8,0},{1,9},{9,1},{2,10},{10,2},{3,11},{11,3},{4,12},{12,4},... | collective-permute-start | bytes 786440 | tf_op jit(solution)/shard_map/ppermute | solution.py:203
  154.1 0.0 copy-done.14
  154.1 0.0 copy-done.15
  154.1 0.8 convert_reduce_fusion.1
  154.9 0.1 reshape.69
  155.0 0.8 convolution_bitcast_fusion
  155.8 0.0 collective-permute-done.7.core_own
  155.8 0.0 collective-permute-done.9.core_back
  155.8 1.0 copy-done.5
  156.9 2.6 %assemble.1 = bf16[128,4096]{1,0:T(8,128)(2,1)} custom-call(s32[3]{0:T(128)S(1)} %pad_add_fusion.where, bf16[256,1024]{1,0:T(8,128)(2,1)S(1)} %copy-done.5, bf16[128,1024]{1,0:T(8,128)(2,1)S(1)} %collective-permute-done.7.core_own, bf16[128,1024]{1,0:T(8,128)(2,1)S(1)} %collective-permute-done.9.core_back, bf16[256,1024]{1,0:T(8,128)(2,1)} %collective-permute-done.8.back), custom_call_target="tpu_custom_call" | custom-call | bytes 2097152 | tf_op jit(solution)/shard_map/assemble/pallas_call | solution.py:145
  (18 shorter events, 0.1 us)
Async XLA Ops:
  7.2 110.9 %all-gather.3.cloned.1.call-start = ((), (), s32[]{:S(2)}) async-start(), calls=%async_computation.4 | async-start | bytes 3342336 | tf_op jit(solution)/shard_map/all_gather | solution.py:171
  7.2 53.1 %copy-start.6 = (bf16[128,2048]{1,0:T(8,128)(2,1)S(1)}, bf16[128,2048]{1,0:T(8,128)(2,1)}, u32[]{:S(2)}) copy-start(bf16[128,2048]{1,0:T(8,128)(2,1)} %g0.1) | copy-start | bytes 1572868
  7.2 68.3 %copy-start.10 = (bf16[128,4096]{1,0:T(8,128)(2,1)S(1)}, bf16[128,4096]{1,0:T(8,128)(2,1)}, u32[]{:S(2)}) copy-start(bf16[128,4096]{1,0:T(8,128)(2,1)} %x0.1) | copy-start | bytes 3145732
  8.2 16.5 %collective-permute-start.4 = (bf16[16,2048]{1,0:T(8,128)(2,1)S(1)}, bf16[16,2048]{1,0:T(8,128)(2,1)S(1)}, u32[]{:S(2)}, u32[]{:S(2)}) collective-permute-start(bf16[16,2048]{1,0:T(8,128)(2,1)S(1)} %constant_dynamic-slice_fusion), channel_id=1, source_target_pairs={{2,0},{4,2},{6,4},{0,6},{3,1},{5,3},{7,5},{1,7},{10,8},{12,10},{14... | collective-permute-start | bytes 196616 | tf_op jit(solution)/shard_map/ppermute | solution.py:169
  20.6 8.9 %collective-permute-start.5 = (bf16[16,2048]{1,0:T(8,128)(2,1)S(1)}, bf16[16,2048]{1,0:T(8,128)(2,1)S(1)}, u32[]{:S(2)}, u32[]{:S(2)}) collective-permute-start(bf16[16,2048]{1,0:T(8,128)(2,1)S(1)} %constant_dynamic-slice_fusion), channel_id=1, source_target_pairs={{4,0},{6,2},{0,4},{2,6},{5,1},{7,3},{1,5},{3,7},{12,8},{14,10},{8,... | collective-permute-start | bytes 196616 | tf_op jit(solution)/shard_map/ppermute | solution.py:169
  22.5 10.7 %collective-permute-start.6 = (bf16[16,2048]{1,0:T(8,128)(2,1)S(1)}, bf16[16,2048]{1,0:T(8,128)(2,1)S(1)}, u32[]{:S(2)}, u32[]{:S(2)}) collective-permute-start(bf16[16,2048]{1,0:T(8,128)(2,1)S(1)} %constant_dynamic-slice_fusion), channel_id=1, source_target_pairs={{6,0},{0,2},{2,4},{4,6},{7,1},{1,3},{3,5},{5,7},{14,8},{8,10},{10,... | collective-permute-start | bytes 196616 | tf_op jit(solution)/shard_map/ppermute | solution.py:169
  35.3 17.1 %all-to-all-start = ((bf16[8,32,128]{2,1,0:T(8,128)(2,1)}), bf16[8,32,128]{2,1,0:T(8,128)(2,1)S(1)}, u32[]{:S(2)}, u32[]{:S(2)}) async-start(bf16[8,32,128]{2,1,0:T(8,128)(2,1)} %broadcast_in_dim.6), calls=%async_computation | async-start | bytes 131072 | tf_op jit(solution)/shard_map/all_to_all | solution.py:30
  42.6 22.5 %collective-permute-start.2 = (bf16[128,2048]{1,0:T(8,128)(2,1)}, bf16[128,2048]{1,0:T(8,128)(2,1)}, u32[]{:S(2)}, u32[]{:S(2)}) collective-permute-start(bf16[128,2048]{1,0:T(8,128)(2,1)} %g0.1), channel_id=1, source_target_pairs={{0,1},{1,0},{2,3},{3,2},{4,5},{5,4},{6,7},{7,6},{8,9},{9,8},{10,11... | collective-permute-start | bytes 1572872 | tf_op jit(solution)/shard_map/ppermute | solution.py:175
  46.0 23.9 %collective-permute-start = (bf16[128,4096]{1,0:T(8,128)(2,1)}, bf16[128,4096]{1,0:T(8,128)(2,1)}, u32[]{:S(2)}, u32[]{:S(2)}) collective-permute-start(bf16[128,4096]{1,0:T(8,128)(2,1)} %x0.1), channel_id=1, source_target_pairs={{0,8},{8,0},{1,9},{9,1},{2,10},{10,2},{3,11},{11,3},{4,12},{12,4},... | collective-permute-start | bytes 3145736 | tf_op jit(solution)/shard_map/ppermute | solution.py:177
  53.5 22.0 %all-to-all-start.1 = ((bf16[16,8,32,128]{3,2,1,0:T(8,128)(2,1)}), bf16[16,8,32,128]{3,2,1,0:T(8,128)(2,1)S(1)}, u32[]{:S(2)}, u32[]{:S(2)}) async-start(bf16[16,8,32,128]{3,2,1,0:T(8,128)(2,1)} %broadcast_in_dim.7), calls=%async_computation.1 | async-start | bytes 2097152 | tf_op jit(solution)/shard_map/all_to_all | solution.py:30
  60.3 6.7 %collective-permute-start.1 = (bf16[128,2048]{1,0:T(8,128)(2,1)S(1)}, bf16[128,2048]{1,0:T(8,128)(2,1)S(1)}, u32[]{:S(2)}, u32[]{:S(2)}) collective-permute-start(bf16[128,2048]{1,0:T(8,128)(2,1)S(1)} %copy-done.6), channel_id=1, source_target_pairs={{0,8},{8,0},{1,9},{9,1},{2,10},{10,2},{3,11},{11,3},{4,12},{12,4},... | collective-permute-start | bytes 1572872 | tf_op jit(solution)/shard_map/ppermute | solution.py:176
  65.1 4.0 %collective-permute-start.3 = (bf16[128,2048]{1,0:T(8,128)(2,1)}, bf16[128,2048]{1,0:T(8,128)(2,1)S(1)}, u32[]{:S(2)}, u32[]{:S(2)}) collective-permute-start(bf16[128,2048]{1,0:T(8,128)(2,1)} %collective-permute-done.2.a), channel_id=1, source_target_pairs={{0,8},{8,0},{1,9},{9,1},{2,10},{10,2},{3,11},{11,3},{4,12},{12,4},... | collective-permute-start | bytes 1572872 | tf_op jit(solution)/shard_map/ppermute | solution.py:178
  67.0 10.9 %copy-start.8 = (bf16[128,2048]{1,0:T(8,128)(2,1)}, bf16[128,2048]{1,0:T(8,128)(2,1)S(1)}, u32[]{:S(2)}) copy-start(bf16[128,2048]{1,0:T(8,128)(2,1)S(1)} %collective-permute-done.1.b.g1) | copy-start | bytes 1572868
  69.1 0.8 copy-start.11
  101.9 37.6 %all-to-all-start.3 = ((bf16[32,32,128]{2,1,0:T(8,128)(2,1)}), bf16[32,32,128]{2,1,0:T(8,128)(2,1)S(1)}, u32[]{:S(2)}, u32[]{:S(2)}) async-start(bf16[32,32,128]{2,1,0:T(8,128)(2,1)} %bitcast.8), calls=%async_computation.3 | async-start | bytes 524288 | tf_op jit(solution)/shard_map/all_to_all | solution.py:188
  118.1 1.9 %copy-start = (bf16[48,16,2048]{2,1,0:T(8,128)(2,1)S(1)}, bf16[48,16,2048]{2,1,0:T(8,128)(2,1)}, u32[]{:S(2)}) copy-start(bf16[48,16,2048]{2,1,0:T(8,128)(2,1)} %all-gather.3.cloned.1.call-done) | copy-start | bytes 9437188
  120.0 1.6 copy-start.2
  121.6 1.0 copy-start.12
  122.6 17.1 %copy-start.1 = (bf16[48,16,2048]{2,1,0:T(8,128)(2,1)S(1)}, bf16[48,16,2048]{2,1,0:T(8,128)(2,1)}, u32[]{:S(2)}) copy-start(bf16[48,16,2048]{2,1,0:T(8,128)(2,1)} %all-gather.3.cloned.1.call-done) | copy-start | bytes 9437188
  128.0 23.1 %collective-permute-start.8 = (bf16[256,1024]{1,0:T(8,128)(2,1)}, bf16[256,1024]{1,0:T(8,128)(2,1)}, u32[]{:S(2)}, u32[]{:S(2)}) collective-permute-start(bf16[256,1024]{1,0:T(8,128)(2,1)} %features.3), channel_id=1, source_target_pairs={{0,1},{1,0},{2,3},{3,2},{4,5},{5,4},{6,7},{7,6},{8,9},{9,8},{10,11... | collective-permute-start | bytes 1572872 | tf_op jit(solution)/shard_map/ppermute | solution.py:200
  139.7 1.6 copy-start.3
  141.3 1.0 copy-start.7
  142.4 1.0 copy-start.9
  143.4 10.6 %copy-start.14 = (f32[1,8192]{1,0:T(1,128)S(1)}, f32[1,8192]{1,0:T(1,128)}, u32[]{:S(2)}) copy-start(f32[1,8192]{1,0:T(1,128)} %param.11) | copy-start | bytes 98308
  143.4 10.7 %copy-start.15 = (f32[1,8192]{1,0:T(1,128)S(1)}, f32[1,8192]{1,0:T(1,128)}, u32[]{:S(2)}) copy-start(f32[1,8192]{1,0:T(1,128)} %param.10) | copy-start | bytes 98308
  143.4 11.6 %copy-start.13 = (bf16[512,256]{1,0:T(8,128)(2,1)S(1)}, bf16[512,256]{1,0:T(8,128)(2,1)}, u32[]{:S(2)}) copy-start(bf16[512,256]{1,0:T(8,128)(2,1)} %param.9) | copy-start | bytes 786436
  147.1 0.8 copy-start.4
  147.8 8.0 %collective-permute-start.7 = (bf16[128,1024]{1,0:T(8,128)(2,1)S(1)}, bf16[128,1024]{1,0:T(8,128)(2,1)S(1)}, u32[]{:S(2)}, u32[]{:S(2)}) collective-permute-start(bf16[128,1024]{1,0:T(8,128)(2,1)S(1)} %slice.8), channel_id=1, source_target_pairs={{0,8},{8,0},{1,9},{9,1},{2,10},{10,2},{3,11},{11,3},{4,12},{12,4},... | collective-permute-start | bytes 786440 | tf_op jit(solution)/shard_map/ppermute | solution.py:202
  152.1 3.7 %collective-permute-start.9 = (bf16[128,1024]{1,0:T(8,128)(2,1)S(1)}, bf16[128,1024]{1,0:T(8,128)(2,1)S(1)}, u32[]{:S(2)}, u32[]{:S(2)}) collective-permute-start(bf16[128,1024]{1,0:T(8,128)(2,1)S(1)} %slice.9), channel_id=1, source_target_pairs={{0,8},{8,0},{1,9},{9,1},{2,10},{10,2},{3,11},{11,3},{4,12},{12,4},... | collective-permute-start | bytes 786440 | tf_op jit(solution)/shard_map/ppermute | solution.py:203
  155.8 1.0 copy-start.5
Sparse Core Ops, SparseCore 0:
  34.0 77.6 all-gather.2

commit v3 on v2

v3 whole, which is shorter than its diff:
```python
import functools
import math

import jax
import jax.numpy as jnp
from jax import lax
from jax.experimental import pallas as pl
from jax.experimental.pallas import tpu as pltpu
from jax.sharding import Mesh
from jax.sharding import PartitionSpec as P

STEP = 1000

beta_one = 0.9
beta_two = 0.999
epsilon = 1e-08

AXES = ("y", "zh", "x", "c", "q", "p")
SIZES = (4, 2, 4, 2, 4, 2)
PLANE = ("y", "x")
LINE = ("q", "p")
RING = ("zh", "q", "p")
COLUMN = ("zh", "c", "q", "p")
F32, BF16 = jnp.float32, jnp.bfloat16


def spread(block, axes, count):
    sent = jnp.broadcast_to(block[None], (count,) + block.shape)
    return lax.all_to_all(sent, axes, 0, 0, tiled=True)


def dot(a, b, dims):
    return lax.dot_general(a, b, (dims, ((), ())), preferred_element_type=F32)


def low_kernel(scale, x0, x1, g0, g1, basis, out):
    shards, half = 8, basis.shape[2]
    rows = basis.shape[1] // shards
    depth = 16 * rows
    proj = []
    for x in (x0, x1):
        total = None
        for s in range(shards):
            part = dot(
                x[:, s * depth : (s + 1) * depth],
                basis[:, s * rows : (s + 1) * rows, :].reshape(depth, half),
                ((1,), (0,)),
            )
            total = part if total is None else total + part
        proj.append(total.astype(BF16))
    width = out.shape[1] // 2
    for y in range(4):
        for zh in range(2):
            at = (y * 2 + zh) * 4 * width
            part = dot(g0[:, at : at + 4 * width], proj[0], ((0,), (0,))) + dot(
                g1[:, at : at + 4 * width], proj[1], ((0,), (0,))
            )
            part = part * scale
            for x in range(4):
                out[y * 4 + x, zh * width : (zh + 1) * width, :] = part[
                    x * width : (x + 1) * width
                ]


def low_rank(x0, x1, g0, g1, mixed, scale):
    n, cols = g0.shape
    half = mixed.shape[2]
    whole = lambda v: pl.BlockSpec(v.shape, lambda i: (0, 0))
    return pl.pallas_call(
        functools.partial(low_kernel, scale),
        grid=(1,),
        in_specs=[whole(x0), whole(x1), whole(g0), whole(g1)]
        + [pl.BlockSpec((16, 256, half), lambda i: (0, 0, 0))],
        out_specs=pl.BlockSpec((16, cols // 16, half), lambda i: (0, 0, 0)),
        out_shape=jax.ShapeDtypeStruct((16, cols // 16, half), F32),
        cost_estimate=pl.CostEstimate(
            flops=4 * n * half * (x0.shape[1] + cols), bytes_accessed=6 << 20, transcendentals=0
        ),
        name="low_rank",
    )(x0, x1, g0, g1, mixed)


def feature_kernel(pairs, core, *refs):
    del core
    tokens, (own, rest), outs = refs[: 2 * pairs], refs[2 * pairs : 2 * pairs + 2], refs[2 * pairs + 2 : -1]
    rows = refs[-1]
    n = tokens[0].shape[0]
    first = pl.program_id(0) == 0

    @pl.when(first)
    def _():
        rows[...] = own[...]

    @pl.when(jnp.logical_not(first))
    def _():
        for g in range(16):
            group = rest[:, g * 16 : (g + 1) * 16, :]
            rows[:, g * 128 : (g + 1) * 128] = group.reshape(rows.shape[0], 128)

    for i, out in enumerate(outs):
        for j in range(2):
            out[j * n : (j + 1) * n, :] = dot(tokens[2 * i + j][...], rows[...], ((1,), (1,))).astype(
                BF16
            )


def features(core, tokens, own, mixed):
    n, depth = tokens[0].shape
    feat = own.shape[0] // 2
    pairs = len(tokens) // 2
    spec = pltpu.PrefetchScalarGridSpec(
        num_scalar_prefetch=1,
        grid=(2,),
        in_specs=[pl.BlockSpec((n, depth), lambda r, c: (0, 0)) for _ in tokens]
        + [
            pl.BlockSpec((feat, depth), lambda r, c: (c[0], 0)),
            pl.BlockSpec((16, 256, 128), lambda r, c: (0, 1, 0)),
        ],
        out_specs=[pl.BlockSpec((2 * n, feat), lambda r, c: (0, r))] * pairs,
        scratch_shapes=[pltpu.VMEM((feat, depth), BF16)],
    )
    return pl.pallas_call(
        functools.partial(feature_kernel, pairs),
        grid_spec=spec,
        out_shape=[jax.ShapeDtypeStruct((2 * n, 2 * feat), BF16)] * pairs,
        cost_estimate=pl.CostEstimate(
            flops=1 << 20, bytes_accessed=1 << 16, transcendentals=0
        ),
        name="features",
    )(core[None], *tokens, own, mixed)


def assemble_kernel(where, near, up, down, down2, crossed, out):
    line, core = where[0], where[1]
    feat = near.shape[1] // 2
    for i, (ref, offset) in enumerate(((near, 0), (up, 1), (down, 7), (down2, 6))):
        for r in range(2):
            shard = lax.rem(line + offset + 4 * r, 8)
            at = pl.multiple_of((shard * 2 + core) * feat, feat)
            out[:, pl.ds(at, feat)] = ref[:, r * feat : (r + 1) * feat]
            at = pl.multiple_of((shard * 2 + 1 - core) * feat, feat)
            out[:, pl.ds(at, feat)] = crossed[i, :, r * feat : (r + 1) * feat]


def assemble(where, pieces, crossed):
    _, n, wide = crossed.shape
    spec = pltpu.PrefetchScalarGridSpec(
        num_scalar_prefetch=1,
        grid=(1,),
        in_specs=[pl.BlockSpec((n, wide), lambda i, w: (0, 0))] * 4
        + [pl.BlockSpec((4, n, wide), lambda i, w: (0, 0, 0))],
        out_specs=pl.BlockSpec((n, 8 * wide), lambda i, w: (0, 0)),
    )
    return pl.pallas_call(
        assemble_kernel,
        grid_spec=spec,
        out_shape=jax.ShapeDtypeStruct((n, 8 * wide), BF16),
        cost_estimate=pl.CostEstimate(flops=0, bytes_accessed=1 << 16, transcendentals=0),
        name="assemble",
    )(where, *pieces, crossed)


def ring(value, step):
    return lax.ppermute(value, RING, [(i, (i + step) % 16) for i in range(16)])


def swap_cores(value):
    return lax.ppermute(value, "c", [(0, 1), (1, 0)])


def on_device(inputs, out_grad, weight, proj_basis, first_moment, second_moment):
    core = lax.axis_index("c")
    line = lax.axis_index(LINE)
    plane = lax.axis_index(PLANE)
    n, feat = inputs.shape[0], weight.shape[0] // 2
    scale = 1.0 / math.sqrt(n * 512)
    half = proj_basis.shape[1] // 2

    rows = feat // 16
    piece = lax.dynamic_slice(weight, (core * feat + plane * rows, 0), (rows, weight.shape[1]))
    piece = lax.ppermute(piece, LINE, [(i, (i + 4) % 8) for i in range(8)])
    piece = piece.reshape(rows, 16, 128).transpose(1, 0, 2).reshape(256, 128)
    p_rows = proj_basis.shape[0] // 16
    p_piece = lax.dynamic_slice(proj_basis, (plane * p_rows, core * half), (p_rows, half))
    before = ring(out_grad, 1)
    after = ring(out_grad, -1)
    p_line = spread(p_piece, LINE, 8).reshape(256, half)
    p_line, before, after = lax.optimization_barrier((p_line, before, after))
    mixed = spread(jnp.concatenate([p_line, piece]), PLANE, 16)

    grad_c = swap_cores(out_grad)
    inputs_c = swap_cores(inputs)
    after2 = ring(after, -1)
    far = [before, swap_cores(before), after, swap_cores(after), after2, swap_cores(after2)]
    mixed, inputs_c, grad_c, far = lax.optimization_barrier((mixed, inputs_c, grad_c, far))

    low = low_rank(inputs, inputs_c, out_grad, grad_c, mixed, scale)
    cols = low.shape[1] // 4
    low = lax.all_to_all(low, PLANE, 0, 0, tiled=True).sum(axis=0)
    low = low.reshape(2, 2, 1, cols, half).astype(BF16)
    far_out = features(core, far, weight, mixed)
    (near,) = features(core, [out_grad, grad_c], weight, mixed)
    pieces = [near, ring(far_out[0], -1), ring(far_out[1], 1), ring(far_out[2], 2)]
    low, pieces = lax.optimization_barrier((low, pieces))
    low = jnp.broadcast_to(low, (2, 2, 8, cols, half)).reshape(32, cols, half)
    low = lax.all_to_all(low, COLUMN, 0, 0, tiled=True).reshape(2, 2, 8, cols, half)
    low = low.astype(F32).sum(axis=(0, 2))
    flat_grad = low.transpose(0, 2, 1).reshape(1, 2 * half * cols)
    new_first = beta_one * first_moment + (1.0 - beta_one) * flat_grad
    new_second = beta_two * second_moment + (1.0 - beta_two) * flat_grad * flat_grad
    corr_one = 1.0 - beta_one**STEP
    corr_two = 1.0 - beta_two**STEP
    direction = (new_first / corr_one / (jnp.sqrt(new_second / corr_two) + epsilon)).astype(BF16)
    direction = direction.reshape(2 * half, cols)
    update = jnp.dot(proj_basis, direction, preferred_element_type=F32)

    crossed = swap_cores(jnp.stack([v[n:] for v in pieces]))
    input_grad = assemble(jnp.stack([line, core]), pieces, crossed)
    return (input_grad, new_first, new_second, update)


def solution(mesh):
    fine = Mesh(mesh.devices.reshape(SIZES), AXES)
    dp, fsdp = AXES[:4], AXES[4:]
    in_specs = (
        P(AXES, None),
        P(AXES, None),
        P(fsdp, None),
        P(fsdp, None),
        P(dp, None),
        P(dp, None),
    )
    out_specs = (P(AXES, None), P(dp, None), P(dp, None), P(fsdp, dp))
    return jax.shard_map(
        on_device, mesh=fine, in_specs=in_specs, out_specs=out_specs, check_vma=False
    )
```

time: 167 us -> 153 us (0.916)
  blocking collectives: 23.1 us -> 0 us
  starting transfers between devices: 69 us -> 87.6 us
  between operations: 14.4 us -> 1.04 us
  local copies, waits for them, and re-layouts: 16.4 us -> 10.2 us
  Pallas kernels: 14 us -> 19.9 us
  waiting for transfers between devices: 27 us -> 31 us
    all_to_all x1 -> x0, blocking collectives: 23.1 us -> none  [on_device(): low = lax.all_to_all(low, PLANE, 0, 0, tiled=True).sum(axis=0)]
    ppermute x10 -> x13, starting transfers between devices: 38.7 us -> 57.9 us  [the longest x6 31.9 us: ring(): return lax.ppermute(value, RING, [(i, (i + step) % 16) for i in range(16)])]
    all_to_all x2, waiting for transfers between devices: 8.33 us -> 0.01 us  [spread(): return lax.all_to_all(sent, axes, 0, 0, tiled=True)]
    ppermute x10 -> x13, waiting for transfers between devices: 10.6 us -> 18.4 us  [the longest x6 13.8 us: ring(): return lax.ppermute(value, RING, [(i, (i + step) % 16) for i in range(16)])]
    all_to_all x0 -> x1, starting transfers between devices: none -> 6.93 us  [on_device(): low = lax.all_to_all(low, PLANE, 0, 0, tiled=True).sum(axis=0)]
    unnamed x32 -> x31, local copies, waits for them, and re-layouts: 10.8 us -> 4.17 us
    all_to_all x1, starting transfers between devices: 16.2 us -> 10.1 us  [on_device(): lax.all_to_all(low, COLUMN, 0, 0, tiled=True).reshape(2, 2, 8, cols, half)]
    pallas_call x3, Pallas kernels: 11.4 us -> 16.8 us  [the longest x2 12.5 us: features(): pl.pallas_call(functools.partial(feature_kernel, pairs), grid_spec=spec,...]
  transfers between devices with their start and end apart: 14 -> 17, of which waited for: 6 -> 5; matrix products, arithmetic and copies ran while one was open for 4% -> 3% of each run, Pallas kernels for 7% -> 10%
where the time goes in v3:
time: 153 us; the launch traced here: 152 us
  starting transfers between devices  87.6 us (57%)
  waiting for transfers between devices  31 us (20%)
  Pallas kernels  19.9 us (13%)
  local copies, waits for them, and re-layouts  10.2 us (7%)
  other arithmetic  1.57 us (1%)
    ppermute x6, starting transfers between devices, ring(): return lax.ppermute(value, RING, [(i, (i + step) % 16) for i in range(16)])  31.9 us
    ppermute x6, starting transfers between devices, swap_cores(): return lax.ppermute(value, 'c', [(0, 1), (1, 0)])  18.7 us
    ppermute x6, waiting for transfers between devices, ring(): return lax.ppermute(value, RING, [(i, (i + step) % 16) for i in range(16)])  13.8 us
    all_to_all x2, starting transfers between devices, spread(): return lax.all_to_all(sent, axes, 0, 0, tiled=True)  12.8 us
    all_to_all x1, waiting for transfers between devices, on_device(): lax.all_to_all(low, COLUMN, 0, 0, tiled=True).reshape(2, 2, 8, cols, half)  12.6 us
    pallas_call x2, Pallas kernels, features(): pl.pallas_call(functools.partial(feature_kernel, pairs), grid_spec=spec,...  12.5 us
    all_to_all x1, starting transfers between devices, on_device(): lax.all_to_all(low, COLUMN, 0, 0, tiled=True).reshape(2, 2, 8, cols, half)  10.1 us
    ppermute x1, starting transfers between devices, on_device(): piece = lax.ppermute(piece, LINE, [(i, (i + 4) % 8) for i in range(8)])  7.27 us
  transfers between devices with their start and end apart: 17, of which 5 were waited for; matrix products, arithmetic and copies ran while one was open for 3% of the time, Pallas kernels for 10%

profile of v3, /device:TPU:1, one launch (start us, length us, event | category | flops | bytes accessed | tf_op | source)
XLA Modules:
  0.0 152.2 jit_solution(14898492675163546481)
XLA Ops:
  0.6 4.4 %collective-permute-start = (bf16[128,2048]{1,0:T(8,128)(2,1)}, bf16[128,2048]{1,0:T(8,128)(2,1)S(1)}, u32[]{:S(2)}, u32[]{:S(2)}) collective-permute-start(bf16[128,2048]{1,0:T(8,128)(2,1)} %refs_0_.1), channel_id=1, source_target_pairs={{0,1},{1,2},{2,3},{3,4},{4,5},{5,6},{6,7},{7,64},{64,65},{65,66},{... | collective-permute-start | bytes 1572872 | tf_op jit(solution)/shard_map/ppermute | solution.py:164
  5.0 9.5 %collective-permute-start.1 = (bf16[128,2048]{1,0:T(8,128)(2,1)}, bf16[128,2048]{1,0:T(8,128)(2,1)}, u32[]{:S(2)}, u32[]{:S(2)}) collective-permute-start(bf16[128,2048]{1,0:T(8,128)(2,1)} %refs_0_.1), channel_id=1, source_target_pairs={{0,71},{1,0},{2,1},{3,2},{4,3},{5,4},{6,5},{7,6},{64,7},{65,64},{6... | collective-permute-start | bytes 1572872 | tf_op jit(solution)/shard_map/ppermute | solution.py:164
  14.5 0.7 dynamic_slice.6
  15.2 0.6 broadcast_in_dim.8
  15.9 5.9 %all-to-all-start = ((bf16[8,32,128]{2,1,0:T(8,128)(2,1)}), bf16[8,32,128]{2,1,0:T(8,128)(2,1)S(1)}, u32[]{:S(2)}, u32[]{:S(2)}) async-start(bf16[8,32,128]{2,1,0:T(8,128)(2,1)} %broadcast_in_dim.8), calls=%async_computation | async-start | bytes 131072 | tf_op jit(solution)/shard_map/all_to_all | solution.py:29
  21.8 0.8 constant_dynamic-slice_fusion
  22.6 7.3 %collective-permute-start.2 = (bf16[16,2048]{1,0:T(8,128)(2,1)S(1)}, bf16[16,2048]{1,0:T(8,128)(2,1)S(1)}, u32[]{:S(2)}, u32[]{:S(2)}) collective-permute-start(bf16[16,2048]{1,0:T(8,128)(2,1)S(1)} %constant_dynamic-slice_fusion), channel_id=1, source_target_pairs={{0,4},{1,5},{2,6},{3,7},{4,0},{5,1},{6,2},{7,3},{8,12},{9,13},{10,... | collective-permute-start | bytes 196616 | tf_op jit(solution)/shard_map/ppermute | solution.py:181
  29.9 3.5 %collective-permute-done.2 = bf16[16,2048]{1,0:T(8,128)(2,1)S(1)} collective-permute-done((bf16[16,2048]{1,0:T(8,128)(2,1)S(1)}, bf16[16,2048]{1,0:T(8,128)(2,1)S(1)}, u32[]{:S(2)}, u32[]{:S(2)}) %collective-permute-start.2) | collective-permute-done | bytes 65568 | tf_op jit(solution)/shard_map/ppermute | solution.py:181
  33.4 0.0 all-to-all-done
  33.4 0.0 collective-permute-done.refs_0_
  33.4 0.0 copy-start.8
  33.4 0.0 collective-permute-done.1.refs_2_
  33.5 1.8 %broadcast_in_dim.9 = bf16[16,512,128]{2,1,0:T(8,128)(2,1)} broadcast(bf16[512,128]{1,0:T(8,128)(2,1)S(1)} %pad_maximum_fusion.1), dimensions={1,2} | broadcast | bytes 2228224 | tf_op jit(solution)/shard_map/broadcast_in_dim | solution.py:28
  35.2 0.0 copy-done.8
  35.2 6.9 %all-to-all-start.1 = ((bf16[16,512,128]{2,1,0:T(8,128)(2,1)}), bf16[16,512,128]{2,1,0:T(8,128)(2,1)S(1)}, u32[]{:S(2)}, u32[]{:S(2)}) async-start(bf16[16,512,128]{2,1,0:T(8,128)(2,1)} %broadcast_in_dim.9), calls=%async_computation.1 | async-start | bytes 4194304 | tf_op jit(solution)/shard_map/all_to_all | solution.py:29
  42.1 7.4 %collective-permute-start.3 = (bf16[128,4096]{1,0:T(8,128)(2,1)}, bf16[128,4096]{1,0:T(8,128)(2,1)S(1)}, u32[]{:S(2)}, u32[]{:S(2)}) collective-permute-start(bf16[128,4096]{1,0:T(8,128)(2,1)} %x0.1), channel_id=1, source_target_pairs={{0,8},{8,0},{1,9},{9,1},{2,10},{10,2},{3,11},{11,3},{4,12},{12,4},... | collective-permute-start | bytes 3145736 | tf_op jit(solution)/shard_map/ppermute | solution.py:168
  49.5 5.4 %collective-permute-start.7 = (bf16[128,2048]{1,0:T(8,128)(2,1)}, bf16[128,2048]{1,0:T(8,128)(2,1)S(1)}, u32[]{:S(2)}, u32[]{:S(2)}) collective-permute-start(bf16[128,2048]{1,0:T(8,128)(2,1)} %collective-permute-done.1.refs_2_), channel_id=1, source_target_pairs={{0,71},{1,0},{2,1},{3,2},{4,3},{5,4},{6,5},{7,6},{64,7},{65,64},{6... | collective-permute-start | bytes 1572872 | tf_op jit(solution)/shard_map/ppermute | solution.py:164
  54.9 2.2 %collective-permute-start.4 = (bf16[128,2048]{1,0:T(8,128)(2,1)S(1)}, bf16[128,2048]{1,0:T(8,128)(2,1)S(1)}, u32[]{:S(2)}, u32[]{:S(2)}) collective-permute-start(bf16[128,2048]{1,0:T(8,128)(2,1)S(1)} %copy-done.1), channel_id=1, source_target_pairs={{0,8},{8,0},{1,9},{9,1},{2,10},{10,2},{3,11},{11,3},{4,12},{12,4},... | collective-permute-start | bytes 1572872 | tf_op jit(solution)/shard_map/ppermute | solution.py:168
  57.1 2.1 %collective-permute-start.6 = (bf16[128,2048]{1,0:T(8,128)(2,1)}, bf16[128,2048]{1,0:T(8,128)(2,1)S(1)}, u32[]{:S(2)}, u32[]{:S(2)}) collective-permute-start(bf16[128,2048]{1,0:T(8,128)(2,1)} %collective-permute-done.1.refs_2_), channel_id=1, source_target_pairs={{0,8},{8,0},{1,9},{9,1},{2,10},{10,2},{3,11},{11,3},{4,12},{12,4},... | collective-permute-start | bytes 1572872 | tf_op jit(solution)/shard_map/ppermute | solution.py:168
  59.3 2.2 %collective-permute-start.5 = (bf16[128,2048]{1,0:T(8,128)(2,1)}, bf16[128,2048]{1,0:T(8,128)(2,1)S(1)}, u32[]{:S(2)}, u32[]{:S(2)}) collective-permute-start(bf16[128,2048]{1,0:T(8,128)(2,1)} %copy-done.8), channel_id=1, source_target_pairs={{0,8},{8,0},{1,9},{9,1},{2,10},{10,2},{3,11},{11,3},{4,12},{12,4},... | collective-permute-start | bytes 1572872 | tf_op jit(solution)/shard_map/ppermute | solution.py:168
  61.5 5.1 %collective-permute-done.7.refs_4_ = bf16[128,2048]{1,0:T(8,128)(2,1)S(1)} collective-permute-done((bf16[128,2048]{1,0:T(8,128)(2,1)}, bf16[128,2048]{1,0:T(8,128)(2,1)S(1)}, u32[]{:S(2)}, u32[]{:S(2)}) %collective-permute-start.7) | collective-permute-done | bytes 524320 | tf_op jit(solution)/shard_map/ppermute | solution.py:164
  66.5 2.7 %collective-permute-start.8 = (bf16[128,2048]{1,0:T(8,128)(2,1)S(1)}, bf16[128,2048]{1,0:T(8,128)(2,1)}, u32[]{:S(2)}, u32[]{:S(2)}) collective-permute-start(bf16[128,2048]{1,0:T(8,128)(2,1)S(1)} %collective-permute-done.7.refs_4_), channel_id=1, source_target_pairs={{0,8},{8,0},{1,9},{9,1},{2,10},{10,2},{3,11},{11,3},{4,12},{12,4},... | collective-permute-start | bytes 1572872 | tf_op jit(solution)/shard_map/ppermute | solution.py:168
  69.2 0.0 collective-permute-done.4.g1.refs_1_
  69.3 0.0 collective-permute-done.6.refs_3_
  69.3 0.0 collective-permute-done.5.refs_1_
  69.3 0.0 copy-start.11
  69.3 0.0 collective-permute-done.3.x1
  69.3 0.8 copy-done.10
  70.1 0.2 copy-done.11
  70.3 1.0 copy-done.3
  71.3 0.0 collective-permute-done.8.refs_5_
  71.3 0.0 all-to-all-done.1.basis.refs_3_.refs_7_
  71.3 1.3 copy-done
  72.6 4.3 %low_rank.1 = f32[16,128,128]{2,1,0:T(8,128)} custom-call(bf16[128,4096]{1,0:T(8,128)(2,1)} %x0.1, bf16[128,4096]{1,0:T(8,128)(2,1)} %copy-done.3, bf16[128,2048]{1,0:T(8,128)(2,1)} %refs_0_.1, bf16[128,2048]{1,0:T(8,128)(2,1)} %copy-done.2, bf16[16,512,128]{2,1,0:T(8,128)(2,1)} %copy-done), custom_call_target="tpu_custom_call" | custom-call | flops 402653184 | bytes 6291456 | tf_op jit(solution)/shard_map/low_rank/pallas_call | solution.py:69
  76.9 6.9 %all-to-all-start.2 = ((f32[16,128,128]{2,1,0:T(8,128)}), f32[16,128,128]{2,1,0:T(8,128)S(1)}, u32[]{:S(2)}, u32[]{:S(2)}) async-start(f32[16,128,128]{2,1,0:T(8,128)} %low_rank.1), calls=%async_computation.2 | async-start | bytes 2097152 | tf_op jit(solution)/shard_map/all_to_all | solution.py:199
  83.9 7.9 %features.3 = (bf16[256,512]{1,0:T(8,128)(2,1)}, bf16[256,512]{1,0:T(8,128)(2,1)}, bf16[256,512]{1,0:T(8,128)(2,1)}) custom-call(s32[1]{0:T(128)} %bitcast.1.core, bf16[128,2048]{1,0:T(8,128)(2,1)} %copy-done.8, bf16[128,2048]{1,0:T(8,128)(2,1)} %copy-done.11, bf16[128,2048]{1,0:T(8,128)(2,1)} %collective-permute-done.1.refs_2_, ...), custom_call_target="tpu_custom_call" | custom-call | flops 1048576 | bytes 65536 | tf_op jit(solution)/shard_map/features/pallas_call | solution.py:122
  91.8 4.6 %collective-permute-start.10 = (bf16[256,512]{1,0:T(8,128)(2,1)}, bf16[256,512]{1,0:T(8,128)(2,1)S(1)}, u32[]{:S(2)}, u32[]{:S(2)}) collective-permute-start(bf16[256,512]{1,0:T(8,128)(2,1)} %get-tuple-element.37), channel_id=1, source_target_pairs={{0,1},{1,2},{2,3},{3,4},{4,5},{5,6},{6,7},{7,64},{64,65},{65,66},{... | collective-permute-start | bytes 786440 | tf_op jit(solution)/shard_map/ppermute | solution.py:164
  96.4 3.5 %collective-permute-start.11 = (bf16[256,512]{1,0:T(8,128)(2,1)}, bf16[256,512]{1,0:T(8,128)(2,1)S(1)}, u32[]{:S(2)}, u32[]{:S(2)}) collective-permute-start(bf16[256,512]{1,0:T(8,128)(2,1)} %get-tuple-element.38), channel_id=1, source_target_pairs={{0,2},{1,3},{2,4},{3,5},{4,6},{5,7},{6,64},{7,65},{64,66},{65,67},... | collective-permute-start | bytes 786440 | tf_op jit(solution)/shard_map/ppermute | solution.py:164
  99.9 4.5 %collective-permute-start.9 = (bf16[256,512]{1,0:T(8,128)(2,1)}, bf16[256,512]{1,0:T(8,128)(2,1)S(1)}, u32[]{:S(2)}, u32[]{:S(2)}) collective-permute-start(bf16[256,512]{1,0:T(8,128)(2,1)} %get-tuple-element.36), channel_id=1, source_target_pairs={{0,71},{1,0},{2,1},{3,2},{4,3},{5,4},{6,5},{7,6},{64,7},{65,64},{6... | collective-permute-start | bytes 786440 | tf_op jit(solution)/shard_map/ppermute | solution.py:164
  104.5 4.6 %features.2.near = bf16[256,512]{1,0:T(8,128)(2,1)} custom-call(s32[1]{0:T(128)} %bitcast.1.core, bf16[128,2048]{1,0:T(8,128)(2,1)} %refs_0_.1, bf16[128,2048]{1,0:T(8,128)(2,1)} %copy-done.2, bf16[512,2048]{1,0:T(8,128)(2,1)} %refs_6_.1, bf16[16,512,128]{2,1,0:T(8,128)(2,1)} %copy-done), custom_call_target="tpu_custom_call" | custom-call | flops 1048576 | bytes 65536 | tf_op jit(solution)/shard_map/features/pallas_call | solution.py:122
  109.0 0.0 all-to-all-done.2
  109.0 0.1 reduce_sum.18
  109.1 0.0 collective-permute-done.10.down
  109.1 8.8 %collective-permute-done.11.down2 = bf16[256,512]{1,0:T(8,128)(2,1)S(1)} collective-permute-done((bf16[256,512]{1,0:T(8,128)(2,1)}, bf16[256,512]{1,0:T(8,128)(2,1)S(1)}, u32[]{:S(2)}, u32[]{:S(2)}) %collective-permute-start.11) | collective-permute-done | bytes 262176 | tf_op jit(solution)/shard_map/ppermute | solution.py:164
  117.9 0.0 collective-permute-done.9.up
  117.9 0.8 broadcast_in_dim.11
  118.7 10.1 %all-to-all-start.3 = ((bf16[32,32,128]{2,1,0:T(8,128)(2,1)}), bf16[32,32,128]{2,1,0:T(8,128)(2,1)S(1)}, u32[]{:S(2)}, u32[]{:S(2)}) async-start(bf16[32,32,128]{2,1,0:T(8,128)(2,1)} %bitcast.11), calls=%async_computation.3 | async-start | bytes 524288 | tf_op jit(solution)/shard_map/all_to_all | solution.py:206
  128.8 0.9 slice_bitcast_fusion.2
  129.7 0.0 copy-start.13
  129.7 0.0 copy-start.14
  129.7 0.0 copy-start.12
  129.8 0.1 pad_maximum_fusion
  129.8 2.1 %collective-permute-start.12 = (bf16[4,128,512]{2,1,0:T(8,128)(2,1)S(1)}, bf16[4,128,512]{2,1,0:T(8,128)(2,1)S(1)}, u32[]{:S(2)}, u32[]{:S(2)}) collective-permute-start(bf16[4,128,512]{2,1,0:T(8,128)(2,1)S(1)} %pad_maximum_fusion), channel_id=1, source_target_pairs={{0,8},{8,0},{1,9},{9,1},{2,10},{10,2},{3,11},{11,3},{4,12},{12,4},... | collective-permute-start | bytes 1572872 | tf_op jit(solution)/shard_map/ppermute | solution.py:168
  132.0 0.6 pad_add_fusion.where
  132.6 1.1 collective-permute-done.12.crossed
  133.6 0.0 copy-done.6
  133.7 0.8 copy-done.7
  134.5 3.1 %assemble.1 = bf16[128,4096]{1,0:T(8,128)(2,1)} custom-call(s32[2]{0:T(128)} %pad_add_fusion.where, bf16[256,512]{1,0:T(8,128)(2,1)} %features.2.near, bf16[256,512]{1,0:T(8,128)(2,1)} %copy-done.6, bf16[256,512]{1,0:T(8,128)(2,1)} %copy-done.4, bf16[256,512]{1,0:T(8,128)(2,1)} %copy-done.5, bf16[4,128,512]{2,1,0:T(8,128)(2,1)} %copy-done.7), custom_call_target="tpu_custom_call" | custom-call | bytes 65536 | tf_op jit(solution)/shard_map/assemble/pallas_call | solution.py:154
  137.5 12.6 %all-to-all-done.3 = bf16[32,32,128]{2,1,0:T(8,128)(2,1)S(1)} async-done(((bf16[32,32,128]{2,1,0:T(8,128)(2,1)}), bf16[32,32,128]{2,1,0:T(8,128)(2,1)S(1)}, u32[]{:S(2)}, u32[]{:S(2)}) %all-to-all-start.3) | async-done | bytes 262176 | tf_op jit(solution)/shard_map/all_to_all | solution.py:206
  150.2 0.1 copy.13
  150.3 0.1 reshape.85
  150.4 0.8 convert_reduce_fusion.1
  151.2 0.1 reshape.86
  151.3 0.8 convolution_bitcast_fusion
  (23 shorter events, 0.1 us)
Async XLA Ops:
  0.6 32.8 %collective-permute-start = (bf16[128,2048]{1,0:T(8,128)(2,1)}, bf16[128,2048]{1,0:T(8,128)(2,1)S(1)}, u32[]{:S(2)}, u32[]{:S(2)}) collective-permute-start(bf16[128,2048]{1,0:T(8,128)(2,1)} %refs_0_.1), channel_id=1, source_target_pairs={{0,1},{1,2},{2,3},{3,4},{4,5},{5,6},{6,7},{7,64},{64,65},{65,66},{... | collective-permute-start | bytes 1572872 | tf_op jit(solution)/shard_map/ppermute | solution.py:164
  5.0 28.4 %collective-permute-start.1 = (bf16[128,2048]{1,0:T(8,128)(2,1)}, bf16[128,2048]{1,0:T(8,128)(2,1)}, u32[]{:S(2)}, u32[]{:S(2)}) collective-permute-start(bf16[128,2048]{1,0:T(8,128)(2,1)} %refs_0_.1), channel_id=1, source_target_pairs={{0,71},{1,0},{2,1},{3,2},{4,3},{5,4},{6,5},{7,6},{64,7},{65,64},{6... | collective-permute-start | bytes 1572872 | tf_op jit(solution)/shard_map/ppermute | solution.py:164
  15.9 17.5 %all-to-all-start = ((bf16[8,32,128]{2,1,0:T(8,128)(2,1)}), bf16[8,32,128]{2,1,0:T(8,128)(2,1)S(1)}, u32[]{:S(2)}, u32[]{:S(2)}) async-start(bf16[8,32,128]{2,1,0:T(8,128)(2,1)} %broadcast_in_dim.8), calls=%async_computation | async-start | bytes 131072 | tf_op jit(solution)/shard_map/all_to_all | solution.py:29
  22.6 10.8 %collective-permute-start.2 = (bf16[16,2048]{1,0:T(8,128)(2,1)S(1)}, bf16[16,2048]{1,0:T(8,128)(2,1)S(1)}, u32[]{:S(2)}, u32[]{:S(2)}) collective-permute-start(bf16[16,2048]{1,0:T(8,128)(2,1)S(1)} %constant_dynamic-slice_fusion), channel_id=1, source_target_pairs={{0,4},{1,5},{2,6},{3,7},{4,0},{5,1},{6,2},{7,3},{8,12},{9,13},{10,... | collective-permute-start | bytes 196616 | tf_op jit(solution)/shard_map/ppermute | solution.py:181
  33.4 1.8 %copy-start.8 = (bf16[128,2048]{1,0:T(8,128)(2,1)}, bf16[128,2048]{1,0:T(8,128)(2,1)S(1)}, u32[]{:S(2)}) copy-start(bf16[128,2048]{1,0:T(8,128)(2,1)S(1)} %collective-permute-done.refs_0_) | copy-start | bytes 1572868
  35.2 19.7 %copy-start.1 = (bf16[128,2048]{1,0:T(8,128)(2,1)S(1)}, bf16[128,2048]{1,0:T(8,128)(2,1)}, u32[]{:S(2)}) copy-start(bf16[128,2048]{1,0:T(8,128)(2,1)} %refs_0_.1) | copy-start | bytes 1572868
  35.2 36.1 %all-to-all-start.1 = ((bf16[16,512,128]{2,1,0:T(8,128)(2,1)}), bf16[16,512,128]{2,1,0:T(8,128)(2,1)S(1)}, u32[]{:S(2)}, u32[]{:S(2)}) async-start(bf16[16,512,128]{2,1,0:T(8,128)(2,1)} %broadcast_in_dim.9), calls=%async_computation.1 | async-start | bytes 4194304 | tf_op jit(solution)/shard_map/all_to_all | solution.py:29
  42.1 27.2 %collective-permute-start.3 = (bf16[128,4096]{1,0:T(8,128)(2,1)}, bf16[128,4096]{1,0:T(8,128)(2,1)S(1)}, u32[]{:S(2)}, u32[]{:S(2)}) collective-permute-start(bf16[128,4096]{1,0:T(8,128)(2,1)} %x0.1), channel_id=1, source_target_pairs={{0,8},{8,0},{1,9},{9,1},{2,10},{10,2},{3,11},{11,3},{4,12},{12,4},... | collective-permute-start | bytes 3145736 | tf_op jit(solution)/shard_map/ppermute | solution.py:168
  49.5 17.1 %collective-permute-start.7 = (bf16[128,2048]{1,0:T(8,128)(2,1)}, bf16[128,2048]{1,0:T(8,128)(2,1)S(1)}, u32[]{:S(2)}, u32[]{:S(2)}) collective-permute-start(bf16[128,2048]{1,0:T(8,128)(2,1)} %collective-permute-done.1.refs_2_), channel_id=1, source_target_pairs={{0,71},{1,0},{2,1},{3,2},{4,3},{5,4},{6,5},{7,6},{64,7},{65,64},{6... | collective-permute-start | bytes 1572872 | tf_op jit(solution)/shard_map/ppermute | solution.py:164
  54.9 14.3 %collective-permute-start.4 = (bf16[128,2048]{1,0:T(8,128)(2,1)S(1)}, bf16[128,2048]{1,0:T(8,128)(2,1)S(1)}, u32[]{:S(2)}, u32[]{:S(2)}) collective-permute-start(bf16[128,2048]{1,0:T(8,128)(2,1)S(1)} %copy-done.1), channel_id=1, source_target_pairs={{0,8},{8,0},{1,9},{9,1},{2,10},{10,2},{3,11},{11,3},{4,12},{12,4},... | collective-permute-start | bytes 1572872 | tf_op jit(solution)/shard_map/ppermute | solution.py:168
  57.1 12.1 %collective-permute-start.6 = (bf16[128,2048]{1,0:T(8,128)(2,1)}, bf16[128,2048]{1,0:T(8,128)(2,1)S(1)}, u32[]{:S(2)}, u32[]{:S(2)}) collective-permute-start(bf16[128,2048]{1,0:T(8,128)(2,1)} %collective-permute-done.1.refs_2_), channel_id=1, source_target_pairs={{0,8},{8,0},{1,9},{9,1},{2,10},{10,2},{3,11},{11,3},{4,12},{12,4},... | collective-permute-start | bytes 1572872 | tf_op jit(solution)/shard_map/ppermute | solution.py:168
  59.3 10.0 %collective-permute-start.5 = (bf16[128,2048]{1,0:T(8,128)(2,1)}, bf16[128,2048]{1,0:T(8,128)(2,1)S(1)}, u32[]{:S(2)}, u32[]{:S(2)}) collective-permute-start(bf16[128,2048]{1,0:T(8,128)(2,1)} %copy-done.8), channel_id=1, source_target_pairs={{0,8},{8,0},{1,9},{9,1},{2,10},{10,2},{3,11},{11,3},{4,12},{12,4},... | collective-permute-start | bytes 1572872 | tf_op jit(solution)/shard_map/ppermute | solution.py:168
  66.5 2.8 %copy-start.9 = (bf16[128,2048]{1,0:T(8,128)(2,1)}, bf16[128,2048]{1,0:T(8,128)(2,1)S(1)}, u32[]{:S(2)}) copy-start(bf16[128,2048]{1,0:T(8,128)(2,1)S(1)} %collective-permute-done.7.refs_4_) | copy-start | bytes 1572868
  66.5 4.7 %collective-permute-start.8 = (bf16[128,2048]{1,0:T(8,128)(2,1)S(1)}, bf16[128,2048]{1,0:T(8,128)(2,1)}, u32[]{:S(2)}, u32[]{:S(2)}) collective-permute-start(bf16[128,2048]{1,0:T(8,128)(2,1)S(1)} %collective-permute-done.7.refs_4_), channel_id=1, source_target_pairs={{0,8},{8,0},{1,9},{9,1},{2,10},{10,2},{3,11},{11,3},{4,12},{12,4},... | collective-permute-start | bytes 1572872 | tf_op jit(solution)/shard_map/ppermute | solution.py:168
  69.2 2.0 %copy-start.2 = (bf16[128,2048]{1,0:T(8,128)(2,1)}, bf16[128,2048]{1,0:T(8,128)(2,1)S(1)}, u32[]{:S(2)}) copy-start(bf16[128,2048]{1,0:T(8,128)(2,1)S(1)} %collective-permute-done.4.g1.refs_1_) | copy-start | bytes 1572868
  69.3 0.9 copy-start.10
  69.3 1.0 copy-start.11
  70.3 1.0 copy-start.3
  71.3 1.3 copy-start
  76.9 32.1 %all-to-all-start.2 = ((f32[16,128,128]{2,1,0:T(8,128)}), f32[16,128,128]{2,1,0:T(8,128)S(1)}, u32[]{:S(2)}, u32[]{:S(2)}) async-start(f32[16,128,128]{2,1,0:T(8,128)} %low_rank.1), calls=%async_computation.2 | async-start | bytes 2097152 | tf_op jit(solution)/shard_map/all_to_all | solution.py:199
  91.8 17.3 %collective-permute-start.10 = (bf16[256,512]{1,0:T(8,128)(2,1)}, bf16[256,512]{1,0:T(8,128)(2,1)S(1)}, u32[]{:S(2)}, u32[]{:S(2)}) collective-permute-start(bf16[256,512]{1,0:T(8,128)(2,1)} %get-tuple-element.37), channel_id=1, source_target_pairs={{0,1},{1,2},{2,3},{3,4},{4,5},{5,6},{6,7},{7,64},{64,65},{65,66},{... | collective-permute-start | bytes 786440 | tf_op jit(solution)/shard_map/ppermute | solution.py:164
  96.4 21.4 %collective-permute-start.11 = (bf16[256,512]{1,0:T(8,128)(2,1)}, bf16[256,512]{1,0:T(8,128)(2,1)S(1)}, u32[]{:S(2)}, u32[]{:S(2)}) collective-permute-start(bf16[256,512]{1,0:T(8,128)(2,1)} %get-tuple-element.38), channel_id=1, source_target_pairs={{0,2},{1,3},{2,4},{3,5},{4,6},{5,7},{6,64},{7,65},{64,66},{65,67},... | collective-permute-start | bytes 786440 | tf_op jit(solution)/shard_map/ppermute | solution.py:164
  99.9 17.9 %collective-permute-start.9 = (bf16[256,512]{1,0:T(8,128)(2,1)}, bf16[256,512]{1,0:T(8,128)(2,1)S(1)}, u32[]{:S(2)}, u32[]{:S(2)}) collective-permute-start(bf16[256,512]{1,0:T(8,128)(2,1)} %get-tuple-element.36), channel_id=1, source_target_pairs={{0,71},{1,0},{2,1},{3,2},{4,3},{5,4},{6,5},{7,6},{64,7},{65,64},{6... | collective-permute-start | bytes 786440 | tf_op jit(solution)/shard_map/ppermute | solution.py:164
  109.1 24.5 %copy-start.4 = (bf16[256,512]{1,0:T(8,128)(2,1)}, bf16[256,512]{1,0:T(8,128)(2,1)S(1)}, u32[]{:S(2)}) copy-start(bf16[256,512]{1,0:T(8,128)(2,1)S(1)} %collective-permute-done.10.down) | copy-start | bytes 786436
  117.9 15.8 %copy-start.5 = (bf16[256,512]{1,0:T(8,128)(2,1)}, bf16[256,512]{1,0:T(8,128)(2,1)S(1)}, u32[]{:S(2)}) copy-start(bf16[256,512]{1,0:T(8,128)(2,1)S(1)} %collective-permute-done.11.down2) | copy-start | bytes 786436
  117.9 15.8 %copy-start.6 = (bf16[256,512]{1,0:T(8,128)(2,1)}, bf16[256,512]{1,0:T(8,128)(2,1)S(1)}, u32[]{:S(2)}) copy-start(bf16[256,512]{1,0:T(8,128)(2,1)S(1)} %collective-permute-done.9.up) | copy-start | bytes 786436
  118.7 31.4 %all-to-all-start.3 = ((bf16[32,32,128]{2,1,0:T(8,128)(2,1)}), bf16[32,32,128]{2,1,0:T(8,128)(2,1)S(1)}, u32[]{:S(2)}, u32[]{:S(2)}) async-start(bf16[32,32,128]{2,1,0:T(8,128)(2,1)} %bitcast.11), calls=%async_computation.3 | async-start | bytes 524288 | tf_op jit(solution)/shard_map/all_to_all | solution.py:206
  129.7 20.7 %copy-start.13 = (f32[1,8192]{1,0:T(1,128)S(1)}, f32[1,8192]{1,0:T(1,128)}, u32[]{:S(2)}) copy-start(f32[1,8192]{1,0:T(1,128)} %param.11) | copy-start | bytes 98308
  129.7 20.7 %copy-start.14 = (f32[1,8192]{1,0:T(1,128)S(1)}, f32[1,8192]{1,0:T(1,128)}, u32[]{:S(2)}) copy-start(f32[1,8192]{1,0:T(1,128)} %param.10) | copy-start | bytes 98308
  129.7 21.6 %copy-start.12 = (bf16[512,256]{1,0:T(8,128)(2,1)S(1)}, bf16[512,256]{1,0:T(8,128)(2,1)}, u32[]{:S(2)}) copy-start(bf16[512,256]{1,0:T(8,128)(2,1)} %param.9) | copy-start | bytes 786436
  129.8 3.8 %collective-permute-start.12 = (bf16[4,128,512]{2,1,0:T(8,128)(2,1)S(1)}, bf16[4,128,512]{2,1,0:T(8,128)(2,1)S(1)}, u32[]{:S(2)}, u32[]{:S(2)}) collective-permute-start(bf16[4,128,512]{2,1,0:T(8,128)(2,1)S(1)} %pad_maximum_fusion), channel_id=1, source_target_pairs={{0,8},{8,0},{1,9},{9,1},{2,10},{10,2},{3,11},{11,3},{4,12},{12,4},... | collective-permute-start | bytes 1572872 | tf_op jit(solution)/shard_map/ppermute | solution.py:168
  133.6 0.8 copy-start.7

commit v4 on v3

v4 whole, which is shorter than its diff:
```python
import functools
import math

import jax
import jax.numpy as jnp
from jax import lax
from jax.experimental import pallas as pl
from jax.experimental.pallas import tpu as pltpu
from jax.sharding import Mesh
from jax.sharding import PartitionSpec as P

STEP = 1000

beta_one = 0.9
beta_two = 0.999
epsilon = 1e-08

AXES = ("y", "zh", "x", "c", "q", "p")
SIZES = (4, 2, 4, 2, 4, 2)
PLANE = ("y", "x")
LINE = ("q", "p")
RING = ("zh", "q", "p")
COLUMN = ("zh", "c", "q", "p")
F32, BF16 = jnp.float32, jnp.bfloat16
COST = 20 << 30
LINE_COST = 20 << 30
FEATURE_COST = 1 << 20
HBM = pl.BlockSpec(memory_space=pltpu.HBM)
VMEM = pl.BlockSpec(memory_space=pltpu.VMEM)
PARAMS = pltpu.CompilerParams(vmem_limit_bytes=20 * 1024 * 1024)


def spread(block, axes, count):
    sent = jnp.broadcast_to(block[None], (count,) + block.shape)
    return lax.all_to_all(sent, axes, 0, 0, tiled=True)


def dot(a, b, dims):
    return lax.dot_general(a, b, (dims, ((), ())), preferred_element_type=F32)


def low_kernel(scale, x0, x1, g0, g1, mixed, out, sent, sems):
    members, _, half = mixed.shape
    rows = 256 // 8
    depth = members * rows
    proj = []
    for x in (x0, x1):
        total = None
        for s in range(8):
            basis = mixed[:, s * rows : (s + 1) * rows, :].reshape(depth, half)
            part = dot(x[:, s * depth : (s + 1) * depth], basis, ((1,), (0,)))
            total = part if total is None else total + part
        proj.append(total.astype(BF16))
    width = out.shape[1] // 2
    stores = []
    for y in range(4):
        for zh in range(2):
            at = (y * 2 + zh) * 4 * width
            part = dot(g0[:, at : at + 4 * width], proj[0], ((0,), (0,))) + dot(
                g1[:, at : at + 4 * width], proj[1], ((0,), (0,))
            )
            part = (part * scale).astype(BF16)
            for x in range(4):
                sent[y * 4 + x, zh * width : (zh + 1) * width, :] = part[
                    x * width : (x + 1) * width
                ]
        own = pl.ds(4 * y, 4)
        stores.append(pltpu.make_async_copy(sent.at[own], out.at[own], sems.at[y]))
        stores[-1].start()
    for store in stores:
        store.wait()


def low_rank(x0, x1, g0, g1, mixed, scale):
    members, _, half = mixed.shape
    shape = (members, g0.shape[1] // members, half)
    return pl.pallas_call(
        functools.partial(low_kernel, scale),
        in_specs=[VMEM] * 5,
        out_specs=HBM,
        out_shape=jax.ShapeDtypeStruct(shape, BF16),
        scratch_shapes=[pltpu.VMEM(shape, BF16), pltpu.SemaphoreType.DMA((4,))],
        cost_estimate=pl.CostEstimate(flops=1 << 20, bytes_accessed=1 << 16, transcendentals=0),
        name="low_rank",
    )(x0, x1, g0, g1, mixed)


def line_kernel(came, out):
    total = came[0].astype(F32)
    for i in range(1, came.shape[0]):
        total = total + came[i].astype(F32)
    total = total.astype(BF16)
    cols = out.shape[1]
    for i in range(32):
        out[i] = total[(i // 8) * cols : (i // 8 + 1) * cols]


def to_line(came):
    _, rows, half = came.shape
    return pl.pallas_call(
        line_kernel,
        out_shape=jax.ShapeDtypeStruct((32, rows // 4, half), BF16),
        compiler_params=PARAMS,
        cost_estimate=pl.CostEstimate(flops=LINE_COST, bytes_accessed=1 << 16, transcendentals=0),
        name="to_line",
    )(came)


def total_kernel(parts, out):
    for c in range(2):
        total = None
        for zh in range(2):
            for i in range(8):
                part = parts[(zh * 2 + c) * 8 + i].astype(F32)
                total = part if total is None else total + part
        out[c] = total


def total_of(parts):
    return pl.pallas_call(
        total_kernel,
        out_shape=jax.ShapeDtypeStruct((2,) + parts.shape[1:], F32),
        compiler_params=PARAMS,
        cost_estimate=pl.CostEstimate(flops=COST, bytes_accessed=1 << 16, transcendentals=0),
        name="total",
    )(parts)


def feature_kernel(count, core, *refs):
    tokens, (weight, mixed), outs = refs[:count], refs[count : count + 2], refs[count + 2 : -3]
    rows, made, sems = refs[-3:]
    feat = weight.shape[0] // 2
    rows[:feat, :] = weight[pl.ds(pl.multiple_of(core[0] * feat, feat), feat), :]
    for g in range(16):
        group = mixed[:, 256 + g * 16 : 256 + (g + 1) * 16, :]
        rows[feat:, g * 128 : (g + 1) * 128] = group.reshape(feat, 128)
    stores = []
    for i in reversed(range(len(outs))):
        pair = jnp.concatenate([tokens[2 * i][...], tokens[2 * i + 1][...]], axis=0)
        made[i] = dot(pair, rows[...], ((1,), (1,))).astype(BF16)
        stores.append(pltpu.make_async_copy(made.at[i], outs[i], sems.at[i]))
        stores[-1].start()
    for store in stores:
        store.wait()


def features(core, tokens, weight, mixed):
    n = tokens[0].shape[0]
    count = len(tokens)
    shape = (2 * n, weight.shape[0])
    return pl.pallas_call(
        functools.partial(feature_kernel, count),
        in_specs=[pl.BlockSpec(memory_space=pltpu.SMEM)] + [VMEM] * (count + 2),
        out_specs=[HBM] * (count // 2),
        out_shape=[jax.ShapeDtypeStruct(shape, BF16)] * (count // 2),
        scratch_shapes=[
            pltpu.VMEM(weight.shape, BF16),
            pltpu.VMEM((count // 2,) + shape, BF16),
            pltpu.SemaphoreType.DMA((count // 2,)),
        ],
        cost_estimate=pl.CostEstimate(
            flops=FEATURE_COST, bytes_accessed=1 << 16, transcendentals=0
        ),
        name="features",
    )(core[None], *tokens, weight, mixed)


def assemble_kernel(where, near, up, down, down2, crossed, out):
    line, core = where[0], where[1]
    feat, n = near.shape[1] // 2, crossed.shape[1]
    for i, (ref, offset) in enumerate(((near, 0), (up, 1), (down, 7), (down2, 6))):
        for r in range(2):
            shard = lax.rem(line + offset + 4 * r, 8)
            at = pl.multiple_of((shard * 2 + core) * feat, feat)
            out[:, pl.ds(at, feat)] = ref[:n, r * feat : (r + 1) * feat]
            at = pl.multiple_of((shard * 2 + 1 - core) * feat, feat)
            out[:, pl.ds(at, feat)] = crossed[i, :, r * feat : (r + 1) * feat]


def assemble(where, pieces, crossed):
    _, n, wide = crossed.shape
    return pl.pallas_call(
        assemble_kernel,
        in_specs=[pl.BlockSpec(memory_space=pltpu.SMEM)] + [VMEM] * 5,
        out_shape=jax.ShapeDtypeStruct((n, 8 * wide), BF16),
        compiler_params=PARAMS,
        cost_estimate=pl.CostEstimate(flops=0, bytes_accessed=1 << 16, transcendentals=0),
        name="assemble",
    )(where, *pieces, crossed)


def ring(value, step):
    return lax.ppermute(value, RING, [(i, (i + step) % 16) for i in range(16)])


def swap_cores(value):
    return lax.ppermute(value, "c", [(0, 1), (1, 0)])


def on_device(inputs, out_grad, weight, proj_basis, first_moment, second_moment):
    core = lax.axis_index("c")
    line = lax.axis_index(LINE)
    plane = lax.axis_index(PLANE)
    n, feat = inputs.shape[0], weight.shape[0] // 2
    scale = 1.0 / math.sqrt(n * 512)
    half = proj_basis.shape[1] // 2

    rows = feat // 16
    piece = lax.dynamic_slice(weight, (core * feat + plane * rows, 0), (rows, weight.shape[1]))
    piece = ring(piece, 4)
    piece = piece.reshape(rows, 16, 128).transpose(1, 0, 2).reshape(16 * rows, 128)
    p_rows = proj_basis.shape[0] // 16
    p_piece = lax.dynamic_slice(proj_basis, (plane * p_rows, core * half), (p_rows, half))
    p_line = spread(p_piece, LINE, 8).reshape(8 * p_rows, half)

    grad_c = swap_cores(out_grad)
    inputs_c = swap_cores(inputs)
    after = ring(out_grad, -1)
    before = ring(out_grad, 1)
    p_line, after = lax.optimization_barrier((p_line, after))
    mixed = spread(jnp.concatenate([p_line, piece]), PLANE, 16)
    after2 = ring(after, -1)
    far = [before, swap_cores(before), after, swap_cores(after), after2, swap_cores(after2)]
    mixed, inputs_c, grad_c, far = lax.optimization_barrier((mixed, inputs_c, grad_c, far))

    low = low_rank(inputs, inputs_c, out_grad, grad_c, mixed, scale)
    low, mixed = lax.optimization_barrier((low, mixed))
    came = lax.all_to_all(low, PLANE, 0, 0, tiled=True)
    near, o_before, o_after, o_after2 = features(
        core, [out_grad, grad_c] + far, weight, mixed
    )
    line_parts = to_line(came)
    line_parts, o_after2 = lax.optimization_barrier((line_parts, o_after2))
    low = total_of(lax.all_to_all(line_parts, COLUMN, 0, 0, tiled=True))
    cols = out_grad.shape[1] // 64
    flat_grad = low.transpose(0, 2, 1).reshape(1, 2 * half * cols)
    new_first = beta_one * first_moment + (1.0 - beta_one) * flat_grad
    new_second = beta_two * second_moment + (1.0 - beta_two) * flat_grad * flat_grad
    corr_one = 1.0 - beta_one**STEP
    corr_two = 1.0 - beta_two**STEP
    direction = (new_first / corr_one / (jnp.sqrt(new_second / corr_two) + epsilon)).astype(BF16)
    direction = direction.reshape(2 * half, cols)
    update = jnp.dot(proj_basis, direction, preferred_element_type=F32)

    pieces = [near, ring(o_before, -1), ring(o_after, 1), ring(o_after2, 2)]
    crossed = swap_cores(jnp.stack([v[n:] for v in pieces]))
    input_grad = assemble(jnp.stack([line, core]), pieces, crossed)
    return (input_grad, new_first, new_second, update)


def solution(mesh):
    fine = Mesh(mesh.devices.reshape(SIZES), AXES)
    dp, fsdp = AXES[:4], AXES[4:]
    in_specs = (
        P(AXES, None),
        P(AXES, None),
        P(fsdp, None),
        P(fsdp, None),
        P(dp, None),
        P(dp, None),
    )
    out_specs = (P(AXES, None), P(dp, None), P(dp, None), P(fsdp, dp))
    return jax.shard_map(
        on_device, mesh=fine, in_specs=in_specs, out_specs=out_specs, check_vma=False
    )
```

time: 153 us -> 136 us (0.89)
  waiting for transfers between devices: 31 us -> 21.1 us
  Pallas kernels: 19.9 us -> 13.5 us
    ppermute x6 -> x7, starting transfers between devices: 31.9 us -> 41.8 us  [ring(): return lax.ppermute(value, RING, [(i, (i + step) % 16) for i in range(16)])]
    ppermute x1 -> x0, starting transfers between devices: 7.27 us -> none  [on_device(): piece = lax.ppermute(piece, LINE, [(i, (i + 4) % 8) for i in range(8)])]
    all_to_all x2, waiting for transfers between devices: 12.6 us -> 5.61 us  [the longest x1 5.61 us: on_device(): low = total_of(lax.all_to_all(line_parts, COLUMN, 0, 0, tiled=True))]
    pallas_call x4 -> x5, Pallas kernels: 19.9 us -> 13.5 us  [the longest x1 6.66 us: features(): pl.pallas_call(functools.partial(feature_kernel, count), in_specs=[pl.Blo...]
    ppermute x1 -> x0, waiting for transfers between devices: 3.48 us -> none  [on_device(): piece = lax.ppermute(piece, LINE, [(i, (i + 4) % 8) for i in range(8)])]
    all_to_all x2, starting transfers between devices: 12.8 us -> 10.2 us  [spread(): return lax.all_to_all(sent, axes, 0, 0, tiled=True)]
    ppermute x6, starting transfers between devices: 18.7 us -> 20.8 us  [swap_cores(): return lax.ppermute(value, 'c', [(0, 1), (1, 0)])]
    all_to_all x2, starting transfers between devices: 17 us -> 15.2 us  [the longest x1 8.24 us: on_device(): low = total_of(lax.all_to_all(line_parts, COLUMN, 0, 0, tiled=True))]
  transfers between devices with their start and end apart: 17 -> 17, of which waited for: 5 -> 6; matrix products, arithmetic and copies ran while one was open for 3% -> 2% of each run, Pallas kernels for 10% -> 7%
where the time goes in v4:
time: 136 us; the launch traced here: 134 us
  starting transfers between devices  88 us (65%)
  waiting for transfers between devices  21.1 us (16%)
  Pallas kernels  13.5 us (10%)
  local copies, waits for them, and re-layouts  8.72 us (6%)
    ppermute x7, starting transfers between devices, ring(): return lax.ppermute(value, RING, [(i, (i + step) % 16) for i in range(16)])  41.8 us
    ppermute x6, starting transfers between devices, swap_cores(): return lax.ppermute(value, 'c', [(0, 1), (1, 0)])  20.8 us
    ppermute x7, waiting for transfers between devices, ring(): return lax.ppermute(value, RING, [(i, (i + step) % 16) for i in range(16)])  14.1 us
    all_to_all x2, starting transfers between devices, spread(): return lax.all_to_all(sent, axes, 0, 0, tiled=True)  10.2 us
    all_to_all x1, starting transfers between devices, on_device(): low = total_of(lax.all_to_all(line_parts, COLUMN, 0, 0, tiled=True))  8.24 us
    all_to_all x1, starting transfers between devices, on_device(): came = lax.all_to_all(low, PLANE, 0, 0, tiled=True)  6.95 us
    pallas_call x1, Pallas kernels, features(): pl.pallas_call(functools.partial(feature_kernel, count), in_specs=[pl.Blo...  6.66 us
    all_to_all x1, waiting for transfers between devices, on_device(): low = total_of(lax.all_to_all(line_parts, COLUMN, 0, 0, tiled=True))  5.61 us
  transfers between devices with their start and end apart: 17, of which 6 were waited for; matrix products, arithmetic and copies ran while one was open for 2% of the time, Pallas kernels for 7%

profile of v4, /device:TPU:1, one launch (start us, length us, event | category | flops | bytes accessed | tf_op | source)
XLA Modules:
  0.0 134.1 jit_solution(1860058090854915027)
XLA Ops:
  0.6 12.0 %collective-permute-start = (bf16[128,2048]{1,0:T(8,128)(2,1)}, bf16[128,2048]{1,0:T(8,128)(2,1)}, u32[]{:S(2)}, u32[]{:S(2)}) collective-permute-start(bf16[128,2048]{1,0:T(8,128)(2,1)} %refs_0_.1), channel_id=1, source_target_pairs={{0,71},{1,0},{2,1},{3,2},{4,3},{5,4},{6,5},{7,6},{64,7},{65,64},{6... | collective-permute-start | bytes 1572872 | tf_op jit(solution)/shard_map/ppermute | solution.py:193
  12.6 0.7 dynamic_slice.6
  13.3 0.6 broadcast_in_dim.4
  13.9 3.4 %all-to-all-start = ((bf16[8,32,128]{2,1,0:T(8,128)(2,1)}), bf16[8,32,128]{2,1,0:T(8,128)(2,1)S(1)}, u32[]{:S(2)}, u32[]{:S(2)}) async-start(bf16[8,32,128]{2,1,0:T(8,128)(2,1)} %broadcast_in_dim.4), calls=%async_computation | async-start | bytes 131072 | tf_op jit(solution)/shard_map/all_to_all | solution.py:35
  17.3 0.8 constant_dynamic-slice_fusion
  18.2 7.2 %collective-permute-start.1 = (bf16[16,2048]{1,0:T(8,128)(2,1)S(1)}, bf16[16,2048]{1,0:T(8,128)(2,1)S(1)}, u32[]{:S(2)}, u32[]{:S(2)}) collective-permute-start(bf16[16,2048]{1,0:T(8,128)(2,1)S(1)} %constant_dynamic-slice_fusion), channel_id=1, source_target_pairs={{0,4},{1,5},{2,6},{3,7},{4,64},{5,65},{6,66},{7,67},{64,68},{65,69... | collective-permute-start | bytes 196616 | tf_op jit(solution)/shard_map/ppermute | solution.py:193
  25.3 3.4 %collective-permute-done.1 = bf16[16,2048]{1,0:T(8,128)(2,1)S(1)} collective-permute-done((bf16[16,2048]{1,0:T(8,128)(2,1)S(1)}, bf16[16,2048]{1,0:T(8,128)(2,1)S(1)}, u32[]{:S(2)}, u32[]{:S(2)}) %collective-permute-start.1) | collective-permute-done | bytes 65568 | tf_op jit(solution)/shard_map/ppermute | solution.py:193
  28.7 0.0 all-to-all-done
  28.8 0.0 collective-permute-done.refs_4_
  28.8 1.8 %broadcast_in_dim.5 = bf16[16,512,128]{2,1,0:T(8,128)(2,1)} broadcast(bf16[512,128]{1,0:T(8,128)(2,1)S(1)} %pad_maximum_fusion.1), dimensions={1,2} | broadcast | bytes 2228224 | tf_op jit(solution)/shard_map/broadcast_in_dim | solution.py:34
  30.6 6.9 %all-to-all-start.1 = ((bf16[16,512,128]{2,1,0:T(8,128)(2,1)}), bf16[16,512,128]{2,1,0:T(8,128)(2,1)S(1)}, u32[]{:S(2)}, u32[]{:S(2)}) async-start(bf16[16,512,128]{2,1,0:T(8,128)(2,1)} %broadcast_in_dim.5), calls=%async_computation.1 | async-start | bytes 4194304 | tf_op jit(solution)/shard_map/all_to_all | solution.py:35
  37.4 0.0 copy-done.2
  37.5 3.8 %collective-permute-start.4 = (bf16[128,2048]{1,0:T(8,128)(2,1)S(1)}, bf16[128,2048]{1,0:T(8,128)(2,1)S(1)}, u32[]{:S(2)}, u32[]{:S(2)}) collective-permute-start(bf16[128,2048]{1,0:T(8,128)(2,1)S(1)} %copy-done.2), channel_id=1, source_target_pairs={{0,1},{1,2},{2,3},{3,4},{4,5},{5,6},{6,7},{7,64},{64,65},{65,66},{... | collective-permute-start | bytes 1572872 | tf_op jit(solution)/shard_map/ppermute | solution.py:193
  41.2 4.6 %collective-permute-start.2 = (bf16[128,4096]{1,0:T(8,128)(2,1)}, bf16[128,4096]{1,0:T(8,128)(2,1)S(1)}, u32[]{:S(2)}, u32[]{:S(2)}) collective-permute-start(bf16[128,4096]{1,0:T(8,128)(2,1)} %x0.1), channel_id=1, source_target_pairs={{0,8},{8,0},{1,9},{9,1},{2,10},{10,2},{3,11},{11,3},{4,12},{12,4},... | collective-permute-start | bytes 3145736 | tf_op jit(solution)/shard_map/ppermute | solution.py:197
  45.8 8.0 %collective-permute-start.7 = (bf16[128,2048]{1,0:T(8,128)(2,1)}, bf16[128,2048]{1,0:T(8,128)(2,1)S(1)}, u32[]{:S(2)}, u32[]{:S(2)}) collective-permute-start(bf16[128,2048]{1,0:T(8,128)(2,1)} %collective-permute-done.refs_4_), channel_id=1, source_target_pairs={{0,71},{1,0},{2,1},{3,2},{4,3},{5,4},{6,5},{7,6},{64,7},{65,64},{6... | collective-permute-start | bytes 1572872 | tf_op jit(solution)/shard_map/ppermute | solution.py:193
  53.8 2.2 %collective-permute-start.3 = (bf16[128,2048]{1,0:T(8,128)(2,1)S(1)}, bf16[128,2048]{1,0:T(8,128)(2,1)S(1)}, u32[]{:S(2)}, u32[]{:S(2)}) collective-permute-start(bf16[128,2048]{1,0:T(8,128)(2,1)S(1)} %copy-done.2), channel_id=1, source_target_pairs={{0,8},{8,0},{1,9},{9,1},{2,10},{10,2},{3,11},{11,3},{4,12},{12,4},... | collective-permute-start | bytes 1572872 | tf_op jit(solution)/shard_map/ppermute | solution.py:197
  56.0 2.1 %collective-permute-start.6 = (bf16[128,2048]{1,0:T(8,128)(2,1)}, bf16[128,2048]{1,0:T(8,128)(2,1)S(1)}, u32[]{:S(2)}, u32[]{:S(2)}) collective-permute-start(bf16[128,2048]{1,0:T(8,128)(2,1)} %collective-permute-done.refs_4_), channel_id=1, source_target_pairs={{0,8},{8,0},{1,9},{9,1},{2,10},{10,2},{3,11},{11,3},{4,12},{12,4},... | collective-permute-start | bytes 1572872 | tf_op jit(solution)/shard_map/ppermute | solution.py:197
  58.2 2.6 %collective-permute-done.4.refs_2_ = bf16[128,2048]{1,0:T(8,128)(2,1)S(1)} collective-permute-done((bf16[128,2048]{1,0:T(8,128)(2,1)S(1)}, bf16[128,2048]{1,0:T(8,128)(2,1)S(1)}, u32[]{:S(2)}, u32[]{:S(2)}) %collective-permute-start.4) | collective-permute-done | bytes 524320 | tf_op jit(solution)/shard_map/ppermute | solution.py:193
  60.7 3.2 %collective-permute-start.5 = (bf16[128,2048]{1,0:T(8,128)(2,1)S(1)}, bf16[128,2048]{1,0:T(8,128)(2,1)S(1)}, u32[]{:S(2)}, u32[]{:S(2)}) collective-permute-start(bf16[128,2048]{1,0:T(8,128)(2,1)S(1)} %collective-permute-done.4.refs_2_), channel_id=1, source_target_pairs={{0,8},{8,0},{1,9},{9,1},{2,10},{10,2},{3,11},{11,3},{4,12},{12,4},... | collective-permute-start | bytes 1572872 | tf_op jit(solution)/shard_map/ppermute | solution.py:197
  64.0 1.5 %collective-permute-done.7.refs_6_ = bf16[128,2048]{1,0:T(8,128)(2,1)S(1)} collective-permute-done((bf16[128,2048]{1,0:T(8,128)(2,1)}, bf16[128,2048]{1,0:T(8,128)(2,1)S(1)}, u32[]{:S(2)}, u32[]{:S(2)}) %collective-permute-start.7) | collective-permute-done | bytes 524320 | tf_op jit(solution)/shard_map/ppermute | solution.py:193
  65.5 2.7 %collective-permute-start.8 = (bf16[128,2048]{1,0:T(8,128)(2,1)S(1)}, bf16[128,2048]{1,0:T(8,128)(2,1)}, u32[]{:S(2)}, u32[]{:S(2)}) collective-permute-start(bf16[128,2048]{1,0:T(8,128)(2,1)S(1)} %collective-permute-done.7.refs_6_), channel_id=1, source_target_pairs={{0,8},{8,0},{1,9},{9,1},{2,10},{10,2},{3,11},{11,3},{4,12},{12,4},... | collective-permute-start | bytes 1572872 | tf_op jit(solution)/shard_map/ppermute | solution.py:197
  68.1 0.0 collective-permute-done.3.g1.refs_1_
  68.2 0.0 copy-start.3
  68.2 0.0 collective-permute-done.6.refs_5_
  68.2 0.0 copy-start.7
  68.2 0.0 collective-permute-done.5.refs_3_
  68.2 0.0 copy-start.8
  68.2 0.0 collective-permute-done.2.x1
  68.2 0.8 copy-done.7
  69.0 0.2 copy-done.8
  69.2 1.0 copy-done.4
  70.2 0.0 collective-permute-done.8.refs_7_
  70.2 0.0 all-to-all-done.1.mixed.refs_9_
  70.2 0.0 copy-done.3
  70.2 0.0 copy-start.1
  70.2 1.3 %copy-done.1 = bf16[16,512,128]{2,1,0:T(8,128)(2,1)} copy-done((bf16[16,512,128]{2,1,0:T(8,128)(2,1)}, bf16[16,512,128]{2,1,0:T(8,128)(2,1)S(1)}, u32[]{:S(2)}) %copy-start.1) | copy-done | bytes 2097176
  71.5 4.4 %low_rank.1 = bf16[16,128,128]{2,1,0:T(8,128)(2,1)} custom-call(bf16[128,4096]{1,0:T(8,128)(2,1)} %x0.1, bf16[128,4096]{1,0:T(8,128)(2,1)} %copy-done.4, bf16[128,2048]{1,0:T(8,128)(2,1)} %refs_0_.1, bf16[128,2048]{1,0:T(8,128)(2,1)} %copy-done.3, bf16[16,512,128]{2,1,0:T(8,128)(2,1)} %copy-done.1), custom_call_target="tpu_custom_call" | custom-call | flops 1048576 | bytes 65536 | tf_op jit(solution)/shard_map/low_rank/pallas_call | solution.py:77
  75.9 6.9 %all-to-all-start.2 = ((bf16[16,128,128]{2,1,0:T(8,128)(2,1)}), bf16[16,128,128]{2,1,0:T(8,128)(2,1)S(1)}, u32[]{:S(2)}, u32[]{:S(2)}) async-start(bf16[16,128,128]{2,1,0:T(8,128)(2,1)} %low_rank.1), calls=%async_computation.2 | async-start | bytes 1048576 | tf_op jit(solution)/shard_map/all_to_all | solution.py:228
  82.9 6.7 %features.1 = (bf16[256,512]{1,0:T(8,128)(2,1)}, bf16[256,512]{1,0:T(8,128)(2,1)}, bf16[256,512]{1,0:T(8,128)(2,1)}, bf16[256,512]{1,0:T(8,128)(2,1)}) custom-call(s32[1]{0:T(128)} %bitcast.1.core, bf16[128,2048]{1,0:T(8,128)(2,1)} %refs_0_.1, bf16[128,2048]{1,0:T(8,128)(2,1)} %copy-done.3, bf16[128,2048]{1,0:T(8,128)(2,1)} %copy-done.5, ...), custom_call_target="tpu_custom_call" | custom-call | flops 1048576 | bytes 65536 | tf_op jit(solution)/shard_map/features/pallas_call | solution.py:151
  89.5 1.9 %collective-permute-start.10 = (bf16[256,512]{1,0:T(8,128)(2,1)}, bf16[256,512]{1,0:T(8,128)(2,1)S(1)}, u32[]{:S(2)}, u32[]{:S(2)}) collective-permute-start(bf16[256,512]{1,0:T(8,128)(2,1)} %get-tuple-element.37), channel_id=1, source_target_pairs={{0,1},{1,2},{2,3},{3,4},{4,5},{5,6},{6,7},{7,64},{64,65},{65,66},{... | collective-permute-start | bytes 786440 | tf_op jit(solution)/shard_map/ppermute | solution.py:193
  91.5 7.1 %collective-permute-start.9 = (bf16[256,512]{1,0:T(8,128)(2,1)}, bf16[256,512]{1,0:T(8,128)(2,1)S(1)}, u32[]{:S(2)}, u32[]{:S(2)}) collective-permute-start(bf16[256,512]{1,0:T(8,128)(2,1)} %get-tuple-element.36), channel_id=1, source_target_pairs={{0,71},{1,0},{2,1},{3,2},{4,3},{5,4},{6,5},{7,6},{64,7},{65,64},{6... | collective-permute-start | bytes 786440 | tf_op jit(solution)/shard_map/ppermute | solution.py:193
  98.5 0.9 slice_bitcast_fusion.3
  99.5 0.0 copy-start.12
  99.5 0.0 all-to-all-done.2.came
  99.5 0.8 to_line.1
  100.2 0.2 copy-done.12
  100.4 1.9 %collective-permute-start.11 = (bf16[256,512]{1,0:T(8,128)(2,1)S(1)}, bf16[256,512]{1,0:T(8,128)(2,1)S(1)}, u32[]{:S(2)}, u32[]{:S(2)}) collective-permute-start(bf16[256,512]{1,0:T(8,128)(2,1)S(1)} %copy-done.12), channel_id=1, source_target_pairs={{0,2},{1,3},{2,4},{3,5},{4,6},{5,7},{6,64},{7,65},{64,66},{65,67},... | collective-permute-start | bytes 786440 | tf_op jit(solution)/shard_map/ppermute | solution.py:193
  102.3 0.0 collective-permute-done.10.down
  102.4 8.2 %all-to-all-start.3 = ((bf16[32,32,128]{2,1,0:T(8,128)(2,1)}), bf16[32,32,128]{2,1,0:T(8,128)(2,1)S(1)}, u32[]{:S(2)}, u32[]{:S(2)}) async-start(bf16[32,32,128]{2,1,0:T(8,128)(2,1)} %to_line.1), calls=%async_computation.3 | async-start | bytes 524288 | tf_op jit(solution)/shard_map/all_to_all | solution.py:234
  110.6 0.0 collective-permute-done.9.up
  110.6 6.6 %collective-permute-done.11.down2 = bf16[256,512]{1,0:T(8,128)(2,1)S(1)} collective-permute-done((bf16[256,512]{1,0:T(8,128)(2,1)S(1)}, bf16[256,512]{1,0:T(8,128)(2,1)S(1)}, u32[]{:S(2)}, u32[]{:S(2)}) %collective-permute-start.11) | collective-permute-done | bytes 262176 | tf_op jit(solution)/shard_map/ppermute | solution.py:193
  117.3 0.1 pad_maximum_fusion
  117.4 5.9 %collective-permute-start.12 = (bf16[4,128,512]{2,1,0:T(8,128)(2,1)S(1)}, bf16[4,128,512]{2,1,0:T(8,128)(2,1)S(1)}, u32[]{:S(2)}, u32[]{:S(2)}) collective-permute-start(bf16[4,128,512]{2,1,0:T(8,128)(2,1)S(1)} %pad_maximum_fusion), channel_id=1, source_target_pairs={{0,8},{8,0},{1,9},{9,1},{2,10},{10,2},{3,11},{11,3},{4,12},{12,4},... | collective-permute-start | bytes 1572872 | tf_op jit(solution)/shard_map/ppermute | solution.py:197
  123.3 0.1 pad_add_fusion.where
  123.4 1.4 %collective-permute-done.12.crossed = bf16[4,128,512]{2,1,0:T(8,128)(2,1)S(1)} collective-permute-done((bf16[4,128,512]{2,1,0:T(8,128)(2,1)S(1)}, bf16[4,128,512]{2,1,0:T(8,128)(2,1)S(1)}, u32[]{:S(2)}, u32[]{:S(2)}) %collective-permute-start.12) | collective-permute-done | bytes 524320 | tf_op jit(solution)/shard_map/ppermute | solution.py:197
  124.8 0.0 copy-done
  124.8 1.6 %assemble.1 = bf16[128,4096]{1,0:T(8,128)(2,1)} custom-call(s32[2]{0:T(128)S(1)} %pad_add_fusion.where, bf16[256,512]{1,0:T(8,128)(2,1)S(1)} %copy-done, bf16[256,512]{1,0:T(8,128)(2,1)S(1)} %collective-permute-done.9.up, bf16[256,512]{1,0:T(8,128)(2,1)S(1)} %collective-permute-done.10.down, bf16[256,512]{1,0:T(8,128)(2,1)S(1)} %collective-permute-done.11.down2, ...), custom_call_target="tpu_custom_call" | custom-call | bytes 65536 | tf_op jit(solution)/shard_map/assemble/pallas_call | solution.py:182
  126.5 5.6 %all-to-all-done.3.parts = bf16[32,32,128]{2,1,0:T(8,128)(2,1)S(1)} async-done(((bf16[32,32,128]{2,1,0:T(8,128)(2,1)}), bf16[32,32,128]{2,1,0:T(8,128)(2,1)S(1)}, u32[]{:S(2)}, u32[]{:S(2)}) %all-to-all-start.3) | async-done | bytes 262176 | tf_op jit(solution)/shard_map/all_to_all | solution.py:234
  132.1 0.1 copy.12
  132.2 0.1 reshape.64
  132.4 0.8 convert_reduce_fusion
  133.2 0.1 reshape.65
  133.3 0.0 copy-done.9
  133.3 0.8 convolution_bitcast_fusion
  (19 shorter events, 0.1 us)
Async XLA Ops:
  0.6 28.1 %collective-permute-start = (bf16[128,2048]{1,0:T(8,128)(2,1)}, bf16[128,2048]{1,0:T(8,128)(2,1)}, u32[]{:S(2)}, u32[]{:S(2)}) collective-permute-start(bf16[128,2048]{1,0:T(8,128)(2,1)} %refs_0_.1), channel_id=1, source_target_pairs={{0,71},{1,0},{2,1},{3,2},{4,3},{5,4},{6,5},{7,6},{64,7},{65,64},{6... | collective-permute-start | bytes 1572872 | tf_op jit(solution)/shard_map/ppermute | solution.py:193
  13.9 14.8 %all-to-all-start = ((bf16[8,32,128]{2,1,0:T(8,128)(2,1)}), bf16[8,32,128]{2,1,0:T(8,128)(2,1)S(1)}, u32[]{:S(2)}, u32[]{:S(2)}) async-start(bf16[8,32,128]{2,1,0:T(8,128)(2,1)} %broadcast_in_dim.4), calls=%async_computation | async-start | bytes 131072 | tf_op jit(solution)/shard_map/all_to_all | solution.py:35
  18.2 10.5 %collective-permute-start.1 = (bf16[16,2048]{1,0:T(8,128)(2,1)S(1)}, bf16[16,2048]{1,0:T(8,128)(2,1)S(1)}, u32[]{:S(2)}, u32[]{:S(2)}) collective-permute-start(bf16[16,2048]{1,0:T(8,128)(2,1)S(1)} %constant_dynamic-slice_fusion), channel_id=1, source_target_pairs={{0,4},{1,5},{2,6},{3,7},{4,64},{5,65},{6,66},{7,67},{64,68},{65,69... | collective-permute-start | bytes 196616 | tf_op jit(solution)/shard_map/ppermute | solution.py:193
  30.5 6.9 %copy-start.2 = (bf16[128,2048]{1,0:T(8,128)(2,1)S(1)}, bf16[128,2048]{1,0:T(8,128)(2,1)}, u32[]{:S(2)}) copy-start(bf16[128,2048]{1,0:T(8,128)(2,1)} %refs_0_.1) | copy-start | bytes 1572868
  30.6 39.6 %all-to-all-start.1 = ((bf16[16,512,128]{2,1,0:T(8,128)(2,1)}), bf16[16,512,128]{2,1,0:T(8,128)(2,1)S(1)}, u32[]{:S(2)}, u32[]{:S(2)}) async-start(bf16[16,512,128]{2,1,0:T(8,128)(2,1)} %broadcast_in_dim.5), calls=%async_computation.1 | async-start | bytes 4194304 | tf_op jit(solution)/shard_map/all_to_all | solution.py:35
  37.5 23.3 %collective-permute-start.4 = (bf16[128,2048]{1,0:T(8,128)(2,1)S(1)}, bf16[128,2048]{1,0:T(8,128)(2,1)S(1)}, u32[]{:S(2)}, u32[]{:S(2)}) collective-permute-start(bf16[128,2048]{1,0:T(8,128)(2,1)S(1)} %copy-done.2), channel_id=1, source_target_pairs={{0,1},{1,2},{2,3},{3,4},{4,5},{5,6},{6,7},{7,64},{64,65},{65,66},{... | collective-permute-start | bytes 1572872 | tf_op jit(solution)/shard_map/ppermute | solution.py:193
  41.2 27.0 %collective-permute-start.2 = (bf16[128,4096]{1,0:T(8,128)(2,1)}, bf16[128,4096]{1,0:T(8,128)(2,1)S(1)}, u32[]{:S(2)}, u32[]{:S(2)}) collective-permute-start(bf16[128,4096]{1,0:T(8,128)(2,1)} %x0.1), channel_id=1, source_target_pairs={{0,8},{8,0},{1,9},{9,1},{2,10},{10,2},{3,11},{11,3},{4,12},{12,4},... | collective-permute-start | bytes 3145736 | tf_op jit(solution)/shard_map/ppermute | solution.py:197
  45.8 19.6 %collective-permute-start.7 = (bf16[128,2048]{1,0:T(8,128)(2,1)}, bf16[128,2048]{1,0:T(8,128)(2,1)S(1)}, u32[]{:S(2)}, u32[]{:S(2)}) collective-permute-start(bf16[128,2048]{1,0:T(8,128)(2,1)} %collective-permute-done.refs_4_), channel_id=1, source_target_pairs={{0,71},{1,0},{2,1},{3,2},{4,3},{5,4},{6,5},{7,6},{64,7},{65,64},{6... | collective-permute-start | bytes 1572872 | tf_op jit(solution)/shard_map/ppermute | solution.py:193
  53.8 14.3 %collective-permute-start.3 = (bf16[128,2048]{1,0:T(8,128)(2,1)S(1)}, bf16[128,2048]{1,0:T(8,128)(2,1)S(1)}, u32[]{:S(2)}, u32[]{:S(2)}) collective-permute-start(bf16[128,2048]{1,0:T(8,128)(2,1)S(1)} %copy-done.2), channel_id=1, source_target_pairs={{0,8},{8,0},{1,9},{9,1},{2,10},{10,2},{3,11},{11,3},{4,12},{12,4},... | collective-permute-start | bytes 1572872 | tf_op jit(solution)/shard_map/ppermute | solution.py:197
  56.0 12.2 %collective-permute-start.6 = (bf16[128,2048]{1,0:T(8,128)(2,1)}, bf16[128,2048]{1,0:T(8,128)(2,1)S(1)}, u32[]{:S(2)}, u32[]{:S(2)}) collective-permute-start(bf16[128,2048]{1,0:T(8,128)(2,1)} %collective-permute-done.refs_4_), channel_id=1, source_target_pairs={{0,8},{8,0},{1,9},{9,1},{2,10},{10,2},{3,11},{11,3},{4,12},{12,4},... | collective-permute-start | bytes 1572872 | tf_op jit(solution)/shard_map/ppermute | solution.py:197
  60.7 7.5 %copy-start.5 = (bf16[128,2048]{1,0:T(8,128)(2,1)}, bf16[128,2048]{1,0:T(8,128)(2,1)S(1)}, u32[]{:S(2)}) copy-start(bf16[128,2048]{1,0:T(8,128)(2,1)S(1)} %collective-permute-done.4.refs_2_) | copy-start | bytes 1572868
  60.7 7.5 %collective-permute-start.5 = (bf16[128,2048]{1,0:T(8,128)(2,1)S(1)}, bf16[128,2048]{1,0:T(8,128)(2,1)S(1)}, u32[]{:S(2)}, u32[]{:S(2)}) collective-permute-start(bf16[128,2048]{1,0:T(8,128)(2,1)S(1)} %collective-permute-done.4.refs_2_), channel_id=1, source_target_pairs={{0,8},{8,0},{1,9},{9,1},{2,10},{10,2},{3,11},{11,3},{4,12},{12,4},... | collective-permute-start | bytes 1572872 | tf_op jit(solution)/shard_map/ppermute | solution.py:197
  65.4 2.8 %copy-start.6 = (bf16[128,2048]{1,0:T(8,128)(2,1)}, bf16[128,2048]{1,0:T(8,128)(2,1)S(1)}, u32[]{:S(2)}) copy-start(bf16[128,2048]{1,0:T(8,128)(2,1)S(1)} %collective-permute-done.7.refs_6_) | copy-start | bytes 1572868
  65.5 4.7 %collective-permute-start.8 = (bf16[128,2048]{1,0:T(8,128)(2,1)S(1)}, bf16[128,2048]{1,0:T(8,128)(2,1)}, u32[]{:S(2)}, u32[]{:S(2)}) collective-permute-start(bf16[128,2048]{1,0:T(8,128)(2,1)S(1)} %collective-permute-done.7.refs_6_), channel_id=1, source_target_pairs={{0,8},{8,0},{1,9},{9,1},{2,10},{10,2},{3,11},{11,3},{4,12},{12,4},... | collective-permute-start | bytes 1572872 | tf_op jit(solution)/shard_map/ppermute | solution.py:197
  68.2 2.0 %copy-start.3 = (bf16[128,2048]{1,0:T(8,128)(2,1)}, bf16[128,2048]{1,0:T(8,128)(2,1)S(1)}, u32[]{:S(2)}) copy-start(bf16[128,2048]{1,0:T(8,128)(2,1)S(1)} %collective-permute-done.3.g1.refs_1_) | copy-start | bytes 1572868
  68.2 0.8 copy-start.7
  68.2 1.0 copy-start.8
  69.2 1.0 copy-start.4
  70.2 1.4 %copy-start.1 = (bf16[16,512,128]{2,1,0:T(8,128)(2,1)}, bf16[16,512,128]{2,1,0:T(8,128)(2,1)S(1)}, u32[]{:S(2)}) copy-start(bf16[16,512,128]{2,1,0:T(8,128)(2,1)S(1)} %all-to-all-done.1.mixed.refs_9_) | copy-start | bytes 6291460
  75.9 23.6 %all-to-all-start.2 = ((bf16[16,128,128]{2,1,0:T(8,128)(2,1)}), bf16[16,128,128]{2,1,0:T(8,128)(2,1)S(1)}, u32[]{:S(2)}, u32[]{:S(2)}) async-start(bf16[16,128,128]{2,1,0:T(8,128)(2,1)} %low_rank.1), calls=%async_computation.2 | async-start | bytes 1048576 | tf_op jit(solution)/shard_map/all_to_all | solution.py:228
  89.5 12.8 %collective-permute-start.10 = (bf16[256,512]{1,0:T(8,128)(2,1)}, bf16[256,512]{1,0:T(8,128)(2,1)S(1)}, u32[]{:S(2)}, u32[]{:S(2)}) collective-permute-start(bf16[256,512]{1,0:T(8,128)(2,1)} %get-tuple-element.37), channel_id=1, source_target_pairs={{0,1},{1,2},{2,3},{3,4},{4,5},{5,6},{6,7},{7,64},{64,65},{65,66},{... | collective-permute-start | bytes 786440 | tf_op jit(solution)/shard_map/ppermute | solution.py:193
  91.5 19.1 %collective-permute-start.9 = (bf16[256,512]{1,0:T(8,128)(2,1)}, bf16[256,512]{1,0:T(8,128)(2,1)S(1)}, u32[]{:S(2)}, u32[]{:S(2)}) collective-permute-start(bf16[256,512]{1,0:T(8,128)(2,1)} %get-tuple-element.36), channel_id=1, source_target_pairs={{0,71},{1,0},{2,1},{3,2},{4,3},{5,4},{6,5},{7,6},{64,7},{65,64},{6... | collective-permute-start | bytes 786440 | tf_op jit(solution)/shard_map/ppermute | solution.py:193
  99.5 1.0 copy-start.12
  100.2 24.6 %copy-start = (bf16[256,512]{1,0:T(8,128)(2,1)S(1)}, bf16[256,512]{1,0:T(8,128)(2,1)}, u32[]{:S(2)}) copy-start(bf16[256,512]{1,0:T(8,128)(2,1)} %get-tuple-element.35.near) | copy-start | bytes 786436
  100.4 16.9 %collective-permute-start.11 = (bf16[256,512]{1,0:T(8,128)(2,1)S(1)}, bf16[256,512]{1,0:T(8,128)(2,1)S(1)}, u32[]{:S(2)}, u32[]{:S(2)}) collective-permute-start(bf16[256,512]{1,0:T(8,128)(2,1)S(1)} %copy-done.12), channel_id=1, source_target_pairs={{0,2},{1,3},{2,4},{3,5},{4,6},{5,7},{6,64},{7,65},{64,66},{65,67},... | collective-permute-start | bytes 786440 | tf_op jit(solution)/shard_map/ppermute | solution.py:193
  102.4 29.7 %all-to-all-start.3 = ((bf16[32,32,128]{2,1,0:T(8,128)(2,1)}), bf16[32,32,128]{2,1,0:T(8,128)(2,1)S(1)}, u32[]{:S(2)}, u32[]{:S(2)}) async-start(bf16[32,32,128]{2,1,0:T(8,128)(2,1)} %to_line.1), calls=%async_computation.3 | async-start | bytes 524288 | tf_op jit(solution)/shard_map/all_to_all | solution.py:234
  117.4 7.4 %collective-permute-start.12 = (bf16[4,128,512]{2,1,0:T(8,128)(2,1)S(1)}, bf16[4,128,512]{2,1,0:T(8,128)(2,1)S(1)}, u32[]{:S(2)}, u32[]{:S(2)}) collective-permute-start(bf16[4,128,512]{2,1,0:T(8,128)(2,1)S(1)} %pad_maximum_fusion), channel_id=1, source_target_pairs={{0,8},{8,0},{1,9},{9,1},{2,10},{10,2},{3,11},{11,3},{4,12},{12,4},... | collective-permute-start | bytes 1572872 | tf_op jit(solution)/shard_map/ppermute | solution.py:197
  126.5 5.9 %copy-start.10 = (f32[1,8192]{1,0:T(1,128)S(1)}, f32[1,8192]{1,0:T(1,128)}, u32[]{:S(2)}) copy-start(f32[1,8192]{1,0:T(1,128)} %param.11) | copy-start | bytes 98308
  126.5 5.9 %copy-start.11 = (f32[1,8192]{1,0:T(1,128)S(1)}, f32[1,8192]{1,0:T(1,128)}, u32[]{:S(2)}) copy-start(f32[1,8192]{1,0:T(1,128)} %param.10) | copy-start | bytes 98308
  126.5 6.8 %copy-start.9 = (bf16[512,256]{1,0:T(8,128)(2,1)S(1)}, bf16[512,256]{1,0:T(8,128)(2,1)}, u32[]{:S(2)}) copy-start(bf16[512,256]{1,0:T(8,128)(2,1)} %param.9) | copy-start | bytes 786436

commit v5 on v4

--- a/solution.py
+++ b/solution.py
@@ -39,25 +39,42 @@
     return lax.dot_general(a, b, (dims, ((), ())), preferred_element_type=F32)
 
 
-def low_kernel(scale, x0, x1, g0, g1, mixed, out, sent, sems):
-    members, _, half = mixed.shape
-    rows = 256 // 8
+def low_kernel(scale, x0, x1, g0, g1, mixed, out, xs, gs, basis, sent, sems):
+    members, tail, half = basis.shape
+    first = pltpu.make_async_copy(mixed.at[:, pl.ds(0, tail)], basis, sems.at[0])
+    loads = [
+        pltpu.make_async_copy(ref, buf, sems.at[1 + i])
+        for i, (ref, buf) in enumerate(
+            ((x0, xs.at[0]), (x1, xs.at[1]), (g0, gs.at[0]), (g1, gs.at[1]))
+        )
+    ]
+    first.start()
+    for load in loads:
+        load.start()
+    first.wait()
+    rows = tail // 8
     depth = members * rows
     proj = []
-    for x in (x0, x1):
+    for i in range(2):
+        loads[i].wait()
         total = None
         for s in range(8):
-            basis = mixed[:, s * rows : (s + 1) * rows, :].reshape(depth, half)
-            part = dot(x[:, s * depth : (s + 1) * depth], basis, ((1,), (0,)))
+            part = dot(
+                xs[i, :, s * depth : (s + 1) * depth],
+                basis[:, s * rows : (s + 1) * rows, :].reshape(depth, half),
+                ((1,), (0,)),
+            )
             total = part if total is None else total + part
         proj.append(total.astype(BF16))
+    loads[2].wait()
+    loads[3].wait()
     width = out.shape[1] // 2
     stores = []
     for y in range(4):
         for zh in range(2):
             at = (y * 2 + zh) * 4 * width
-            part = dot(g0[:, at : at + 4 * width], proj[0], ((0,), (0,))) + dot(
-                g1[:, at : at + 4 * width], proj[1], ((0,), (0,))
+            part = dot(gs[0, :, at : at + 4 * width], proj[0], ((0,), (0,))) + dot(
+                gs[1, :, at : at + 4 * width], proj[1], ((0,), (0,))
             )
             part = (part * scale).astype(BF16)
             for x in range(4):
@@ -65,7 +82,7 @@
                     x * width : (x + 1) * width
                 ]
         own = pl.ds(4 * y, 4)
-        stores.append(pltpu.make_async_copy(sent.at[own], out.at[own], sems.at[y]))
+        stores.append(pltpu.make_async_copy(sent.at[own], out.at[own], sems.at[5 + y]))
         stores[-1].start()
     for store in stores:
         store.wait()
@@ -76,10 +93,16 @@
     shape = (members, g0.shape[1] // members, half)
     return pl.pallas_call(
         functools.partial(low_kernel, scale),
-        in_specs=[VMEM] * 5,
+        in_specs=[HBM] * 5,
         out_specs=HBM,
         out_shape=jax.ShapeDtypeStruct(shape, BF16),
-        scratch_shapes=[pltpu.VMEM(shape, BF16), pltpu.SemaphoreType.DMA((4,))],
+        scratch_shapes=[
+            pltpu.VMEM((2,) + x0.shape, BF16),
+            pltpu.VMEM((2,) + g0.shape, BF16),
+            pltpu.VMEM((members, 256, half), BF16),
+            pltpu.VMEM(shape, BF16),
+            pltpu.SemaphoreType.DMA((9,)),
+        ],
         cost_estimate=pl.CostEstimate(flops=1 << 20, bytes_accessed=1 << 16, transcendentals=0),
         name="low_rank",
     )(x0, x1, g0, g1, mixed)
@@ -127,36 +150,52 @@
 
 
 def feature_kernel(count, core, *refs):
-    tokens, (weight, mixed), outs = refs[:count], refs[count : count + 2], refs[count + 2 : -3]
-    rows, made, sems = refs[-3:]
+    tokens, (weight, mixed), outs = refs[:count], refs[count : count + 2], refs[count + 2 : -5]
+    held, came, rows, made, sems = refs[-5:]
     feat = weight.shape[0] // 2
-    rows[:feat, :] = weight[pl.ds(pl.multiple_of(core[0] * feat, feat), feat), :]
+    other = pltpu.make_async_copy(mixed.at[:, pl.ds(256, 256)], came, sems.at[count])
+    own = pltpu.make_async_copy(
+        weight.at[pl.ds(pl.multiple_of(core[0] * feat, feat), feat)],
+        rows.at[pl.ds(0, feat)],
+        sems.at[count + 1],
+    )
+    loads = [pltpu.make_async_copy(ref, held.at[i], sems.at[i]) for i, ref in enumerate(tokens)]
+    other.start()
+    own.start()
+    for load in reversed(loads):
+        load.start()
+    other.wait()
     for g in range(16):
-        group = mixed[:, 256 + g * 16 : 256 + (g + 1) * 16, :]
+        group = came[:, g * 16 : (g + 1) * 16, :]
         rows[feat:, g * 128 : (g + 1) * 128] = group.reshape(feat, 128)
+    own.wait()
     stores = []
     for i in reversed(range(len(outs))):
-        pair = jnp.concatenate([tokens[2 * i][...], tokens[2 * i + 1][...]], axis=0)
+        loads[2 * i + 1].wait()
+        loads[2 * i].wait()
+        pair = jnp.concatenate([held[2 * i], held[2 * i + 1]], axis=0)
         made[i] = dot(pair, rows[...], ((1,), (1,))).astype(BF16)
-        stores.append(pltpu.make_async_copy(made.at[i], outs[i], sems.at[i]))
+        stores.append(pltpu.make_async_copy(made.at[i], outs[i], sems.at[count + 2 + i]))
         stores[-1].start()
     for store in stores:
         store.wait()
 
 
 def features(core, tokens, weight, mixed):
-    n = tokens[0].shape[0]
+    n, depth = tokens[0].shape
     count = len(tokens)
     shape = (2 * n, weight.shape[0])
     return pl.pallas_call(
         functools.partial(feature_kernel, count),
-        in_specs=[pl.BlockSpec(memory_space=pltpu.SMEM)] + [VMEM] * (count + 2),
+        in_specs=[pl.BlockSpec(memory_space=pltpu.SMEM)] + [HBM] * (count + 2),
         out_specs=[HBM] * (count // 2),
         out_shape=[jax.ShapeDtypeStruct(shape, BF16)] * (count // 2),
         scratch_shapes=[
+            pltpu.VMEM((count, n, depth), BF16),
+            pltpu.VMEM((mixed.shape[0], 256, mixed.shape[2]), BF16),
             pltpu.VMEM(weight.shape, BF16),
             pltpu.VMEM((count // 2,) + shape, BF16),
-            pltpu.SemaphoreType.DMA((count // 2,)),
+            pltpu.SemaphoreType.DMA((count + 2 + count // 2,)),
         ],
         cost_estimate=pl.CostEstimate(
             flops=FEATURE_COST, bytes_accessed=1 << 16, transcendentals=0

time: 136 us -> 134 us (0.985)
  Pallas kernels: 13.5 us -> 11.7 us
  transfers between devices with their start and end apart: 17 -> 17, of which waited for: 6 -> 6; matrix products, arithmetic and copies ran while one was open for 2% -> 3% of each run, Pallas kernels for 7% -> 6%
where the time goes in v5:
time: 134 us; the launch traced here: 132 us
  starting transfers between devices  87.9 us (66%)
  waiting for transfers between devices  21.1 us (16%)
  Pallas kernels  11.7 us (9%)
  local copies, waits for them, and re-layouts  8.72 us (7%)
    ppermute x7, starting transfers between devices, ring(): return lax.ppermute(value, RING, [(i, (i + step) % 16) for i in range(16)])  41.8 us
    ppermute x6, starting transfers between devices, swap_cores(): return lax.ppermute(value, 'c', [(0, 1), (1, 0)])  20.7 us
    ppermute x7, waiting for transfers between devices, ring(): return lax.ppermute(value, RING, [(i, (i + step) % 16) for i in range(16)])  14.1 us
    all_to_all x2, starting transfers between devices, spread(): return lax.all_to_all(sent, axes, 0, 0, tiled=True)  10.2 us
    all_to_all x1, starting transfers between devices, on_device(): low = total_of(lax.all_to_all(line_parts, COLUMN, 0, 0, tiled=True))  8.24 us
    all_to_all x1, starting transfers between devices, on_device(): came = lax.all_to_all(low, PLANE, 0, 0, tiled=True)  6.95 us
    pallas_call x1, Pallas kernels, features(): pl.pallas_call(functools.partial(feature_kernel, count), in_specs=[pl.Blo...  5.64 us
    all_to_all x1, waiting for transfers between devices, on_device(): low = total_of(lax.all_to_all(line_parts, COLUMN, 0, 0, tiled=True))  5.63 us
  transfers between devices with their start and end apart: 17, of which 6 were waited for; matrix products, arithmetic and copies ran while one was open for 3% of the time, Pallas kernels for 6%

profile of v5, /device:TPU:1, one launch (start us, length us, event | category | flops | bytes accessed | tf_op | source)
XLA Modules:
  0.0 132.3 jit_solution(9690207124776104453)
XLA Ops:
  0.6 12.0 %collective-permute-start = (bf16[128,2048]{1,0:T(8,128)(2,1)}, bf16[128,2048]{1,0:T(8,128)(2,1)}, u32[]{:S(2)}, u32[]{:S(2)}) collective-permute-start(bf16[128,2048]{1,0:T(8,128)(2,1)} %refs_0_.1), channel_id=1, source_target_pairs={{0,71},{1,0},{2,1},{3,2},{4,3},{5,4},{6,5},{7,6},{64,7},{65,64},{6... | collective-permute-start | bytes 1572872 | tf_op jit(solution)/shard_map/ppermute | solution.py:232
  12.6 0.7 dynamic_slice.6
  13.3 0.6 broadcast_in_dim.4
  13.9 3.4 %all-to-all-start = ((bf16[8,32,128]{2,1,0:T(8,128)(2,1)}), bf16[8,32,128]{2,1,0:T(8,128)(2,1)S(1)}, u32[]{:S(2)}, u32[]{:S(2)}) async-start(bf16[8,32,128]{2,1,0:T(8,128)(2,1)} %broadcast_in_dim.4), calls=%async_computation | async-start | bytes 131072 | tf_op jit(solution)/shard_map/all_to_all | solution.py:35
  17.3 0.8 constant_dynamic-slice_fusion
  18.2 7.2 %collective-permute-start.1 = (bf16[16,2048]{1,0:T(8,128)(2,1)S(1)}, bf16[16,2048]{1,0:T(8,128)(2,1)S(1)}, u32[]{:S(2)}, u32[]{:S(2)}) collective-permute-start(bf16[16,2048]{1,0:T(8,128)(2,1)S(1)} %constant_dynamic-slice_fusion), channel_id=1, source_target_pairs={{0,4},{1,5},{2,6},{3,7},{4,64},{5,65},{6,66},{7,67},{64,68},{65,69... | collective-permute-start | bytes 196616 | tf_op jit(solution)/shard_map/ppermute | solution.py:232
  25.3 3.4 %collective-permute-done.1 = bf16[16,2048]{1,0:T(8,128)(2,1)S(1)} collective-permute-done((bf16[16,2048]{1,0:T(8,128)(2,1)S(1)}, bf16[16,2048]{1,0:T(8,128)(2,1)S(1)}, u32[]{:S(2)}, u32[]{:S(2)}) %collective-permute-start.1) | collective-permute-done | bytes 65568 | tf_op jit(solution)/shard_map/ppermute | solution.py:232
  28.7 0.0 all-to-all-done
  28.8 0.0 collective-permute-done.refs_4_
  28.8 1.8 %broadcast_in_dim.5 = bf16[16,512,128]{2,1,0:T(8,128)(2,1)} broadcast(bf16[512,128]{1,0:T(8,128)(2,1)S(1)} %pad_maximum_fusion.1), dimensions={1,2} | broadcast | bytes 2228224 | tf_op jit(solution)/shard_map/broadcast_in_dim | solution.py:34
  30.6 6.9 %all-to-all-start.1 = ((bf16[16,512,128]{2,1,0:T(8,128)(2,1)}), bf16[16,512,128]{2,1,0:T(8,128)(2,1)S(1)}, u32[]{:S(2)}, u32[]{:S(2)}) async-start(bf16[16,512,128]{2,1,0:T(8,128)(2,1)} %broadcast_in_dim.5), calls=%async_computation.1 | async-start | bytes 4194304 | tf_op jit(solution)/shard_map/all_to_all | solution.py:35
  37.4 0.0 copy-done.2
  37.5 3.8 %collective-permute-start.4 = (bf16[128,2048]{1,0:T(8,128)(2,1)S(1)}, bf16[128,2048]{1,0:T(8,128)(2,1)S(1)}, u32[]{:S(2)}, u32[]{:S(2)}) collective-permute-start(bf16[128,2048]{1,0:T(8,128)(2,1)S(1)} %copy-done.2), channel_id=1, source_target_pairs={{0,1},{1,2},{2,3},{3,4},{4,5},{5,6},{6,7},{7,64},{64,65},{65,66},{... | collective-permute-start | bytes 1572872 | tf_op jit(solution)/shard_map/ppermute | solution.py:232
  41.2 4.6 %collective-permute-start.2 = (bf16[128,4096]{1,0:T(8,128)(2,1)}, bf16[128,4096]{1,0:T(8,128)(2,1)S(1)}, u32[]{:S(2)}, u32[]{:S(2)}) collective-permute-start(bf16[128,4096]{1,0:T(8,128)(2,1)} %x0.1), channel_id=1, source_target_pairs={{0,8},{8,0},{1,9},{9,1},{2,10},{10,2},{3,11},{11,3},{4,12},{12,4},... | collective-permute-start | bytes 3145736 | tf_op jit(solution)/shard_map/ppermute | solution.py:236
  45.8 8.0 %collective-permute-start.7 = (bf16[128,2048]{1,0:T(8,128)(2,1)}, bf16[128,2048]{1,0:T(8,128)(2,1)S(1)}, u32[]{:S(2)}, u32[]{:S(2)}) collective-permute-start(bf16[128,2048]{1,0:T(8,128)(2,1)} %collective-permute-done.refs_4_), channel_id=1, source_target_pairs={{0,71},{1,0},{2,1},{3,2},{4,3},{5,4},{6,5},{7,6},{64,7},{65,64},{6... | collective-permute-start | bytes 1572872 | tf_op jit(solution)/shard_map/ppermute | solution.py:232
  53.8 2.2 %collective-permute-start.3 = (bf16[128,2048]{1,0:T(8,128)(2,1)S(1)}, bf16[128,2048]{1,0:T(8,128)(2,1)S(1)}, u32[]{:S(2)}, u32[]{:S(2)}) collective-permute-start(bf16[128,2048]{1,0:T(8,128)(2,1)S(1)} %copy-done.2), channel_id=1, source_target_pairs={{0,8},{8,0},{1,9},{9,1},{2,10},{10,2},{3,11},{11,3},{4,12},{12,4},... | collective-permute-start | bytes 1572872 | tf_op jit(solution)/shard_map/ppermute | solution.py:236
  56.0 2.1 %collective-permute-start.6 = (bf16[128,2048]{1,0:T(8,128)(2,1)}, bf16[128,2048]{1,0:T(8,128)(2,1)S(1)}, u32[]{:S(2)}, u32[]{:S(2)}) collective-permute-start(bf16[128,2048]{1,0:T(8,128)(2,1)} %collective-permute-done.refs_4_), channel_id=1, source_target_pairs={{0,8},{8,0},{1,9},{9,1},{2,10},{10,2},{3,11},{11,3},{4,12},{12,4},... | collective-permute-start | bytes 1572872 | tf_op jit(solution)/shard_map/ppermute | solution.py:236
  58.2 2.6 %collective-permute-done.4.refs_2_ = bf16[128,2048]{1,0:T(8,128)(2,1)S(1)} collective-permute-done((bf16[128,2048]{1,0:T(8,128)(2,1)S(1)}, bf16[128,2048]{1,0:T(8,128)(2,1)S(1)}, u32[]{:S(2)}, u32[]{:S(2)}) %collective-permute-start.4) | collective-permute-done | bytes 524320 | tf_op jit(solution)/shard_map/ppermute | solution.py:232
  60.7 3.2 %collective-permute-start.5 = (bf16[128,2048]{1,0:T(8,128)(2,1)S(1)}, bf16[128,2048]{1,0:T(8,128)(2,1)S(1)}, u32[]{:S(2)}, u32[]{:S(2)}) collective-permute-start(bf16[128,2048]{1,0:T(8,128)(2,1)S(1)} %collective-permute-done.4.refs_2_), channel_id=1, source_target_pairs={{0,8},{8,0},{1,9},{9,1},{2,10},{10,2},{3,11},{11,3},{4,12},{12,4},... | collective-permute-start | bytes 1572872 | tf_op jit(solution)/shard_map/ppermute | solution.py:236
  64.0 1.5 %collective-permute-done.7.refs_6_ = bf16[128,2048]{1,0:T(8,128)(2,1)S(1)} collective-permute-done((bf16[128,2048]{1,0:T(8,128)(2,1)}, bf16[128,2048]{1,0:T(8,128)(2,1)S(1)}, u32[]{:S(2)}, u32[]{:S(2)}) %collective-permute-start.7) | collective-permute-done | bytes 524320 | tf_op jit(solution)/shard_map/ppermute | solution.py:232
  65.5 2.7 %collective-permute-start.8 = (bf16[128,2048]{1,0:T(8,128)(2,1)S(1)}, bf16[128,2048]{1,0:T(8,128)(2,1)}, u32[]{:S(2)}, u32[]{:S(2)}) collective-permute-start(bf16[128,2048]{1,0:T(8,128)(2,1)S(1)} %collective-permute-done.7.refs_6_), channel_id=1, source_target_pairs={{0,8},{8,0},{1,9},{9,1},{2,10},{10,2},{3,11},{11,3},{4,12},{12,4},... | collective-permute-start | bytes 1572872 | tf_op jit(solution)/shard_map/ppermute | solution.py:236
  68.1 0.0 collective-permute-done.3.g1.refs_1_
  68.2 0.0 copy-start.3
  68.2 0.0 collective-permute-done.6.refs_5_
  68.2 0.0 copy-start.7
  68.2 0.0 collective-permute-done.5.refs_3_
  68.2 0.0 copy-start.8
  68.2 0.0 collective-permute-done.2.x1
  68.2 0.0 copy-done.5
  68.2 0.0 copy-done.6
  68.2 0.8 copy-done.7
  69.0 0.2 copy-done.8
  69.2 1.0 copy-done.4
  70.2 0.0 collective-permute-done.8.refs_7_
  70.2 0.0 all-to-all-done.1.mixed.refs_9_
  70.2 0.0 copy-done.3
  70.2 0.0 copy-start.1
  70.2 1.3 %copy-done.1 = bf16[16,512,128]{2,1,0:T(8,128)(2,1)} copy-done((bf16[16,512,128]{2,1,0:T(8,128)(2,1)}, bf16[16,512,128]{2,1,0:T(8,128)(2,1)S(1)}, u32[]{:S(2)}) %copy-start.1) | copy-done | bytes 2097176
  71.5 3.6 %low_rank.1 = bf16[16,128,128]{2,1,0:T(8,128)(2,1)} custom-call(bf16[128,4096]{1,0:T(8,128)(2,1)} %x0.1, bf16[128,4096]{1,0:T(8,128)(2,1)} %copy-done.4, bf16[128,2048]{1,0:T(8,128)(2,1)} %refs_0_.1, bf16[128,2048]{1,0:T(8,128)(2,1)} %copy-done.3, bf16[16,512,128]{2,1,0:T(8,128)(2,1)} %copy-done.1), custom_call_target="tpu_custom_call" | custom-call | flops 1048576 | bytes 65536 | tf_op jit(solution)/shard_map/low_rank/pallas_call | solution.py:94
  75.2 7.0 %all-to-all-start.2 = ((bf16[16,128,128]{2,1,0:T(8,128)(2,1)}), bf16[16,128,128]{2,1,0:T(8,128)(2,1)S(1)}, u32[]{:S(2)}, u32[]{:S(2)}) async-start(bf16[16,128,128]{2,1,0:T(8,128)(2,1)} %low_rank.1), calls=%async_computation.2 | async-start | bytes 1048576 | tf_op jit(solution)/shard_map/all_to_all | solution.py:267
  82.1 5.6 %features.1 = (bf16[256,512]{1,0:T(8,128)(2,1)}, bf16[256,512]{1,0:T(8,128)(2,1)}, bf16[256,512]{1,0:T(8,128)(2,1)}, bf16[256,512]{1,0:T(8,128)(2,1)}) custom-call(s32[1]{0:T(128)} %bitcast.1.core, bf16[128,2048]{1,0:T(8,128)(2,1)} %refs_0_.1, bf16[128,2048]{1,0:T(8,128)(2,1)} %copy-done.3, bf16[128,2048]{1,0:T(8,128)(2,1)} %copy-done.5, ...), custom_call_target="tpu_custom_call" | custom-call | flops 1048576 | bytes 65536 | tf_op jit(solution)/shard_map/features/pallas_call | solution.py:188
  87.8 1.9 %collective-permute-start.10 = (bf16[256,512]{1,0:T(8,128)(2,1)}, bf16[256,512]{1,0:T(8,128)(2,1)S(1)}, u32[]{:S(2)}, u32[]{:S(2)}) collective-permute-start(bf16[256,512]{1,0:T(8,128)(2,1)} %get-tuple-element.37), channel_id=1, source_target_pairs={{0,1},{1,2},{2,3},{3,4},{4,5},{5,6},{6,7},{7,64},{64,65},{65,66},{... | collective-permute-start | bytes 786440 | tf_op jit(solution)/shard_map/ppermute | solution.py:232
  89.7 7.1 %collective-permute-start.9 = (bf16[256,512]{1,0:T(8,128)(2,1)}, bf16[256,512]{1,0:T(8,128)(2,1)S(1)}, u32[]{:S(2)}, u32[]{:S(2)}) collective-permute-start(bf16[256,512]{1,0:T(8,128)(2,1)} %get-tuple-element.36), channel_id=1, source_target_pairs={{0,71},{1,0},{2,1},{3,2},{4,3},{5,4},{6,5},{7,6},{64,7},{65,64},{6... | collective-permute-start | bytes 786440 | tf_op jit(solution)/shard_map/ppermute | solution.py:232
  96.8 0.9 slice_bitcast_fusion.3
  97.7 0.0 all-to-all-done.2.came
  97.7 0.8 to_line.1
  98.5 0.2 copy-done.12
  98.6 1.9 %collective-permute-start.11 = (bf16[256,512]{1,0:T(8,128)(2,1)S(1)}, bf16[256,512]{1,0:T(8,128)(2,1)S(1)}, u32[]{:S(2)}, u32[]{:S(2)}) collective-permute-start(bf16[256,512]{1,0:T(8,128)(2,1)S(1)} %copy-done.12), channel_id=1, source_target_pairs={{0,2},{1,3},{2,4},{3,5},{4,6},{5,7},{6,64},{7,65},{64,66},{65,67},... | collective-permute-start | bytes 786440 | tf_op jit(solution)/shard_map/ppermute | solution.py:232
  100.5 0.0 collective-permute-done.10.down
  100.6 8.2 %all-to-all-start.3 = ((bf16[32,32,128]{2,1,0:T(8,128)(2,1)}), bf16[32,32,128]{2,1,0:T(8,128)(2,1)S(1)}, u32[]{:S(2)}, u32[]{:S(2)}) async-start(bf16[32,32,128]{2,1,0:T(8,128)(2,1)} %to_line.1), calls=%async_computation.3 | async-start | bytes 524288 | tf_op jit(solution)/shard_map/all_to_all | solution.py:273
  108.8 0.0 collective-permute-done.9.up
  108.8 6.6 %collective-permute-done.11.down2 = bf16[256,512]{1,0:T(8,128)(2,1)S(1)} collective-permute-done((bf16[256,512]{1,0:T(8,128)(2,1)S(1)}, bf16[256,512]{1,0:T(8,128)(2,1)S(1)}, u32[]{:S(2)}, u32[]{:S(2)}) %collective-permute-start.11) | collective-permute-done | bytes 262176 | tf_op jit(solution)/shard_map/ppermute | solution.py:232
  115.5 0.1 pad_maximum_fusion
  115.6 5.9 %collective-permute-start.12 = (bf16[4,128,512]{2,1,0:T(8,128)(2,1)S(1)}, bf16[4,128,512]{2,1,0:T(8,128)(2,1)S(1)}, u32[]{:S(2)}, u32[]{:S(2)}) collective-permute-start(bf16[4,128,512]{2,1,0:T(8,128)(2,1)S(1)} %pad_maximum_fusion), channel_id=1, source_target_pairs={{0,8},{8,0},{1,9},{9,1},{2,10},{10,2},{3,11},{11,3},{4,12},{12,4},... | collective-permute-start | bytes 1572872 | tf_op jit(solution)/shard_map/ppermute | solution.py:236
  121.5 0.1 pad_add_fusion.where
  121.6 1.4 %collective-permute-done.12.crossed = bf16[4,128,512]{2,1,0:T(8,128)(2,1)S(1)} collective-permute-done((bf16[4,128,512]{2,1,0:T(8,128)(2,1)S(1)}, bf16[4,128,512]{2,1,0:T(8,128)(2,1)S(1)}, u32[]{:S(2)}, u32[]{:S(2)}) %collective-permute-start.12) | collective-permute-done | bytes 524320 | tf_op jit(solution)/shard_map/ppermute | solution.py:236
  123.0 0.0 copy-done
  123.0 1.6 %assemble.1 = bf16[128,4096]{1,0:T(8,128)(2,1)} custom-call(s32[2]{0:T(128)S(1)} %pad_add_fusion.where, bf16[256,512]{1,0:T(8,128)(2,1)S(1)} %copy-done, bf16[256,512]{1,0:T(8,128)(2,1)S(1)} %collective-permute-done.9.up, bf16[256,512]{1,0:T(8,128)(2,1)S(1)} %collective-permute-done.10.down, bf16[256,512]{1,0:T(8,128)(2,1)S(1)} %collective-permute-done.11.down2, ...), custom_call_target="tpu_custom_call" | custom-call | bytes 65536 | tf_op jit(solution)/shard_map/assemble/pallas_call | solution.py:221
  124.7 5.6 %all-to-all-done.3.parts = bf16[32,32,128]{2,1,0:T(8,128)(2,1)S(1)} async-done(((bf16[32,32,128]{2,1,0:T(8,128)(2,1)}), bf16[32,32,128]{2,1,0:T(8,128)(2,1)S(1)}, u32[]{:S(2)}, u32[]{:S(2)}) %all-to-all-start.3) | async-done | bytes 262176 | tf_op jit(solution)/shard_map/all_to_all | solution.py:273
  130.3 0.1 copy.12
  130.4 0.1 reshape.64
  130.6 0.8 convert_reduce_fusion
  131.4 0.1 reshape.65
  131.5 0.8 convolution_bitcast_fusion
  (19 shorter events, 0.1 us)
Async XLA Ops:
  0.6 28.1 %collective-permute-start = (bf16[128,2048]{1,0:T(8,128)(2,1)}, bf16[128,2048]{1,0:T(8,128)(2,1)}, u32[]{:S(2)}, u32[]{:S(2)}) collective-permute-start(bf16[128,2048]{1,0:T(8,128)(2,1)} %refs_0_.1), channel_id=1, source_target_pairs={{0,71},{1,0},{2,1},{3,2},{4,3},{5,4},{6,5},{7,6},{64,7},{65,64},{6... | collective-permute-start | bytes 1572872 | tf_op jit(solution)/shard_map/ppermute | solution.py:232
  13.9 14.8 %all-to-all-start = ((bf16[8,32,128]{2,1,0:T(8,128)(2,1)}), bf16[8,32,128]{2,1,0:T(8,128)(2,1)S(1)}, u32[]{:S(2)}, u32[]{:S(2)}) async-start(bf16[8,32,128]{2,1,0:T(8,128)(2,1)} %broadcast_in_dim.4), calls=%async_computation | async-start | bytes 131072 | tf_op jit(solution)/shard_map/all_to_all | solution.py:35
  18.2 10.5 %collective-permute-start.1 = (bf16[16,2048]{1,0:T(8,128)(2,1)S(1)}, bf16[16,2048]{1,0:T(8,128)(2,1)S(1)}, u32[]{:S(2)}, u32[]{:S(2)}) collective-permute-start(bf16[16,2048]{1,0:T(8,128)(2,1)S(1)} %constant_dynamic-slice_fusion), channel_id=1, source_target_pairs={{0,4},{1,5},{2,6},{3,7},{4,64},{5,65},{6,66},{7,67},{64,68},{65,69... | collective-permute-start | bytes 196616 | tf_op jit(solution)/shard_map/ppermute | solution.py:232
  30.5 6.9 %copy-start.2 = (bf16[128,2048]{1,0:T(8,128)(2,1)S(1)}, bf16[128,2048]{1,0:T(8,128)(2,1)}, u32[]{:S(2)}) copy-start(bf16[128,2048]{1,0:T(8,128)(2,1)} %refs_0_.1) | copy-start | bytes 1572868
  30.6 39.6 %all-to-all-start.1 = ((bf16[16,512,128]{2,1,0:T(8,128)(2,1)}), bf16[16,512,128]{2,1,0:T(8,128)(2,1)S(1)}, u32[]{:S(2)}, u32[]{:S(2)}) async-start(bf16[16,512,128]{2,1,0:T(8,128)(2,1)} %broadcast_in_dim.5), calls=%async_computation.1 | async-start | bytes 4194304 | tf_op jit(solution)/shard_map/all_to_all | solution.py:35
  37.5 23.3 %collective-permute-start.4 = (bf16[128,2048]{1,0:T(8,128)(2,1)S(1)}, bf16[128,2048]{1,0:T(8,128)(2,1)S(1)}, u32[]{:S(2)}, u32[]{:S(2)}) collective-permute-start(bf16[128,2048]{1,0:T(8,128)(2,1)S(1)} %copy-done.2), channel_id=1, source_target_pairs={{0,1},{1,2},{2,3},{3,4},{4,5},{5,6},{6,7},{7,64},{64,65},{65,66},{... | collective-permute-start | bytes 1572872 | tf_op jit(solution)/shard_map/ppermute | solution.py:232
  41.2 27.0 %collective-permute-start.2 = (bf16[128,4096]{1,0:T(8,128)(2,1)}, bf16[128,4096]{1,0:T(8,128)(2,1)S(1)}, u32[]{:S(2)}, u32[]{:S(2)}) collective-permute-start(bf16[128,4096]{1,0:T(8,128)(2,1)} %x0.1), channel_id=1, source_target_pairs={{0,8},{8,0},{1,9},{9,1},{2,10},{10,2},{3,11},{11,3},{4,12},{12,4},... | collective-permute-start | bytes 3145736 | tf_op jit(solution)/shard_map/ppermute | solution.py:236
  45.8 19.6 %collective-permute-start.7 = (bf16[128,2048]{1,0:T(8,128)(2,1)}, bf16[128,2048]{1,0:T(8,128)(2,1)S(1)}, u32[]{:S(2)}, u32[]{:S(2)}) collective-permute-start(bf16[128,2048]{1,0:T(8,128)(2,1)} %collective-permute-done.refs_4_), channel_id=1, source_target_pairs={{0,71},{1,0},{2,1},{3,2},{4,3},{5,4},{6,5},{7,6},{64,7},{65,64},{6... | collective-permute-start | bytes 1572872 | tf_op jit(solution)/shard_map/ppermute | solution.py:232
  53.8 14.3 %collective-permute-start.3 = (bf16[128,2048]{1,0:T(8,128)(2,1)S(1)}, bf16[128,2048]{1,0:T(8,128)(2,1)S(1)}, u32[]{:S(2)}, u32[]{:S(2)}) collective-permute-start(bf16[128,2048]{1,0:T(8,128)(2,1)S(1)} %copy-done.2), channel_id=1, source_target_pairs={{0,8},{8,0},{1,9},{9,1},{2,10},{10,2},{3,11},{11,3},{4,12},{12,4},... | collective-permute-start | bytes 1572872 | tf_op jit(solution)/shard_map/ppermute | solution.py:236
  56.0 12.2 %collective-permute-start.6 = (bf16[128,2048]{1,0:T(8,128)(2,1)}, bf16[128,2048]{1,0:T(8,128)(2,1)S(1)}, u32[]{:S(2)}, u32[]{:S(2)}) collective-permute-start(bf16[128,2048]{1,0:T(8,128)(2,1)} %collective-permute-done.refs_4_), channel_id=1, source_target_pairs={{0,8},{8,0},{1,9},{9,1},{2,10},{10,2},{3,11},{11,3},{4,12},{12,4},... | collective-permute-start | bytes 1572872 | tf_op jit(solution)/shard_map/ppermute | solution.py:236
  60.7 7.5 %copy-start.5 = (bf16[128,2048]{1,0:T(8,128)(2,1)}, bf16[128,2048]{1,0:T(8,128)(2,1)S(1)}, u32[]{:S(2)}) copy-start(bf16[128,2048]{1,0:T(8,128)(2,1)S(1)} %collective-permute-done.4.refs_2_) | copy-start | bytes 1572868
  60.7 7.5 %collective-permute-start.5 = (bf16[128,2048]{1,0:T(8,128)(2,1)S(1)}, bf16[128,2048]{1,0:T(8,128)(2,1)S(1)}, u32[]{:S(2)}, u32[]{:S(2)}) collective-permute-start(bf16[128,2048]{1,0:T(8,128)(2,1)S(1)} %collective-permute-done.4.refs_2_), channel_id=1, source_target_pairs={{0,8},{8,0},{1,9},{9,1},{2,10},{10,2},{3,11},{11,3},{4,12},{12,4},... | collective-permute-start | bytes 1572872 | tf_op jit(solution)/shard_map/ppermute | solution.py:236
  65.4 2.8 %copy-start.6 = (bf16[128,2048]{1,0:T(8,128)(2,1)}, bf16[128,2048]{1,0:T(8,128)(2,1)S(1)}, u32[]{:S(2)}) copy-start(bf16[128,2048]{1,0:T(8,128)(2,1)S(1)} %collective-permute-done.7.refs_6_) | copy-start | bytes 1572868
  65.5 4.7 %collective-permute-start.8 = (bf16[128,2048]{1,0:T(8,128)(2,1)S(1)}, bf16[128,2048]{1,0:T(8,128)(2,1)}, u32[]{:S(2)}, u32[]{:S(2)}) collective-permute-start(bf16[128,2048]{1,0:T(8,128)(2,1)S(1)} %collective-permute-done.7.refs_6_), channel_id=1, source_target_pairs={{0,8},{8,0},{1,9},{9,1},{2,10},{10,2},{3,11},{11,3},{4,12},{12,4},... | collective-permute-start | bytes 1572872 | tf_op jit(solution)/shard_map/ppermute | solution.py:236
  68.2 2.0 %copy-start.3 = (bf16[128,2048]{1,0:T(8,128)(2,1)}, bf16[128,2048]{1,0:T(8,128)(2,1)S(1)}, u32[]{:S(2)}) copy-start(bf16[128,2048]{1,0:T(8,128)(2,1)S(1)} %collective-permute-done.3.g1.refs_1_) | copy-start | bytes 1572868
  68.2 0.8 copy-start.7
  68.2 1.0 copy-start.8
  69.2 1.0 copy-start.4
  70.2 1.4 %copy-start.1 = (bf16[16,512,128]{2,1,0:T(8,128)(2,1)}, bf16[16,512,128]{2,1,0:T(8,128)(2,1)S(1)}, u32[]{:S(2)}) copy-start(bf16[16,512,128]{2,1,0:T(8,128)(2,1)S(1)} %all-to-all-done.1.mixed.refs_9_) | copy-start | bytes 6291460
  75.2 22.5 %all-to-all-start.2 = ((bf16[16,128,128]{2,1,0:T(8,128)(2,1)}), bf16[16,128,128]{2,1,0:T(8,128)(2,1)S(1)}, u32[]{:S(2)}, u32[]{:S(2)}) async-start(bf16[16,128,128]{2,1,0:T(8,128)(2,1)} %low_rank.1), calls=%async_computation.2 | async-start | bytes 1048576 | tf_op jit(solution)/shard_map/all_to_all | solution.py:267
  87.8 12.8 %collective-permute-start.10 = (bf16[256,512]{1,0:T(8,128)(2,1)}, bf16[256,512]{1,0:T(8,128)(2,1)S(1)}, u32[]{:S(2)}, u32[]{:S(2)}) collective-permute-start(bf16[256,512]{1,0:T(8,128)(2,1)} %get-tuple-element.37), channel_id=1, source_target_pairs={{0,1},{1,2},{2,3},{3,4},{4,5},{5,6},{6,7},{7,64},{64,65},{65,66},{... | collective-permute-start | bytes 786440 | tf_op jit(solution)/shard_map/ppermute | solution.py:232
  89.7 19.1 %collective-permute-start.9 = (bf16[256,512]{1,0:T(8,128)(2,1)}, bf16[256,512]{1,0:T(8,128)(2,1)S(1)}, u32[]{:S(2)}, u32[]{:S(2)}) collective-permute-start(bf16[256,512]{1,0:T(8,128)(2,1)} %get-tuple-element.36), channel_id=1, source_target_pairs={{0,71},{1,0},{2,1},{3,2},{4,3},{5,4},{6,5},{7,6},{64,7},{65,64},{6... | collective-permute-start | bytes 786440 | tf_op jit(solution)/shard_map/ppermute | solution.py:232
  97.7 1.0 copy-start.12
  98.5 24.5 %copy-start = (bf16[256,512]{1,0:T(8,128)(2,1)S(1)}, bf16[256,512]{1,0:T(8,128)(2,1)}, u32[]{:S(2)}) copy-start(bf16[256,512]{1,0:T(8,128)(2,1)} %get-tuple-element.35.near) | copy-start | bytes 786436
  98.6 16.9 %collective-permute-start.11 = (bf16[256,512]{1,0:T(8,128)(2,1)S(1)}, bf16[256,512]{1,0:T(8,128)(2,1)S(1)}, u32[]{:S(2)}, u32[]{:S(2)}) collective-permute-start(bf16[256,512]{1,0:T(8,128)(2,1)S(1)} %copy-done.12), channel_id=1, source_target_pairs={{0,2},{1,3},{2,4},{3,5},{4,6},{5,7},{6,64},{7,65},{64,66},{65,67},... | collective-permute-start | bytes 786440 | tf_op jit(solution)/shard_map/ppermute | solution.py:232
  100.6 29.7 %all-to-all-start.3 = ((bf16[32,32,128]{2,1,0:T(8,128)(2,1)}), bf16[32,32,128]{2,1,0:T(8,128)(2,1)S(1)}, u32[]{:S(2)}, u32[]{:S(2)}) async-start(bf16[32,32,128]{2,1,0:T(8,128)(2,1)} %to_line.1), calls=%async_computation.3 | async-start | bytes 524288 | tf_op jit(solution)/shard_map/all_to_all | solution.py:273
  115.6 7.4 %collective-permute-start.12 = (bf16[4,128,512]{2,1,0:T(8,128)(2,1)S(1)}, bf16[4,128,512]{2,1,0:T(8,128)(2,1)S(1)}, u32[]{:S(2)}, u32[]{:S(2)}) collective-permute-start(bf16[4,128,512]{2,1,0:T(8,128)(2,1)S(1)} %pad_maximum_fusion), channel_id=1, source_target_pairs={{0,8},{8,0},{1,9},{9,1},{2,10},{10,2},{3,11},{11,3},{4,12},{12,4},... | collective-permute-start | bytes 1572872 | tf_op jit(solution)/shard_map/ppermute | solution.py:236
  124.6 5.9 %copy-start.10 = (f32[1,8192]{1,0:T(1,128)S(1)}, f32[1,8192]{1,0:T(1,128)}, u32[]{:S(2)}) copy-start(f32[1,8192]{1,0:T(1,128)} %param.11) | copy-start | bytes 98308
  124.6 5.9 %copy-start.11 = (f32[1,8192]{1,0:T(1,128)S(1)}, f32[1,8192]{1,0:T(1,128)}, u32[]{:S(2)}) copy-start(f32[1,8192]{1,0:T(1,128)} %param.10) | copy-start | bytes 98308
  124.6 6.8 %copy-start.9 = (bf16[512,256]{1,0:T(8,128)(2,1)S(1)}, bf16[512,256]{1,0:T(8,128)(2,1)}, u32[]{:S(2)}) copy-start(bf16[512,256]{1,0:T(8,128)(2,1)} %param.9) | copy-start | bytes 786436

commit v6 on v5

--- a/solution.py
+++ b/solution.py
@@ -269,9 +269,11 @@
         core, [out_grad, grad_c] + far, weight, mixed
     )
     line_parts = to_line(came)
-    line_parts, o_after2 = lax.optimization_barrier((line_parts, o_after2))
     low = total_of(lax.all_to_all(line_parts, COLUMN, 0, 0, tiled=True))
     cols = out_grad.shape[1] // 64
+    pieces = [near, ring(o_before, -1), ring(o_after, 1), ring(o_after2, 2)]
+    crossed = swap_cores(jnp.stack([v[n:] for v in pieces]))
+    crossed, low = lax.optimization_barrier((crossed, low))
     flat_grad = low.transpose(0, 2, 1).reshape(1, 2 * half * cols)
     new_first = beta_one * first_moment + (1.0 - beta_one) * flat_grad
     new_second = beta_two * second_moment + (1.0 - beta_two) * flat_grad * flat_grad
@@ -281,8 +283,6 @@
     direction = direction.reshape(2 * half, cols)
     update = jnp.dot(proj_basis, direction, preferred_element_type=F32)
 
-    pieces = [near, ring(o_before, -1), ring(o_after, 1), ring(o_after2, 2)]
-    crossed = swap_cores(jnp.stack([v[n:] for v in pieces]))
     input_grad = assemble(jnp.stack([line, core]), pieces, crossed)
     return (input_grad, new_first, new_second, update)
 

time: 134 us -> 133 us (level)
  waiting for transfers between devices: 21.1 us -> 25.9 us
  starting transfers between devices: 87.9 us -> 84.3 us
    all_to_all x1, waiting for transfers between devices: 5.63 us -> 14.4 us  [on_device(): low = total_of(lax.all_to_all(line_parts, COLUMN, 0, 0, tiled=True))]
    ppermute x6, starting transfers between devices: 20.7 us -> 17.5 us  [swap_cores(): return lax.ppermute(value, 'c', [(0, 1), (1, 0)])]
    ppermute x7, waiting for transfers between devices: 14.1 us -> 11.5 us  [ring(): return lax.ppermute(value, RING, [(i, (i + step) % 16) for i in range(16)])]
    ppermute x6, waiting for transfers between devices: 1.44 us -> 0.02 us  [swap_cores(): return lax.ppermute(value, 'c', [(0, 1), (1, 0)])]
    unnamed x27 -> x25, local copies, waits for them, and re-layouts: 3.49 us -> 3.34 us
  transfers between devices with their start and end apart: 17 -> 17, of which waited for: 6 -> 5; matrix products, arithmetic and copies ran while one was open for 3% -> 2% of each run, Pallas kernels for 6% -> 5%
where the time goes in v6:
time: 133 us; the launch traced here: 132 us
  starting transfers between devices  84.3 us (63%)
  waiting for transfers between devices  25.9 us (19%)
  Pallas kernels  11.7 us (9%)
  local copies, waits for them, and re-layouts  7.67 us (6%)
    ppermute x7, starting transfers between devices, ring(): return lax.ppermute(value, RING, [(i, (i + step) % 16) for i in range(16)])  41.9 us
    ppermute x6, starting transfers between devices, swap_cores(): return lax.ppermute(value, 'c', [(0, 1), (1, 0)])  17.5 us
    all_to_all x1, waiting for transfers between devices, on_device(): low = total_of(lax.all_to_all(line_parts, COLUMN, 0, 0, tiled=True))  14.4 us
    ppermute x7, waiting for transfers between devices, ring(): return lax.ppermute(value, RING, [(i, (i + step) % 16) for i in range(16)])  11.5 us
    all_to_all x2, starting transfers between devices, spread(): return lax.all_to_all(sent, axes, 0, 0, tiled=True)  10.2 us
    all_to_all x1, starting transfers between devices, on_device(): low = total_of(lax.all_to_all(line_parts, COLUMN, 0, 0, tiled=True))  7.74 us
    all_to_all x1, starting transfers between devices, on_device(): came = lax.all_to_all(low, PLANE, 0, 0, tiled=True)  6.94 us
    pallas_call x1, Pallas kernels, features(): pl.pallas_call(functools.partial(feature_kernel, count), in_specs=[pl.Blo...  5.63 us
  transfers between devices with their start and end apart: 17, of which 5 were waited for; matrix products, arithmetic and copies ran while one was open for 2% of the time, Pallas kernels for 5%

profile of v6, /device:TPU:1, one launch (start us, length us, event | category | flops | bytes accessed | tf_op | source)
XLA Modules:
  0.0 132.4 jit_solution(14307167316154704714)
XLA Ops:
  0.6 12.0 %collective-permute-start = (bf16[128,2048]{1,0:T(8,128)(2,1)}, bf16[128,2048]{1,0:T(8,128)(2,1)}, u32[]{:S(2)}, u32[]{:S(2)}) collective-permute-start(bf16[128,2048]{1,0:T(8,128)(2,1)} %refs_0_.1), channel_id=1, source_target_pairs={{0,71},{1,0},{2,1},{3,2},{4,3},{5,4},{6,5},{7,6},{64,7},{65,64},{6... | collective-permute-start | bytes 1572872 | tf_op jit(solution)/shard_map/ppermute | solution.py:232
  12.6 0.7 dynamic_slice.6
  13.3 0.6 broadcast_in_dim.4
  13.9 3.4 %all-to-all-start = ((bf16[8,32,128]{2,1,0:T(8,128)(2,1)}), bf16[8,32,128]{2,1,0:T(8,128)(2,1)S(1)}, u32[]{:S(2)}, u32[]{:S(2)}) async-start(bf16[8,32,128]{2,1,0:T(8,128)(2,1)} %broadcast_in_dim.4), calls=%async_computation | async-start | bytes 131072 | tf_op jit(solution)/shard_map/all_to_all | solution.py:35
  17.3 0.8 constant_dynamic-slice_fusion
  18.2 7.2 %collective-permute-start.1 = (bf16[16,2048]{1,0:T(8,128)(2,1)S(1)}, bf16[16,2048]{1,0:T(8,128)(2,1)S(1)}, u32[]{:S(2)}, u32[]{:S(2)}) collective-permute-start(bf16[16,2048]{1,0:T(8,128)(2,1)S(1)} %constant_dynamic-slice_fusion), channel_id=1, source_target_pairs={{0,4},{1,5},{2,6},{3,7},{4,64},{5,65},{6,66},{7,67},{64,68},{65,69... | collective-permute-start | bytes 196616 | tf_op jit(solution)/shard_map/ppermute | solution.py:232
  25.3 3.4 %collective-permute-done.1 = bf16[16,2048]{1,0:T(8,128)(2,1)S(1)} collective-permute-done((bf16[16,2048]{1,0:T(8,128)(2,1)S(1)}, bf16[16,2048]{1,0:T(8,128)(2,1)S(1)}, u32[]{:S(2)}, u32[]{:S(2)}) %collective-permute-start.1) | collective-permute-done | bytes 65568 | tf_op jit(solution)/shard_map/ppermute | solution.py:232
  28.7 0.0 all-to-all-done
  28.8 0.0 collective-permute-done.refs_4_
  28.8 1.8 %broadcast_in_dim.5 = bf16[16,512,128]{2,1,0:T(8,128)(2,1)} broadcast(bf16[512,128]{1,0:T(8,128)(2,1)S(1)} %pad_maximum_fusion.1), dimensions={1,2} | broadcast | bytes 2228224 | tf_op jit(solution)/shard_map/broadcast_in_dim | solution.py:34
  30.6 6.9 %all-to-all-start.1 = ((bf16[16,512,128]{2,1,0:T(8,128)(2,1)}), bf16[16,512,128]{2,1,0:T(8,128)(2,1)S(1)}, u32[]{:S(2)}, u32[]{:S(2)}) async-start(bf16[16,512,128]{2,1,0:T(8,128)(2,1)} %broadcast_in_dim.5), calls=%async_computation.1 | async-start | bytes 4194304 | tf_op jit(solution)/shard_map/all_to_all | solution.py:35
  37.5 0.0 copy-done.2
  37.5 3.8 %collective-permute-start.4 = (bf16[128,2048]{1,0:T(8,128)(2,1)S(1)}, bf16[128,2048]{1,0:T(8,128)(2,1)S(1)}, u32[]{:S(2)}, u32[]{:S(2)}) collective-permute-start(bf16[128,2048]{1,0:T(8,128)(2,1)S(1)} %copy-done.2), channel_id=1, source_target_pairs={{0,1},{1,2},{2,3},{3,4},{4,5},{5,6},{6,7},{7,64},{64,65},{65,66},{... | collective-permute-start | bytes 1572872 | tf_op jit(solution)/shard_map/ppermute | solution.py:232
  41.3 4.6 %collective-permute-start.2 = (bf16[128,4096]{1,0:T(8,128)(2,1)}, bf16[128,4096]{1,0:T(8,128)(2,1)S(1)}, u32[]{:S(2)}, u32[]{:S(2)}) collective-permute-start(bf16[128,4096]{1,0:T(8,128)(2,1)} %x0.1), channel_id=1, source_target_pairs={{0,8},{8,0},{1,9},{9,1},{2,10},{10,2},{3,11},{11,3},{4,12},{12,4},... | collective-permute-start | bytes 3145736 | tf_op jit(solution)/shard_map/ppermute | solution.py:236
  45.8 8.0 %collective-permute-start.7 = (bf16[128,2048]{1,0:T(8,128)(2,1)}, bf16[128,2048]{1,0:T(8,128)(2,1)S(1)}, u32[]{:S(2)}, u32[]{:S(2)}) collective-permute-start(bf16[128,2048]{1,0:T(8,128)(2,1)} %collective-permute-done.refs_4_), channel_id=1, source_target_pairs={{0,71},{1,0},{2,1},{3,2},{4,3},{5,4},{6,5},{7,6},{64,7},{65,64},{6... | collective-permute-start | bytes 1572872 | tf_op jit(solution)/shard_map/ppermute | solution.py:232
  53.8 2.2 %collective-permute-start.3 = (bf16[128,2048]{1,0:T(8,128)(2,1)S(1)}, bf16[128,2048]{1,0:T(8,128)(2,1)S(1)}, u32[]{:S(2)}, u32[]{:S(2)}) collective-permute-start(bf16[128,2048]{1,0:T(8,128)(2,1)S(1)} %copy-done.2), channel_id=1, source_target_pairs={{0,8},{8,0},{1,9},{9,1},{2,10},{10,2},{3,11},{11,3},{4,12},{12,4},... | collective-permute-start | bytes 1572872 | tf_op jit(solution)/shard_map/ppermute | solution.py:236
  56.0 2.1 %collective-permute-start.6 = (bf16[128,2048]{1,0:T(8,128)(2,1)}, bf16[128,2048]{1,0:T(8,128)(2,1)S(1)}, u32[]{:S(2)}, u32[]{:S(2)}) collective-permute-start(bf16[128,2048]{1,0:T(8,128)(2,1)} %collective-permute-done.refs_4_), channel_id=1, source_target_pairs={{0,8},{8,0},{1,9},{9,1},{2,10},{10,2},{3,11},{11,3},{4,12},{12,4},... | collective-permute-start | bytes 1572872 | tf_op jit(solution)/shard_map/ppermute | solution.py:236
  58.2 2.6 %collective-permute-done.4.refs_2_ = bf16[128,2048]{1,0:T(8,128)(2,1)S(1)} collective-permute-done((bf16[128,2048]{1,0:T(8,128)(2,1)S(1)}, bf16[128,2048]{1,0:T(8,128)(2,1)S(1)}, u32[]{:S(2)}, u32[]{:S(2)}) %collective-permute-start.4) | collective-permute-done | bytes 524320 | tf_op jit(solution)/shard_map/ppermute | solution.py:232
  60.7 3.2 %collective-permute-start.5 = (bf16[128,2048]{1,0:T(8,128)(2,1)S(1)}, bf16[128,2048]{1,0:T(8,128)(2,1)S(1)}, u32[]{:S(2)}, u32[]{:S(2)}) collective-permute-start(bf16[128,2048]{1,0:T(8,128)(2,1)S(1)} %collective-permute-done.4.refs_2_), channel_id=1, source_target_pairs={{0,8},{8,0},{1,9},{9,1},{2,10},{10,2},{3,11},{11,3},{4,12},{12,4},... | collective-permute-start | bytes 1572872 | tf_op jit(solution)/shard_map/ppermute | solution.py:236
  64.0 1.5 %collective-permute-done.7.refs_6_ = bf16[128,2048]{1,0:T(8,128)(2,1)S(1)} collective-permute-done((bf16[128,2048]{1,0:T(8,128)(2,1)}, bf16[128,2048]{1,0:T(8,128)(2,1)S(1)}, u32[]{:S(2)}, u32[]{:S(2)}) %collective-permute-start.7) | collective-permute-done | bytes 524320 | tf_op jit(solution)/shard_map/ppermute | solution.py:232
  65.5 2.7 %collective-permute-start.8 = (bf16[128,2048]{1,0:T(8,128)(2,1)S(1)}, bf16[128,2048]{1,0:T(8,128)(2,1)}, u32[]{:S(2)}, u32[]{:S(2)}) collective-permute-start(bf16[128,2048]{1,0:T(8,128)(2,1)S(1)} %collective-permute-done.7.refs_6_), channel_id=1, source_target_pairs={{0,8},{8,0},{1,9},{9,1},{2,10},{10,2},{3,11},{11,3},{4,12},{12,4},... | collective-permute-start | bytes 1572872 | tf_op jit(solution)/shard_map/ppermute | solution.py:236
  68.2 0.0 collective-permute-done.3.g1.refs_1_
  68.2 0.0 copy-start.3
  68.2 0.0 collective-permute-done.6.refs_5_
  68.2 0.0 copy-start.7
  68.2 0.0 collective-permute-done.5.refs_3_
  68.2 0.0 copy-start.8
  68.2 0.0 collective-permute-done.2.x1
  68.2 0.0 copy-done.5
  68.2 0.0 copy-done.6
  68.2 0.8 copy-done.7
  69.0 0.2 copy-done.8
  69.2 1.0 copy-done.4
  70.2 0.0 collective-permute-done.8.refs_7_
  70.2 0.0 all-to-all-done.1.mixed.refs_9_
  70.2 0.0 copy-done.3
  70.2 1.4 %copy-done.1 = bf16[16,512,128]{2,1,0:T(8,128)(2,1)} copy-done((bf16[16,512,128]{2,1,0:T(8,128)(2,1)}, bf16[16,512,128]{2,1,0:T(8,128)(2,1)S(1)}, u32[]{:S(2)}) %copy-start.1) | copy-done | bytes 2097176
  71.6 3.6 %low_rank.1 = bf16[16,128,128]{2,1,0:T(8,128)(2,1)} custom-call(bf16[128,4096]{1,0:T(8,128)(2,1)} %x0.1, bf16[128,4096]{1,0:T(8,128)(2,1)} %copy-done.4, bf16[128,2048]{1,0:T(8,128)(2,1)} %refs_0_.1, bf16[128,2048]{1,0:T(8,128)(2,1)} %copy-done.3, bf16[16,512,128]{2,1,0:T(8,128)(2,1)} %copy-done.1), custom_call_target="tpu_custom_call" | custom-call | flops 1048576 | bytes 65536 | tf_op jit(solution)/shard_map/low_rank/pallas_call | solution.py:94
  75.2 6.9 %all-to-all-start.2 = ((bf16[16,128,128]{2,1,0:T(8,128)(2,1)}), bf16[16,128,128]{2,1,0:T(8,128)(2,1)S(1)}, u32[]{:S(2)}, u32[]{:S(2)}) async-start(bf16[16,128,128]{2,1,0:T(8,128)(2,1)} %low_rank.1), calls=%async_computation.2 | async-start | bytes 1048576 | tf_op jit(solution)/shard_map/all_to_all | solution.py:267
  82.1 0.1 pad_add_fusion.where
  82.2 5.6 %features.1 = (bf16[256,512]{1,0:T(8,128)(2,1)}, bf16[256,512]{1,0:T(8,128)(2,1)}, bf16[256,512]{1,0:T(8,128)(2,1)}, bf16[256,512]{1,0:T(8,128)(2,1)}) custom-call(s32[1]{0:T(128)} %bitcast.1.core, bf16[128,2048]{1,0:T(8,128)(2,1)} %refs_0_.1, bf16[128,2048]{1,0:T(8,128)(2,1)} %copy-done.3, bf16[128,2048]{1,0:T(8,128)(2,1)} %copy-done.5, ...), custom_call_target="tpu_custom_call" | custom-call | flops 1048576 | bytes 65536 | tf_op jit(solution)/shard_map/features/pallas_call | solution.py:188
  87.8 2.5 %collective-permute-start.11 = (bf16[256,512]{1,0:T(8,128)(2,1)}, bf16[256,512]{1,0:T(8,128)(2,1)S(1)}, u32[]{:S(2)}, u32[]{:S(2)}) collective-permute-start(bf16[256,512]{1,0:T(8,128)(2,1)} %get-tuple-element.38), channel_id=1, source_target_pairs={{0,2},{1,3},{2,4},{3,5},{4,6},{5,7},{6,64},{7,65},{64,66},{65,67},... | collective-permute-start | bytes 786440 | tf_op jit(solution)/shard_map/ppermute | solution.py:232
  90.4 4.7 %collective-permute-start.10 = (bf16[256,512]{1,0:T(8,128)(2,1)}, bf16[256,512]{1,0:T(8,128)(2,1)S(1)}, u32[]{:S(2)}, u32[]{:S(2)}) collective-permute-start(bf16[256,512]{1,0:T(8,128)(2,1)} %get-tuple-element.37), channel_id=1, source_target_pairs={{0,1},{1,2},{2,3},{3,4},{4,5},{5,6},{6,7},{7,64},{64,65},{65,66},{... | collective-permute-start | bytes 786440 | tf_op jit(solution)/shard_map/ppermute | solution.py:232
  95.1 0.0 copy-start
  95.1 3.8 %collective-permute-start.9 = (bf16[256,512]{1,0:T(8,128)(2,1)}, bf16[256,512]{1,0:T(8,128)(2,1)S(1)}, u32[]{:S(2)}, u32[]{:S(2)}) collective-permute-start(bf16[256,512]{1,0:T(8,128)(2,1)} %get-tuple-element.36), channel_id=1, source_target_pairs={{0,71},{1,0},{2,1},{3,2},{4,3},{5,4},{6,5},{7,6},{64,7},{65,64},{6... | collective-permute-start | bytes 786440 | tf_op jit(solution)/shard_map/ppermute | solution.py:232
  98.9 0.0 all-to-all-done.2.came
  98.9 0.8 to_line.1
  99.7 7.7 %all-to-all-start.3 = ((bf16[32,32,128]{2,1,0:T(8,128)(2,1)}), bf16[32,32,128]{2,1,0:T(8,128)(2,1)S(1)}, u32[]{:S(2)}, u32[]{:S(2)}) async-start(bf16[32,32,128]{2,1,0:T(8,128)(2,1)} %to_line.1), calls=%async_computation.3 | async-start | bytes 524288 | tf_op jit(solution)/shard_map/all_to_all | solution.py:272
  107.5 0.0 collective-permute-done.11.down2
  107.5 4.1 %collective-permute-done.10.down = bf16[256,512]{1,0:T(8,128)(2,1)S(1)} collective-permute-done((bf16[256,512]{1,0:T(8,128)(2,1)}, bf16[256,512]{1,0:T(8,128)(2,1)S(1)}, u32[]{:S(2)}, u32[]{:S(2)}) %collective-permute-start.10) | collective-permute-done | bytes 262176 | tf_op jit(solution)/shard_map/ppermute | solution.py:232
  111.6 0.0 collective-permute-done.9.up
  111.6 0.1 pad_maximum_fusion
  111.7 0.0 copy-start.10
  111.7 0.0 copy-start.11
  111.7 0.0 copy-start.9
  111.7 2.6 %collective-permute-start.12 = (bf16[4,128,512]{2,1,0:T(8,128)(2,1)S(1)}, bf16[4,128,512]{2,1,0:T(8,128)(2,1)S(1)}, u32[]{:S(2)}, u32[]{:S(2)}) collective-permute-start(bf16[4,128,512]{2,1,0:T(8,128)(2,1)S(1)} %pad_maximum_fusion), channel_id=1, source_target_pairs={{0,8},{8,0},{1,9},{9,1},{2,10},{10,2},{3,11},{11,3},{4,12},{12,4},... | collective-permute-start | bytes 1572872 | tf_op jit(solution)/shard_map/ppermute | solution.py:236
  114.4 14.4 %all-to-all-done.3.parts = bf16[32,32,128]{2,1,0:T(8,128)(2,1)S(1)} async-done(((bf16[32,32,128]{2,1,0:T(8,128)(2,1)}), bf16[32,32,128]{2,1,0:T(8,128)(2,1)S(1)}, u32[]{:S(2)}, u32[]{:S(2)}) %all-to-all-start.3) | async-done | bytes 262176 | tf_op jit(solution)/shard_map/all_to_all | solution.py:272
  128.8 0.0 collective-permute-done.12.crossed
  128.8 0.1 copy.12
  128.9 0.1 reshape.64
  129.0 0.8 convert_reduce_fusion
  129.8 0.1 reshape.65
  130.0 0.8 convolution_bitcast_fusion
  130.8 1.6 %assemble.1 = bf16[128,4096]{1,0:T(8,128)(2,1)} custom-call(s32[2]{0:T(128)S(1)} %pad_add_fusion.where, bf16[256,512]{1,0:T(8,128)(2,1)S(1)} %copy-done, bf16[256,512]{1,0:T(8,128)(2,1)S(1)} %collective-permute-done.9.up, bf16[256,512]{1,0:T(8,128)(2,1)S(1)} %collective-permute-done.10.down, bf16[256,512]{1,0:T(8,128)(2,1)S(1)} %collective-permute-done.11.down2, ...), custom_call_target="tpu_custom_call" | custom-call | bytes 65536 | tf_op jit(solution)/shard_map/assemble/pallas_call | solution.py:221
  (17 shorter events, 0.1 us)
Async XLA Ops:
  0.6 28.1 %collective-permute-start = (bf16[128,2048]{1,0:T(8,128)(2,1)}, bf16[128,2048]{1,0:T(8,128)(2,1)}, u32[]{:S(2)}, u32[]{:S(2)}) collective-permute-start(bf16[128,2048]{1,0:T(8,128)(2,1)} %refs_0_.1), channel_id=1, source_target_pairs={{0,71},{1,0},{2,1},{3,2},{4,3},{5,4},{6,5},{7,6},{64,7},{65,64},{6... | collective-permute-start | bytes 1572872 | tf_op jit(solution)/shard_map/ppermute | solution.py:232
  13.9 14.8 %all-to-all-start = ((bf16[8,32,128]{2,1,0:T(8,128)(2,1)}), bf16[8,32,128]{2,1,0:T(8,128)(2,1)S(1)}, u32[]{:S(2)}, u32[]{:S(2)}) async-start(bf16[8,32,128]{2,1,0:T(8,128)(2,1)} %broadcast_in_dim.4), calls=%async_computation | async-start | bytes 131072 | tf_op jit(solution)/shard_map/all_to_all | solution.py:35
  18.2 10.5 %collective-permute-start.1 = (bf16[16,2048]{1,0:T(8,128)(2,1)S(1)}, bf16[16,2048]{1,0:T(8,128)(2,1)S(1)}, u32[]{:S(2)}, u32[]{:S(2)}) collective-permute-start(bf16[16,2048]{1,0:T(8,128)(2,1)S(1)} %constant_dynamic-slice_fusion), channel_id=1, source_target_pairs={{0,4},{1,5},{2,6},{3,7},{4,64},{5,65},{6,66},{7,67},{64,68},{65,69... | collective-permute-start | bytes 196616 | tf_op jit(solution)/shard_map/ppermute | solution.py:232
  30.6 6.9 %copy-start.2 = (bf16[128,2048]{1,0:T(8,128)(2,1)S(1)}, bf16[128,2048]{1,0:T(8,128)(2,1)}, u32[]{:S(2)}) copy-start(bf16[128,2048]{1,0:T(8,128)(2,1)} %refs_0_.1) | copy-start | bytes 1572868
  30.6 39.6 %all-to-all-start.1 = ((bf16[16,512,128]{2,1,0:T(8,128)(2,1)}), bf16[16,512,128]{2,1,0:T(8,128)(2,1)S(1)}, u32[]{:S(2)}, u32[]{:S(2)}) async-start(bf16[16,512,128]{2,1,0:T(8,128)(2,1)} %broadcast_in_dim.5), calls=%async_computation.1 | async-start | bytes 4194304 | tf_op jit(solution)/shard_map/all_to_all | solution.py:35
  37.5 23.3 %collective-permute-start.4 = (bf16[128,2048]{1,0:T(8,128)(2,1)S(1)}, bf16[128,2048]{1,0:T(8,128)(2,1)S(1)}, u32[]{:S(2)}, u32[]{:S(2)}) collective-permute-start(bf16[128,2048]{1,0:T(8,128)(2,1)S(1)} %copy-done.2), channel_id=1, source_target_pairs={{0,1},{1,2},{2,3},{3,4},{4,5},{5,6},{6,7},{7,64},{64,65},{65,66},{... | collective-permute-start | bytes 1572872 | tf_op jit(solution)/shard_map/ppermute | solution.py:232
  41.3 27.0 %collective-permute-start.2 = (bf16[128,4096]{1,0:T(8,128)(2,1)}, bf16[128,4096]{1,0:T(8,128)(2,1)S(1)}, u32[]{:S(2)}, u32[]{:S(2)}) collective-permute-start(bf16[128,4096]{1,0:T(8,128)(2,1)} %x0.1), channel_id=1, source_target_pairs={{0,8},{8,0},{1,9},{9,1},{2,10},{10,2},{3,11},{11,3},{4,12},{12,4},... | collective-permute-start | bytes 3145736 | tf_op jit(solution)/shard_map/ppermute | solution.py:236
  45.8 19.6 %collective-permute-start.7 = (bf16[128,2048]{1,0:T(8,128)(2,1)}, bf16[128,2048]{1,0:T(8,128)(2,1)S(1)}, u32[]{:S(2)}, u32[]{:S(2)}) collective-permute-start(bf16[128,2048]{1,0:T(8,128)(2,1)} %collective-permute-done.refs_4_), channel_id=1, source_target_pairs={{0,71},{1,0},{2,1},{3,2},{4,3},{5,4},{6,5},{7,6},{64,7},{65,64},{6... | collective-permute-start | bytes 1572872 | tf_op jit(solution)/shard_map/ppermute | solution.py:232
  53.8 14.3 %collective-permute-start.3 = (bf16[128,2048]{1,0:T(8,128)(2,1)S(1)}, bf16[128,2048]{1,0:T(8,128)(2,1)S(1)}, u32[]{:S(2)}, u32[]{:S(2)}) collective-permute-start(bf16[128,2048]{1,0:T(8,128)(2,1)S(1)} %copy-done.2), channel_id=1, source_target_pairs={{0,8},{8,0},{1,9},{9,1},{2,10},{10,2},{3,11},{11,3},{4,12},{12,4},... | collective-permute-start | bytes 1572872 | tf_op jit(solution)/shard_map/ppermute | solution.py:236
  56.0 12.2 %collective-permute-start.6 = (bf16[128,2048]{1,0:T(8,128)(2,1)}, bf16[128,2048]{1,0:T(8,128)(2,1)S(1)}, u32[]{:S(2)}, u32[]{:S(2)}) collective-permute-start(bf16[128,2048]{1,0:T(8,128)(2,1)} %collective-permute-done.refs_4_), channel_id=1, source_target_pairs={{0,8},{8,0},{1,9},{9,1},{2,10},{10,2},{3,11},{11,3},{4,12},{12,4},... | collective-permute-start | bytes 1572872 | tf_op jit(solution)/shard_map/ppermute | solution.py:236
  60.7 7.5 %copy-start.5 = (bf16[128,2048]{1,0:T(8,128)(2,1)}, bf16[128,2048]{1,0:T(8,128)(2,1)S(1)}, u32[]{:S(2)}) copy-start(bf16[128,2048]{1,0:T(8,128)(2,1)S(1)} %collective-permute-done.4.refs_2_) | copy-start | bytes 1572868
  60.7 7.5 %collective-permute-start.5 = (bf16[128,2048]{1,0:T(8,128)(2,1)S(1)}, bf16[128,2048]{1,0:T(8,128)(2,1)S(1)}, u32[]{:S(2)}, u32[]{:S(2)}) collective-permute-start(bf16[128,2048]{1,0:T(8,128)(2,1)S(1)} %collective-permute-done.4.refs_2_), channel_id=1, source_target_pairs={{0,8},{8,0},{1,9},{9,1},{2,10},{10,2},{3,11},{11,3},{4,12},{12,4},... | collective-permute-start | bytes 1572872 | tf_op jit(solution)/shard_map/ppermute | solution.py:236
  65.5 2.8 %copy-start.6 = (bf16[128,2048]{1,0:T(8,128)(2,1)}, bf16[128,2048]{1,0:T(8,128)(2,1)S(1)}, u32[]{:S(2)}) copy-start(bf16[128,2048]{1,0:T(8,128)(2,1)S(1)} %collective-permute-done.7.refs_6_) | copy-start | bytes 1572868
  65.5 4.7 %collective-permute-start.8 = (bf16[128,2048]{1,0:T(8,128)(2,1)S(1)}, bf16[128,2048]{1,0:T(8,128)(2,1)}, u32[]{:S(2)}, u32[]{:S(2)}) collective-permute-start(bf16[128,2048]{1,0:T(8,128)(2,1)S(1)} %collective-permute-done.7.refs_6_), channel_id=1, source_target_pairs={{0,8},{8,0},{1,9},{9,1},{2,10},{10,2},{3,11},{11,3},{4,12},{12,4},... | collective-permute-start | bytes 1572872 | tf_op jit(solution)/shard_map/ppermute | solution.py:236
  68.2 2.0 %copy-start.3 = (bf16[128,2048]{1,0:T(8,128)(2,1)}, bf16[128,2048]{1,0:T(8,128)(2,1)S(1)}, u32[]{:S(2)}) copy-start(bf16[128,2048]{1,0:T(8,128)(2,1)S(1)} %collective-permute-done.3.g1.refs_1_) | copy-start | bytes 1572868
  68.2 0.8 copy-start.7
  68.2 1.0 copy-start.8
  69.2 1.0 copy-start.4
  70.2 1.4 %copy-start.1 = (bf16[16,512,128]{2,1,0:T(8,128)(2,1)}, bf16[16,512,128]{2,1,0:T(8,128)(2,1)S(1)}, u32[]{:S(2)}) copy-start(bf16[16,512,128]{2,1,0:T(8,128)(2,1)S(1)} %all-to-all-done.1.mixed.refs_9_) | copy-start | bytes 6291460
  75.2 23.7 %all-to-all-start.2 = ((bf16[16,128,128]{2,1,0:T(8,128)(2,1)}), bf16[16,128,128]{2,1,0:T(8,128)(2,1)S(1)}, u32[]{:S(2)}, u32[]{:S(2)}) async-start(bf16[16,128,128]{2,1,0:T(8,128)(2,1)} %low_rank.1), calls=%async_computation.2 | async-start | bytes 1048576 | tf_op jit(solution)/shard_map/all_to_all | solution.py:267
  87.8 19.6 %collective-permute-start.11 = (bf16[256,512]{1,0:T(8,128)(2,1)}, bf16[256,512]{1,0:T(8,128)(2,1)S(1)}, u32[]{:S(2)}, u32[]{:S(2)}) collective-permute-start(bf16[256,512]{1,0:T(8,128)(2,1)} %get-tuple-element.38), channel_id=1, source_target_pairs={{0,2},{1,3},{2,4},{3,5},{4,6},{5,7},{6,64},{7,65},{64,66},{65,67},... | collective-permute-start | bytes 786440 | tf_op jit(solution)/shard_map/ppermute | solution.py:232
  90.4 21.2 %collective-permute-start.10 = (bf16[256,512]{1,0:T(8,128)(2,1)}, bf16[256,512]{1,0:T(8,128)(2,1)S(1)}, u32[]{:S(2)}, u32[]{:S(2)}) collective-permute-start(bf16[256,512]{1,0:T(8,128)(2,1)} %get-tuple-element.37), channel_id=1, source_target_pairs={{0,1},{1,2},{2,3},{3,4},{4,5},{5,6},{6,7},{7,64},{64,65},{65,66},{... | collective-permute-start | bytes 786440 | tf_op jit(solution)/shard_map/ppermute | solution.py:232
  95.1 12.4 %copy-start = (bf16[256,512]{1,0:T(8,128)(2,1)S(1)}, bf16[256,512]{1,0:T(8,128)(2,1)}, u32[]{:S(2)}) copy-start(bf16[256,512]{1,0:T(8,128)(2,1)} %get-tuple-element.35.near) | copy-start | bytes 786436
  95.1 16.5 %collective-permute-start.9 = (bf16[256,512]{1,0:T(8,128)(2,1)}, bf16[256,512]{1,0:T(8,128)(2,1)S(1)}, u32[]{:S(2)}, u32[]{:S(2)}) collective-permute-start(bf16[256,512]{1,0:T(8,128)(2,1)} %get-tuple-element.36), channel_id=1, source_target_pairs={{0,71},{1,0},{2,1},{3,2},{4,3},{5,4},{6,5},{7,6},{64,7},{65,64},{6... | collective-permute-start | bytes 786440 | tf_op jit(solution)/shard_map/ppermute | solution.py:232
  99.7 29.0 %all-to-all-start.3 = ((bf16[32,32,128]{2,1,0:T(8,128)(2,1)}), bf16[32,32,128]{2,1,0:T(8,128)(2,1)S(1)}, u32[]{:S(2)}, u32[]{:S(2)}) async-start(bf16[32,32,128]{2,1,0:T(8,128)(2,1)} %to_line.1), calls=%async_computation.3 | async-start | bytes 524288 | tf_op jit(solution)/shard_map/all_to_all | solution.py:272
  111.7 17.3 %copy-start.10 = (f32[1,8192]{1,0:T(1,128)S(1)}, f32[1,8192]{1,0:T(1,128)}, u32[]{:S(2)}) copy-start(f32[1,8192]{1,0:T(1,128)} %param.11) | copy-start | bytes 98308
  111.7 17.3 %copy-start.11 = (f32[1,8192]{1,0:T(1,128)S(1)}, f32[1,8192]{1,0:T(1,128)}, u32[]{:S(2)}) copy-start(f32[1,8192]{1,0:T(1,128)} %param.10) | copy-start | bytes 98308
  111.7 18.2 %copy-start.9 = (bf16[512,256]{1,0:T(8,128)(2,1)S(1)}, bf16[512,256]{1,0:T(8,128)(2,1)}, u32[]{:S(2)}) copy-start(bf16[512,256]{1,0:T(8,128)(2,1)} %param.9) | copy-start | bytes 786436
  111.7 17.1 %collective-permute-start.12 = (bf16[4,128,512]{2,1,0:T(8,128)(2,1)S(1)}, bf16[4,128,512]{2,1,0:T(8,128)(2,1)S(1)}, u32[]{:S(2)}, u32[]{:S(2)}) collective-permute-start(bf16[4,128,512]{2,1,0:T(8,128)(2,1)S(1)} %pad_maximum_fusion), channel_id=1, source_target_pairs={{0,8},{8,0},{1,9},{9,1},{2,10},{10,2},{3,11},{11,3},{4,12},{12,4},... | collective-permute-start | bytes 1572872 | tf_op jit(solution)/shard_map/ppermute | solution.py:236
